TPU v7x, 32 devices: a whole 2x2x4 slice. The times are simulated.
32 devices in a mesh: gx: 8 (over z, core), gy: 4 (over y, x).
Axes of the slice: x: 2, y: 2, z: 4, core: 2. Of those that a mesh axis runs over, the one named last changes fastest.
Arguments:
- initial_temp: float32 [16, 64, 512], P(None, 'gx', 'gy'), may hold values from 0.85 to 1.2
- material: int32 [16, 64, 512], P(None, 'gx', 'gy'), may hold values from 0 to 15
- plate: int32 [16, 64, 512], P(None, 'gx', 'gy'), may hold values 0 or 1
- cooling: float32 [16, 64, 512], P(None, 'gx', 'gy'), may hold values from 0.02 to 0.1
- principal: float32 [16, 3], replicated, may hold values from 0.1 to 1
- angles: float32 [16, 3], replicated, may hold values from -3.140625 to 3.140625
- aging_scale: float32 [16], replicated, may hold values from 0.5 to 2
Outputs:
- temp_sensitivity: float32 [16, 64, 512], P(None, 'gx', 'gy')
- cooling_sensitivity: float32 [16, 64, 512], P(None, 'gx', 'gy')
All inputs are finite; a program needn't handle non-finite values. No bound on the sum of `plate` on one device may be relied on, other than what follows from the above.
Results may differ from a plain program's by a relative error of at most 0.0003.
Values sent between devices are 32-bit elements; how exact they have to be, the bound alone decides.
No kernel may reach another device: no remote copies, remote signals or barrier semaphores. Data moves between devices by JAX's collectives and lax.ppermute only.
A program may use at most 64 MiB of HBM per device.

v0:
```python
import jax
import jax.numpy as jnp
from jax import lax
from jax.sharding import PartitionSpec as P

STEPS = 3


STEP_SCALE = 0.06
COOL_TEMP = 0.85
AGE_BETA = 8.0
HALF_OFFSETS = [
    (first, second, third)
    for first in (-1, 0, 1)
    for second in (-1, 0, 1)
    for third in (-1, 0, 1)
    if (first, second, third) > (0, 0, 0)
]


def padded_2(block, sides, width):
    for axis, dim in sides:
        count = lax.axis_size(axis)
        forward = [(i, i + 1) for i in range(count - 1)]
        backward = [(target, source) for source, target in forward]
        low = lax.ppermute(
            lax.slice_in_dim(block, block.shape[dim] - width, None, axis=dim), axis, forward
        )
        high = lax.ppermute(lax.slice_in_dim(block, 0, width, axis=dim), axis, backward)
        block = jnp.concatenate([low, block, high], axis=dim)
    return block


def weight_table(principal, angles, aging_scale):
    cos_first = jnp.cos(angles[:, 0])
    sin_first = jnp.sin(angles[:, 0])
    cos_second = jnp.cos(angles[:, 1])
    sin_second = jnp.sin(angles[:, 1])
    cos_third = jnp.cos(angles[:, 2])
    sin_third = jnp.sin(angles[:, 2])
    columns = [
        (
            cos_first * cos_third - sin_first * cos_second * sin_third,
            sin_first * cos_third + cos_first * cos_second * sin_third,
            sin_second * sin_third,
        ),
        (
            -cos_first * sin_third - sin_first * cos_second * cos_third,
            -sin_first * sin_third + cos_first * cos_second * cos_third,
            sin_second * cos_third,
        ),
        (sin_first * sin_second, -cos_first * sin_second, cos_second),
    ]
    rows = []
    for offset in HALF_OFFSETS:
        length_sq = float(offset[0] ** 2 + offset[1] ** 2 + offset[2] ** 2)
        kappa = jnp.zeros_like(aging_scale)
        for index in range(3):
            along = (
                columns[index][0] * offset[0]
                + columns[index][1] * offset[1]
                + columns[index][2] * offset[2]
            )
            kappa = kappa + principal[:, index] * along * along
        rows.append(STEP_SCALE * kappa / (length_sq * length_sq))
    rows.append(aging_scale)
    return jnp.stack(rows, 0)


def beside_all(padded, offset, sign):
    size_z = padded.shape[-3] - 2
    size_x = padded.shape[-2] - 2
    size_y = padded.shape[-1] - 2
    start_z = 1 + sign * offset[0]
    start_x = 1 + sign * offset[1]
    start_y = 1 + sign * offset[2]
    return padded[
        start_z : start_z + size_z, start_x : start_x + size_x, start_y : start_y + size_y
    ]


def crop(field, margin):
    if margin == 0:
        return field
    return field[..., margin:-margin, margin:-margin]


def pad_depth(field):
    return jnp.pad(field, ((1, 1), (0, 0), (0, 0)))


def pad_depth_all(stacked):
    return jnp.pad(stacked, ((0, 0), (1, 1), (0, 0), (0, 0)))


def advance(extended, weights, diag_part, coeff_part):
    padded = pad_depth(extended)
    center = extended[:, 1:-1, 1:-1]
    near = jnp.zeros_like(center)
    for index, offset in enumerate(HALF_OFFSETS):
        near = near + weights[index] * (
            beside_all(padded, offset, 1) + beside_all(padded, offset, -1)
        )
    return (1.0 - diag_part) * center + near + coeff_part * COOL_TEMP


def local(initial_temp, material, plate, cooling, principal, angles, aging_scale):
    table = weight_table(principal, angles, aging_scale)
    links = len(HALF_OFFSETS)
    count = table.shape[1]
    plate_float = plate.astype(jnp.float32)
    coeff = cooling * plate_float
    keep = 0
    margin = 1 + keep
    id_ext, coeff_ext = (
        padded_2((material + 1).astype(jnp.float32), (("gx", 1), ("gy", 2)), margin),
        padded_2(coeff, (("gx", 1), ("gy", 2)), margin),
    )
    levels = jnp.arange(count, dtype=jnp.float32) + 1.0
    matches = (id_ext[None] == levels[:, None, None, None]).astype(jnp.float32)
    fields = jnp.einsum("km,mzxy->kzxy", table, matches, precision=lax.Precision.HIGHEST)
    valid = pad_depth((id_ext > 0.5).astype(jnp.float32))
    inner = crop(fields, 1)
    coeff_near = crop(coeff_ext, 1)
    diag = coeff_near
    for index, offset in enumerate(HALF_OFFSETS):
        diag = diag + inner[index] * (beside_all(valid, offset, 1) + beside_all(valid, offset, -1))
    temps = [initial_temp]
    current = initial_temp
    for step in range(STEPS):
        own = crop(current, keep) if step > 0 else current
        extended = padded_2(own, (("gx", 1), ("gy", 2)), 1 + keep)
        current = advance(
            extended,
            crop(fields, margin - keep),
            crop(diag, margin - 1 - keep),
            crop(coeff_near, margin - 1 - keep),
        )
        temps.append(current)
    aging = crop(fields, margin - keep)[links]
    local_total = jnp.zeros((), jnp.float32)
    drives = []
    for state in temps[1:]:
        safe = jnp.where(state > 0.5, state, 1.0)
        rate = jnp.where(state > 0.5, jnp.exp(AGE_BETA * (1.0 - 1.0 / safe)), 0.0)
        local_total = local_total + jnp.sum(crop(aging * rate, keep))
        drives.append(aging * AGE_BETA * rate / (safe * safe))
    total = lax.psum(local_total, ("gx", "gy"))
    adjoint = drives[-1]
    sens = jnp.zeros_like(initial_temp)
    for step in range(STEPS - 1, -1, -1):
        earlier = temps[step] if step == 0 else crop(temps[step], keep)
        sens = sens - crop(adjoint, keep) * (earlier - COOL_TEMP)
        extended = padded_2(adjoint, (("gx", 1), ("gy", 2)), 1)
        center_diag = crop(diag, margin - 1)
        near_fields = pad_depth_all(crop(fields, margin - 1)[:links])
        padded = pad_depth(extended)
        result = (1.0 - center_diag) * crop(extended, 1)
        for transpose_index, transpose_offset in enumerate(HALF_OFFSETS):
            product = near_fields[transpose_index] * padded
            result = (
                result
                + beside_all(product, transpose_offset, -1)
                + beside_all(product, transpose_offset, 1)
            )
        adjoint = result
        if step > 0:
            adjoint = adjoint + crop(drives[step - 1], keep - keep)
    cells = (
        initial_temp.shape[0]
        * initial_temp.shape[1]
        * initial_temp.shape[2]
        * lax.axis_size("gx")
        * lax.axis_size("gy")
    )
    scale = float(cells) / total
    return (adjoint * scale, sens * plate_float * scale)


def solution(mesh):
    return jax.shard_map(
        local,
        mesh=mesh,
        in_specs=(
            P(None, "gx", "gy"),
            P(None, "gx", "gy"),
            P(None, "gx", "gy"),
            P(None, "gx", "gy"),
            P(),
            P(),
            P(),
        ),
        out_specs=(P(None, "gx", "gy"), P(None, "gx", "gy")),
        check_vma=False,
    )
```

profile of v0, /device:TPU:0, one launch (start us, length us, event | category | flops | bytes accessed | tf_op | source)
XLA Modules:
  0.0 176.9 jit_solution(10811094695920362069)
XLA Ops:
  1.6 2.4 %collective-permute-start.4 = (f32[16,1,128]{2,1,0:T(1,128)S(1)}, f32[16,1,128]{2,1,0:T(1,128)S(1)}, u32[]{:S(2)}, u32[]{:S(2)}) collective-permute-start(f32[16,1,128]{2,1,0:T(1,128)S(1)} %get-tuple-element.109), channel_id=1, source_target_pairs={{0,4},{4,8},{8,12},{12,16},{16,20},{20,24},{24,28},{1,5},{5,9},{9,... | collective-permute-start | bytes 24584 | tf_op jit(solution)/shard_map/ppermute | solution.py:26
  6.1 5.2 %collective-permute-start = (f32[16,1,128]{2,1,0:T(1,128)S(1)}, f32[16,1,128]{2,1,0:T(1,128)S(1)}, u32[]{:S(2)}, u32[]{:S(2)}) collective-permute-start(f32[16,1,128]{2,1,0:T(1,128)S(1)} %get-tuple-element.111), channel_id=1, source_target_pairs={{0,4},{4,8},{8,12},{12,16},{16,20},{20,24},{24,28},{1,5},{5,9},{9,... | collective-permute-start | bytes 24584 | tf_op jit(solution)/shard_map/ppermute | solution.py:26
  19.5 3.4 %collective-permute-start.2 = (f32[16,10,1]{2,1,0:T(8,128)S(1)}, f32[16,10,1]{2,1,0:T(8,128)S(1)}, u32[]{:S(2)}, u32[]{:S(2)}) collective-permute-start(f32[16,10,1]{2,1,0:T(8,128)S(1)} %get-tuple-element.97), channel_id=1, source_target_pairs={{0,1},{1,2},{2,3},{4,5},{5,6},{6,7},{8,9},{9,10},{10,11},{12,13},{... | collective-permute-start | bytes 1928 | tf_op jit(solution)/shard_map/ppermute | solution.py:26
  25.2 4.6 %collective-permute-start.7 = (f32[16,10,1]{2,1,0:T(8,128)S(1)}, f32[16,10,1]{2,1,0:T(8,128)S(1)}, u32[]{:S(2)}, u32[]{:S(2)}) collective-permute-start(f32[16,10,1]{2,1,0:T(8,128)S(1)} %get-tuple-element.95), channel_id=1, source_target_pairs={{0,1},{1,2},{2,3},{4,5},{5,6},{6,7},{8,9},{9,10},{10,11},{12,13},{... | collective-permute-start | bytes 1928 | tf_op jit(solution)/shard_map/ppermute | solution.py:26
  34.7 3.8 %collective-permute-done.6 = f32[16,10,1]{2,1,0:T(8,128)S(1)} collective-permute-done((f32[16,10,1]{2,1,0:T(8,128)S(1)}, f32[16,10,1]{2,1,0:T(8,128)S(1)}, u32[]{:S(2)}, u32[]{:S(2)}) %collective-permute-start.6) | collective-permute-done | bytes 672 | tf_op jit(solution)/shard_map/ppermute | solution.py:29
  39.7 2.5 %collective-permute-start.8 = (f32[16,1,128]{2,1,0:T(1,128)S(1)}, f32[16,1,128]{2,1,0:T(1,128)S(1)}, u32[]{:S(2)}, u32[]{:S(2)}) collective-permute-start(f32[16,1,128]{2,1,0:T(1,128)S(1)} %get-tuple-element.107), channel_id=1, source_target_pairs={{0,4},{4,8},{8,12},{12,16},{16,20},{20,24},{24,28},{1,5},{5,9},{9,... | collective-permute-start | bytes 24584 | tf_op jit(solution)/shard_map/ppermute | solution.py:26
  43.4 4.1 %collective-permute-done.9 = f32[16,1,128]{2,1,0:T(1,128)S(1)} collective-permute-done((f32[16,1,128]{2,1,0:T(1,128)S(1)}, f32[16,1,128]{2,1,0:T(1,128)S(1)}, u32[]{:S(2)}, u32[]{:S(2)}) %collective-permute-start.9) | collective-permute-done | bytes 8224 | tf_op jit(solution)/shard_map/ppermute | solution.py:29
  47.7 4.1 %collective-permute-start.11 = (f32[16,10,1]{2,1,0:T(8,128)S(1)}, f32[16,10,1]{2,1,0:T(8,128)S(1)}, u32[]{:S(2)}, u32[]{:S(2)}) collective-permute-start(f32[16,10,1]{2,1,0:T(8,128)S(1)} %get-tuple-element.93), channel_id=1, source_target_pairs={{0,1},{1,2},{2,3},{4,5},{5,6},{6,7},{8,9},{9,10},{10,11},{12,13},{... | collective-permute-start | bytes 1928 | tf_op jit(solution)/shard_map/ppermute | solution.py:26
  54.3 4.6 %collective-permute-done.10 = f32[16,10,1]{2,1,0:T(8,128)S(1)} collective-permute-done((f32[16,10,1]{2,1,0:T(8,128)S(1)}, f32[16,10,1]{2,1,0:T(8,128)S(1)}, u32[]{:S(2)}, u32[]{:S(2)}) %collective-permute-start.10) | collective-permute-done | bytes 672 | tf_op jit(solution)/shard_map/ppermute | solution.py:29
  59.8 2.9 %collective-permute-start.12 = (f32[16,1,128]{2,1,0:T(1,128)S(1)}, f32[16,1,128]{2,1,0:T(1,128)S(1)}, u32[]{:S(2)}, u32[]{:S(2)}) collective-permute-start(f32[16,1,128]{2,1,0:T(1,128)S(1)} %get-tuple-element.105), channel_id=1, source_target_pairs={{0,4},{4,8},{8,12},{12,16},{16,20},{20,24},{24,28},{1,5},{5,9},{9,... | collective-permute-start | bytes 24584 | tf_op jit(solution)/shard_map/ppermute | solution.py:26
  64.0 3.5 %collective-permute-done.13 = f32[16,1,128]{2,1,0:T(1,128)S(1)} collective-permute-done((f32[16,1,128]{2,1,0:T(1,128)S(1)}, f32[16,1,128]{2,1,0:T(1,128)S(1)}, u32[]{:S(2)}, u32[]{:S(2)}) %collective-permute-start.13) | collective-permute-done | bytes 8224 | tf_op jit(solution)/shard_map/ppermute | solution.py:29
  67.6 3.4 %collective-permute-start.15 = (f32[16,10,1]{2,1,0:T(8,128)S(1)}, f32[16,10,1]{2,1,0:T(8,128)S(1)}, u32[]{:S(2)}, u32[]{:S(2)}) collective-permute-start(f32[16,10,1]{2,1,0:T(8,128)S(1)} %get-tuple-element.91), channel_id=1, source_target_pairs={{0,1},{1,2},{2,3},{4,5},{5,6},{6,7},{8,9},{9,10},{10,11},{12,13},{... | collective-permute-start | bytes 1928 | tf_op jit(solution)/shard_map/ppermute | solution.py:26
  73.5 4.6 %collective-permute-done.14 = f32[16,10,1]{2,1,0:T(8,128)S(1)} collective-permute-done((f32[16,10,1]{2,1,0:T(8,128)S(1)}, f32[16,10,1]{2,1,0:T(8,128)S(1)}, u32[]{:S(2)}, u32[]{:S(2)}) %collective-permute-start.14) | collective-permute-done | bytes 672 | tf_op jit(solution)/shard_map/ppermute | solution.py:29
  79.7 2.9 %collective-permute-start.16 = (f32[16,1,128]{2,1,0:T(1,128)S(1)}, f32[16,1,128]{2,1,0:T(1,128)S(1)}, u32[]{:S(2)}, u32[]{:S(2)}) collective-permute-start(f32[16,1,128]{2,1,0:T(1,128)S(1)} %get-tuple-element.103), channel_id=1, source_target_pairs={{0,4},{4,8},{8,12},{12,16},{16,20},{20,24},{24,28},{1,5},{5,9},{9,... | collective-permute-start | bytes 24584 | tf_op jit(solution)/shard_map/ppermute | solution.py:26
  83.9 3.5 %collective-permute-done.17 = f32[16,1,128]{2,1,0:T(1,128)S(1)} collective-permute-done((f32[16,1,128]{2,1,0:T(1,128)S(1)}, f32[16,1,128]{2,1,0:T(1,128)S(1)}, u32[]{:S(2)}, u32[]{:S(2)}) %collective-permute-start.17) | collective-permute-done | bytes 8224 | tf_op jit(solution)/shard_map/ppermute | solution.py:29
  87.5 2.5 %collective-permute-start.18 = (f32[16,10,1]{2,1,0:T(8,128)S(1)}, f32[16,10,1]{2,1,0:T(8,128)S(1)}, u32[]{:S(2)}, u32[]{:S(2)}) collective-permute-start(f32[16,10,1]{2,1,0:T(8,128)S(1)} %get-tuple-element.89), channel_id=1, source_target_pairs={{0,1},{1,2},{2,3},{4,5},{5,6},{6,7},{8,9},{9,10},{10,11},{12,13},{... | collective-permute-start | bytes 1928 | tf_op jit(solution)/shard_map/ppermute | solution.py:26
  93.0 4.1 %collective-permute-done.19 = f32[16,10,1]{2,1,0:T(8,128)S(1)} collective-permute-done((f32[16,10,1]{2,1,0:T(8,128)S(1)}, f32[16,10,1]{2,1,0:T(8,128)S(1)}, u32[]{:S(2)}, u32[]{:S(2)}) %collective-permute-start.19) | collective-permute-done | bytes 672 | tf_op jit(solution)/shard_map/ppermute | solution.py:29
  98.8 2.9 %collective-permute-start.20 = (f32[16,1,128]{2,1,0:T(1,128)S(1)}, f32[16,1,128]{2,1,0:T(1,128)S(1)}, u32[]{:S(2)}, u32[]{:S(2)}) collective-permute-start(f32[16,1,128]{2,1,0:T(1,128)S(1)} %get-tuple-element.101), channel_id=1, source_target_pairs={{0,4},{4,8},{8,12},{12,16},{16,20},{20,24},{24,28},{1,5},{5,9},{9,... | collective-permute-start | bytes 24584 | tf_op jit(solution)/shard_map/ppermute | solution.py:26
  103.0 3.1 %collective-permute-done.21 = f32[16,1,128]{2,1,0:T(1,128)S(1)} collective-permute-done((f32[16,1,128]{2,1,0:T(1,128)S(1)}, f32[16,1,128]{2,1,0:T(1,128)S(1)}, u32[]{:S(2)}, u32[]{:S(2)}) %collective-permute-start.21) | collective-permute-done | bytes 8224 | tf_op jit(solution)/shard_map/ppermute | solution.py:29
  106.2 2.5 %collective-permute-start.22 = (f32[16,10,1]{2,1,0:T(8,128)S(1)}, f32[16,10,1]{2,1,0:T(8,128)S(1)}, u32[]{:S(2)}, u32[]{:S(2)}) collective-permute-start(f32[16,10,1]{2,1,0:T(8,128)S(1)} %get-tuple-element.87), channel_id=1, source_target_pairs={{0,1},{1,2},{2,3},{4,5},{5,6},{6,7},{8,9},{9,10},{10,11},{12,13},{... | collective-permute-start | bytes 1928 | tf_op jit(solution)/shard_map/ppermute | solution.py:26
  112.0 42.1 %psum.7 = f32[]{:T(128)} all-reduce(f32[]{:T(128)S(6)} %add.1910), channel_id=1, replica_groups=mesh['gx'=8,'gy'=4] {'gx','gy'}, use_global_device_ids=true, to_apply=%region_3.4 | all-reduce | flops 1 | bytes 8 | tf_op jit(solution)/shard_map/psum | solution.py:148
  159.8 2.3 %collective-permute-done.25 = f32[16,1,128]{2,1,0:T(1,128)S(1)} collective-permute-done((f32[16,1,128]{2,1,0:T(1,128)S(1)}, f32[16,1,128]{2,1,0:T(1,128)S(1)}, u32[]{:S(2)}, u32[]{:S(2)}) %collective-permute-start.25) | collective-permute-done | bytes 8224 | tf_op jit(solution)/shard_map/ppermute | solution.py:29
  162.2 4.2 %collective-permute-start.26 = (f32[16,10,1]{2,1,0:T(8,128)S(1)}, f32[16,10,1]{2,1,0:T(8,128)S(1)}, u32[]{:S(2)}, u32[]{:S(2)}) collective-permute-start(f32[16,10,1]{2,1,0:T(8,128)S(1)} %get-tuple-element.85), channel_id=1, source_target_pairs={{0,1},{1,2},{2,3},{4,5},{5,6},{6,7},{8,9},{9,10},{10,11},{12,13},{... | collective-permute-start | bytes 1928 | tf_op jit(solution)/shard_map/ppermute | solution.py:26
  168.9 5.7 %collective-permute-done.27 = f32[16,10,1]{2,1,0:T(8,128)S(1)} collective-permute-done((f32[16,10,1]{2,1,0:T(8,128)S(1)}, f32[16,10,1]{2,1,0:T(8,128)S(1)}, u32[]{:S(2)}, u32[]{:S(2)}) %collective-permute-start.27) | collective-permute-done | bytes 672 | tf_op jit(solution)/shard_map/ppermute | solution.py:29
  (99 shorter events, 48.0 us)
Async XLA Ops:
  1.6 22.6 %collective-permute-start.4 = (f32[16,1,128]{2,1,0:T(1,128)S(1)}, f32[16,1,128]{2,1,0:T(1,128)S(1)}, u32[]{:S(2)}, u32[]{:S(2)}) collective-permute-start(f32[16,1,128]{2,1,0:T(1,128)S(1)} %get-tuple-element.109), channel_id=1, source_target_pairs={{0,4},{4,8},{8,12},{12,16},{16,20},{20,24},{24,28},{1,5},{5,9},{9,... | collective-permute-start | bytes 24584 | tf_op jit(solution)/shard_map/ppermute | solution.py:26
  4.0 20.2 %collective-permute-start.5 = (f32[16,1,128]{2,1,0:T(1,128)S(1)}, f32[16,1,128]{2,1,0:T(1,128)S(1)}, u32[]{:S(2)}, u32[]{:S(2)}) collective-permute-start(f32[16,1,128]{2,1,0:T(1,128)S(1)} %get-tuple-element.110), channel_id=1, source_target_pairs={{4,0},{8,4},{12,8},{16,12},{20,16},{24,20},{28,24},{5,1},{9,5},{13... | collective-permute-start | bytes 24584 | tf_op jit(solution)/shard_map/ppermute | solution.py:29
  6.1 13.2 %collective-permute-start = (f32[16,1,128]{2,1,0:T(1,128)S(1)}, f32[16,1,128]{2,1,0:T(1,128)S(1)}, u32[]{:S(2)}, u32[]{:S(2)}) collective-permute-start(f32[16,1,128]{2,1,0:T(1,128)S(1)} %get-tuple-element.111), channel_id=1, source_target_pairs={{0,4},{4,8},{8,12},{12,16},{16,20},{20,24},{24,28},{1,5},{5,9},{9,... | collective-permute-start | bytes 24584 | tf_op jit(solution)/shard_map/ppermute | solution.py:26
  11.3 8.0 %collective-permute-start.1 = (f32[16,1,128]{2,1,0:T(1,128)S(1)}, f32[16,1,128]{2,1,0:T(1,128)S(1)}, u32[]{:S(2)}, u32[]{:S(2)}) collective-permute-start(f32[16,1,128]{2,1,0:T(1,128)S(1)} %get-tuple-element.112), channel_id=1, source_target_pairs={{4,0},{8,4},{12,8},{16,12},{20,16},{24,20},{28,24},{5,1},{9,5},{13... | collective-permute-start | bytes 24584 | tf_op jit(solution)/shard_map/ppermute | solution.py:29
  19.5 11.7 %collective-permute-start.2 = (f32[16,10,1]{2,1,0:T(8,128)S(1)}, f32[16,10,1]{2,1,0:T(8,128)S(1)}, u32[]{:S(2)}, u32[]{:S(2)}) collective-permute-start(f32[16,10,1]{2,1,0:T(8,128)S(1)} %get-tuple-element.97), channel_id=1, source_target_pairs={{0,1},{1,2},{2,3},{4,5},{5,6},{6,7},{8,9},{9,10},{10,11},{12,13},{... | collective-permute-start | bytes 1928 | tf_op jit(solution)/shard_map/ppermute | solution.py:26
  22.9 8.3 %collective-permute-start.3 = (f32[16,10,1]{2,1,0:T(8,128)S(1)}, f32[16,10,1]{2,1,0:T(8,128)S(1)}, u32[]{:S(2)}, u32[]{:S(2)}) collective-permute-start(f32[16,10,1]{2,1,0:T(8,128)S(1)} %get-tuple-element.98), channel_id=1, source_target_pairs={{1,0},{2,1},{3,2},{5,4},{6,5},{7,6},{9,8},{10,9},{11,10},{13,12},{... | collective-permute-start | bytes 1928 | tf_op jit(solution)/shard_map/ppermute | solution.py:29
  25.2 9.5 %collective-permute-start.7 = (f32[16,10,1]{2,1,0:T(8,128)S(1)}, f32[16,10,1]{2,1,0:T(8,128)S(1)}, u32[]{:S(2)}, u32[]{:S(2)}) collective-permute-start(f32[16,10,1]{2,1,0:T(8,128)S(1)} %get-tuple-element.95), channel_id=1, source_target_pairs={{0,1},{1,2},{2,3},{4,5},{5,6},{6,7},{8,9},{9,10},{10,11},{12,13},{... | collective-permute-start | bytes 1928 | tf_op jit(solution)/shard_map/ppermute | solution.py:26
  29.7 8.8 %collective-permute-start.6 = (f32[16,10,1]{2,1,0:T(8,128)S(1)}, f32[16,10,1]{2,1,0:T(8,128)S(1)}, u32[]{:S(2)}, u32[]{:S(2)}) collective-permute-start(f32[16,10,1]{2,1,0:T(8,128)S(1)} %get-tuple-element.96), channel_id=1, source_target_pairs={{1,0},{2,1},{3,2},{5,4},{6,5},{7,6},{9,8},{10,9},{11,10},{13,12},{... | collective-permute-start | bytes 1928 | tf_op jit(solution)/shard_map/ppermute | solution.py:29
  42.1 5.4 %collective-permute-start.9 = (f32[16,1,128]{2,1,0:T(1,128)S(1)}, f32[16,1,128]{2,1,0:T(1,128)S(1)}, u32[]{:S(2)}, u32[]{:S(2)}) collective-permute-start(f32[16,1,128]{2,1,0:T(1,128)S(1)} %get-tuple-element.108), channel_id=1, source_target_pairs={{4,0},{8,4},{12,8},{16,12},{20,16},{24,20},{28,24},{5,1},{9,5},{13... | collective-permute-start | bytes 24584 | tf_op jit(solution)/shard_map/ppermute | solution.py:29
  47.7 6.6 %collective-permute-start.11 = (f32[16,10,1]{2,1,0:T(8,128)S(1)}, f32[16,10,1]{2,1,0:T(8,128)S(1)}, u32[]{:S(2)}, u32[]{:S(2)}) collective-permute-start(f32[16,10,1]{2,1,0:T(8,128)S(1)} %get-tuple-element.93), channel_id=1, source_target_pairs={{0,1},{1,2},{2,3},{4,5},{5,6},{6,7},{8,9},{9,10},{10,11},{12,13},{... | collective-permute-start | bytes 1928 | tf_op jit(solution)/shard_map/ppermute | solution.py:26
  51.8 7.1 %collective-permute-start.10 = (f32[16,10,1]{2,1,0:T(8,128)S(1)}, f32[16,10,1]{2,1,0:T(8,128)S(1)}, u32[]{:S(2)}, u32[]{:S(2)}) collective-permute-start(f32[16,10,1]{2,1,0:T(8,128)S(1)} %get-tuple-element.94), channel_id=1, source_target_pairs={{1,0},{2,1},{3,2},{5,4},{6,5},{7,6},{9,8},{10,9},{11,10},{13,12},{... | collective-permute-start | bytes 1928 | tf_op jit(solution)/shard_map/ppermute | solution.py:29
  59.8 4.2 %collective-permute-start.12 = (f32[16,1,128]{2,1,0:T(1,128)S(1)}, f32[16,1,128]{2,1,0:T(1,128)S(1)}, u32[]{:S(2)}, u32[]{:S(2)}) collective-permute-start(f32[16,1,128]{2,1,0:T(1,128)S(1)} %get-tuple-element.105), channel_id=1, source_target_pairs={{0,4},{4,8},{8,12},{12,16},{16,20},{20,24},{24,28},{1,5},{5,9},{9,... | collective-permute-start | bytes 24584 | tf_op jit(solution)/shard_map/ppermute | solution.py:26
  62.6 4.8 %collective-permute-start.13 = (f32[16,1,128]{2,1,0:T(1,128)S(1)}, f32[16,1,128]{2,1,0:T(1,128)S(1)}, u32[]{:S(2)}, u32[]{:S(2)}) collective-permute-start(f32[16,1,128]{2,1,0:T(1,128)S(1)} %get-tuple-element.106), channel_id=1, source_target_pairs={{4,0},{8,4},{12,8},{16,12},{20,16},{24,20},{28,24},{5,1},{9,5},{13... | collective-permute-start | bytes 24584 | tf_op jit(solution)/shard_map/ppermute | solution.py:29
  67.6 5.9 %collective-permute-start.15 = (f32[16,10,1]{2,1,0:T(8,128)S(1)}, f32[16,10,1]{2,1,0:T(8,128)S(1)}, u32[]{:S(2)}, u32[]{:S(2)}) collective-permute-start(f32[16,10,1]{2,1,0:T(8,128)S(1)} %get-tuple-element.91), channel_id=1, source_target_pairs={{0,1},{1,2},{2,3},{4,5},{5,6},{6,7},{8,9},{9,10},{10,11},{12,13},{... | collective-permute-start | bytes 1928 | tf_op jit(solution)/shard_map/ppermute | solution.py:26
  71.0 7.1 %collective-permute-start.14 = (f32[16,10,1]{2,1,0:T(8,128)S(1)}, f32[16,10,1]{2,1,0:T(8,128)S(1)}, u32[]{:S(2)}, u32[]{:S(2)}) collective-permute-start(f32[16,10,1]{2,1,0:T(8,128)S(1)} %get-tuple-element.92), channel_id=1, source_target_pairs={{1,0},{2,1},{3,2},{5,4},{6,5},{7,6},{9,8},{10,9},{11,10},{13,12},{... | collective-permute-start | bytes 1928 | tf_op jit(solution)/shard_map/ppermute | solution.py:29
  82.5 4.8 %collective-permute-start.17 = (f32[16,1,128]{2,1,0:T(1,128)S(1)}, f32[16,1,128]{2,1,0:T(1,128)S(1)}, u32[]{:S(2)}, u32[]{:S(2)}) collective-permute-start(f32[16,1,128]{2,1,0:T(1,128)S(1)} %get-tuple-element.104), channel_id=1, source_target_pairs={{4,0},{8,4},{12,8},{16,12},{20,16},{24,20},{28,24},{5,1},{9,5},{13... | collective-permute-start | bytes 24584 | tf_op jit(solution)/shard_map/ppermute | solution.py:29
  87.5 5.5 %collective-permute-start.18 = (f32[16,10,1]{2,1,0:T(8,128)S(1)}, f32[16,10,1]{2,1,0:T(8,128)S(1)}, u32[]{:S(2)}, u32[]{:S(2)}) collective-permute-start(f32[16,10,1]{2,1,0:T(8,128)S(1)} %get-tuple-element.89), channel_id=1, source_target_pairs={{0,1},{1,2},{2,3},{4,5},{5,6},{6,7},{8,9},{9,10},{10,11},{12,13},{... | collective-permute-start | bytes 1928 | tf_op jit(solution)/shard_map/ppermute | solution.py:26
  90.0 7.1 %collective-permute-start.19 = (f32[16,10,1]{2,1,0:T(8,128)S(1)}, f32[16,10,1]{2,1,0:T(8,128)S(1)}, u32[]{:S(2)}, u32[]{:S(2)}) collective-permute-start(f32[16,10,1]{2,1,0:T(8,128)S(1)} %get-tuple-element.90), channel_id=1, source_target_pairs={{1,0},{2,1},{3,2},{5,4},{6,5},{7,6},{9,8},{10,9},{11,10},{13,12},{... | collective-permute-start | bytes 1928 | tf_op jit(solution)/shard_map/ppermute | solution.py:29
  98.8 4.2 %collective-permute-start.20 = (f32[16,1,128]{2,1,0:T(1,128)S(1)}, f32[16,1,128]{2,1,0:T(1,128)S(1)}, u32[]{:S(2)}, u32[]{:S(2)}) collective-permute-start(f32[16,1,128]{2,1,0:T(1,128)S(1)} %get-tuple-element.101), channel_id=1, source_target_pairs={{0,4},{4,8},{8,12},{12,16},{16,20},{20,24},{24,28},{1,5},{5,9},{9,... | collective-permute-start | bytes 24584 | tf_op jit(solution)/shard_map/ppermute | solution.py:26
  101.7 4.4 %collective-permute-start.21 = (f32[16,1,128]{2,1,0:T(1,128)S(1)}, f32[16,1,128]{2,1,0:T(1,128)S(1)}, u32[]{:S(2)}, u32[]{:S(2)}) collective-permute-start(f32[16,1,128]{2,1,0:T(1,128)S(1)} %get-tuple-element.102), channel_id=1, source_target_pairs={{4,0},{8,4},{12,8},{16,12},{20,16},{24,20},{28,24},{5,1},{9,5},{13... | collective-permute-start | bytes 24584 | tf_op jit(solution)/shard_map/ppermute | solution.py:29
  106.2 48.6 %collective-permute-start.22 = (f32[16,10,1]{2,1,0:T(8,128)S(1)}, f32[16,10,1]{2,1,0:T(8,128)S(1)}, u32[]{:S(2)}, u32[]{:S(2)}) collective-permute-start(f32[16,10,1]{2,1,0:T(8,128)S(1)} %get-tuple-element.87), channel_id=1, source_target_pairs={{0,1},{1,2},{2,3},{4,5},{5,6},{6,7},{8,9},{9,10},{10,11},{12,13},{... | collective-permute-start | bytes 1928 | tf_op jit(solution)/shard_map/ppermute | solution.py:26
  108.8 46.1 %collective-permute-start.23 = (f32[16,10,1]{2,1,0:T(8,128)S(1)}, f32[16,10,1]{2,1,0:T(8,128)S(1)}, u32[]{:S(2)}, u32[]{:S(2)}) collective-permute-start(f32[16,10,1]{2,1,0:T(8,128)S(1)} %get-tuple-element.88), channel_id=1, source_target_pairs={{1,0},{2,1},{3,2},{5,4},{6,5},{7,6},{9,8},{10,9},{11,10},{13,12},{... | collective-permute-start | bytes 1928 | tf_op jit(solution)/shard_map/ppermute | solution.py:29
  162.2 6.7 %collective-permute-start.26 = (f32[16,10,1]{2,1,0:T(8,128)S(1)}, f32[16,10,1]{2,1,0:T(8,128)S(1)}, u32[]{:S(2)}, u32[]{:S(2)}) collective-permute-start(f32[16,10,1]{2,1,0:T(8,128)S(1)} %get-tuple-element.85), channel_id=1, source_target_pairs={{0,1},{1,2},{2,3},{4,5},{5,6},{6,7},{8,9},{9,10},{10,11},{12,13},{... | collective-permute-start | bytes 1928 | tf_op jit(solution)/shard_map/ppermute | solution.py:26
  166.4 8.2 %collective-permute-start.27 = (f32[16,10,1]{2,1,0:T(8,128)S(1)}, f32[16,10,1]{2,1,0:T(8,128)S(1)}, u32[]{:S(2)}, u32[]{:S(2)}) collective-permute-start(f32[16,10,1]{2,1,0:T(8,128)S(1)} %get-tuple-element.86), channel_id=1, source_target_pairs={{1,0},{2,1},{3,2},{5,4},{6,5},{7,6},{9,8},{10,9},{11,10},{13,12},{... | collective-permute-start | bytes 1928 | tf_op jit(solution)/shard_map/ppermute | solution.py:29
  (7 other events, 37.5 us)
where the time goes:
time: 178 us; the launch traced here: 177 us
  starting transfers between devices  63 us (35%)
  waiting for transfers between devices  43 us (24%)
  blocking collectives  42.1 us (24%)
  other arithmetic  17.7 us (10%)
  local copies, waits for them, and re-layouts  5.97 us (3%)
  between operations  3.95 us (2%)
    ppermute x14, starting transfers between devices, padded_2(): lax.ppermute(lax.slice_in_dim(block, block.shape[dim] - width, None, axis...  44.7 us
    psum x1, blocking collectives, local(): total = lax.psum(local_total, ('gx', 'gy'))  42.1 us
    ppermute x14, waiting for transfers between devices, padded_2(): lax.ppermute(lax.slice_in_dim(block, 0, width, axis=dim), axis, backward)  39.3 us
    ppermute x14, starting transfers between devices, padded_2(): lax.ppermute(lax.slice_in_dim(block, 0, width, axis=dim), axis, backward)  18.2 us
    div x7, other arithmetic, weight_table(): rows.append(STEP_SCALE * kappa / (length_sq * length_sq))  5.94 us
    mul x15, other arithmetic, local(): product = near_fields[transpose_index] * padded  3.74 us
    ppermute x14, waiting for transfers between devices, padded_2(): lax.ppermute(lax.slice_in_dim(block, block.shape[dim] - width, None, axis...  3.62 us
  transfers between devices with their start and end apart: 28, of which 13 were waited for; matrix products, arithmetic and copies ran while one was open for 8% of the time, Pallas kernels for 0%

commit v1 on v0

v1 whole, which is shorter than its diff:
```python
import functools

import jax
import jax.numpy as jnp
from jax import lax
from jax.experimental import pallas as pl
from jax.experimental.pallas import tpu as pltpu
from jax.sharding import PartitionSpec as P

STEPS = 3
STEP_SCALE = 0.06
COOL_TEMP = 0.85
AGE_BETA = 8.0
HALF_OFFSETS = [
    (first, second, third)
    for first in (-1, 0, 1)
    for second in (-1, 0, 1)
    for third in (-1, 0, 1)
    if (first, second, third) > (0, 0, 0)
]
LINKS = len(HALF_OFFSETS)
HALO = 2 * STEPS
LANES = 128
SLOT = 16
T0, ID, COEFF = 0, 1, 2
VMEM = pl.BlockSpec(memory_space=pltpu.VMEM)


def table_rows(raw):
    angles = raw[3:6]
    cosine, sine = jnp.cos(angles), jnp.sin(angles)
    c1, c2, c3 = cosine[0:1], cosine[1:2], cosine[2:3]
    s1, s2, s3 = sine[0:1], sine[1:2], sine[2:3]
    columns = [
        (c1 * c3 - s1 * c2 * s3, s1 * c3 + c1 * c2 * s3, s2 * s3),
        (-c1 * s3 - s1 * c2 * c3, -s1 * s3 + c1 * c2 * c3, s2 * c3),
        (s1 * s2, -c1 * s2, c2),
    ]
    rows = []
    for offset in HALF_OFFSETS:
        length_sq = float(offset[0] ** 2 + offset[1] ** 2 + offset[2] ** 2)
        kappa = jnp.zeros_like(c1)
        for index in range(3):
            along = (
                columns[index][0] * offset[0]
                + columns[index][1] * offset[1]
                + columns[index][2] * offset[2]
            )
            kappa = kappa + raw[index : index + 1] * along * along
        rows.append(STEP_SCALE * kappa / (length_sq * length_sq))
    rows.append(raw[6:7])
    return rows


def lane_of(shape):
    return lax.broadcasted_iota(jnp.int32, shape, len(shape) - 1)


def pack_kernel(temp, material, plate, cooling, raw, own, send_a, send_b, pack, table):
    depth, rows, _ = temp.shape
    lane = lane_of((depth, LANES))
    packs = [jnp.zeros((depth, LANES), jnp.float32) for _ in range(3)]
    for x in range(rows):
        fields = (
            temp[:, x, :],
            (material[:, x, :] + 1).astype(jnp.float32),
            cooling[:, x, :] * plate[:, x, :].astype(jnp.float32),
        )
        mine = (lane >= SLOT * x) & (lane < SLOT * (x + 1))
        for f in range(3):
            own[f, x] = fields[f]
            moved = pltpu.roll(fields[f], (SLOT * x + HALO) % LANES, 1)
            packs[f] = jnp.where(mine, moved, packs[f])
    even = lax.rem(lax.axis_index("gx"), 2) == 0
    first_a = jnp.where(even, rows - HALO, 0)
    first_b = jnp.where(even, 0, rows - HALO)
    for f in range(3):
        pack[f] = packs[f]
        for r in range(HALO):
            send_a[f, r] = own[f, first_a + r]
            send_b[f, r] = own[f, first_b + r]
    for k, row in enumerate(table_rows(raw)):
        table[k] = jnp.broadcast_to(row, (8, LANES))


class Field:
    def __init__(self):
        self.where = {}

    def add(self, ref, rows, lead=(), first=None):
        for r in rows:
            self.where[r] = (ref, (*lead, r if first is None else r - first))

    def get(self, r, t, start=None, size=16):
        ref, index = self.where[r]
        if start is None:
            return ref[(*index, t)]
        return ref[(*index, t, pl.ds(start, size))]

    def put(self, r, t, value, start=None):
        ref, index = self.where[r]
        if start is None:
            ref[(*index, t)] = value
        else:
            ref[(*index, t, pl.ds(start, value.shape[0]))] = value


PAD = 8
DEPTH_PAD = 8 + 16 + 8


def clear_pads(field, rows, depth, tiles=(0, 1)):
    zero = jnp.zeros((8, LANES), jnp.float32)
    for r in rows:
        for t in tiles:
            field.put(r, t, zero, 0)
            field.put(r, t, zero, PAD + depth)


def lane_shift(pair, by):
    lane = lane_of(pair[0].shape)
    moved = [pltpu.roll(value, (-by) % LANES, 1) for value in pair]
    edge = lane == (LANES - 1 if by > 0 else 0)
    return [jnp.where(edge, moved[1 - t], moved[t]) for t in (0, 1)]


def put_shifted(fields, r, pair):
    for by in (-1, 0, 1):
        moved = pair if by == 0 else lane_shift(pair, by)
        for t in (0, 1):
            fields[by].put(r, t, moved[t], PAD)


def near_sum(weights, fields, r, t, depth, cache):
    total = None

    def read(oz, ox, oy):
        key = (oz, r + ox, oy, t)
        if key not in cache:
            cache[key] = fields[oy].get(r + ox, t, PAD + oz, depth)
        return cache[key]

    for k, (oz, ox, oy) in enumerate(HALF_OFFSETS):
        term = weights[k].get(r, t, PAD, depth) * (read(oz, ox, oy) + read(-oz, -ox, -oy))
        total = term if total is None else total + term
    return total


def expand(table, weights, ids, rows, depth):
    for r in rows:
        for t in (0, 1):
            index = ids.get(r, t).astype(jnp.int32)
            for half in range(depth // 8):
                part = index[8 * half : 8 * half + 8]
                for k in range(LINKS + 1):
                    got = jnp.take_along_axis(
                        table[k], part, axis=1, mode="promise_in_bounds"
                    )
                    weights[k].put(r, t, got, PAD + 8 * half)


def rate_of(state):
    good = state > 0.5
    inverse = 1.0 / jnp.where(good, state, 1.0)
    return jnp.where(good, jnp.exp(AGE_BETA * (1.0 - inverse)), 0.0), inverse


class Plan:
    def __init__(self, rows):
        self.rows = rows
        self.all = range(rows + 2 * HALO)

    def cone(self, radius):
        return range(HALO - radius, HALO + self.rows + radius)

    def ring(self, radius, inner):
        middle = self.cone(inner)
        return [r for r in self.cone(radius) if r not in middle]


def front_kernel(
    own, got_a, got_b, mid, mid_a, mid_b, table,
    ext, weights_ref, diag_ref, shifted_ref, third_ref, part,
    valid_ref,
):
    _, rows, depth, _ = own.shape
    plan = Plan(rows)
    even = lax.rem(lax.axis_index("gx"), 2) == 0
    base_a = jnp.where(even, HALO + rows, 0)
    base_b = jnp.where(even, 0, HALO + rows)
    lane = lane_of((depth, LANES))
    halo_lane = (lane < HALO) | (lane >= LANES - HALO)
    for f in range(3):
        for r in range(HALO):
            ext[f, base_a + r, 0] = got_a[f, r]
            ext[f, base_b + r, 0] = got_b[f, r]
        for x in range(rows):
            ext[f, HALO + x, 0] = own[f, x]
        low = jnp.where(even, mid_b[f], mid_a[f])
        high = jnp.where(even, mid_a[f], mid_b[f])
        for r in plan.all:
            x = r - HALO
            source, x = (
                (low, x + rows) if x < 0 else (high, x - rows) if x >= rows else (mid[f], x)
            )
            moved = pltpu.roll(source, (-(SLOT * x + HALO)) % LANES, 1)
            ext[f, r, 1] = jnp.where(halo_lane, moved, 0.0)

    temp, ids, coeff = Field(), Field(), Field()
    for field, f in ((temp, T0), (ids, ID), (coeff, COEFF)):
        field.add(ext, plan.all, (f,))
    weights = [Field() for _ in range(LINKS + 1)]
    for k in range(LINKS + 1):
        weights[k].add(weights_ref, plan.cone(2), (k,), HALO - 2)
        clear_pads(weights[k], plan.cone(2), depth)
    diag = Field()
    diag.add(diag_ref, plan.cone(2), (), HALO - 2)
    valid = {}
    shifted = []
    for oy in (-1, 0, 1):
        valid[oy] = Field()
        valid[oy].add(valid_ref, plan.cone(3), (oy + 1,), HALO - 3)
        clear_pads(valid[oy], plan.cone(3), depth)
    for n in range(3):
        shifted.append({})
        for oy in (-1, 0, 1):
            shifted[n][oy] = Field()
            shifted[n][oy].add(shifted_ref, plan.cone(3 - n), (n, oy + 1), HALO - 3)
            clear_pads(shifted[n][oy], plan.cone(3 - n), depth)

    expand(table, weights, ids, plan.cone(2), depth)
    for r in plan.cone(3):
        put_shifted(valid, r, [jnp.where(ids.get(r, t) > 0.5, 1.0, 0.0) for t in (0, 1)])
        put_shifted(shifted[0], r, [temp.get(r, t) for t in (0, 1)])
    cache = {}
    for r in plan.cone(2):
        for t in (0, 1):
            diag.put(r, t, coeff.get(r, t) + near_sum(weights, valid, r, t, depth, cache))
    loss = jnp.zeros((depth, LANES), jnp.float32)
    for n in range(STEPS):
        cache = {}
        for r in plan.cone(2 - n):
            pair = []
            for t in (0, 1) if n < 2 else (0,):
                center = shifted[n][0].get(r, t, PAD, depth)
                near = near_sum(weights, shifted[n], r, t, depth, cache)
                pair.append(
                    (1.0 - diag.get(r, t)) * center + near + coeff.get(r, t) * COOL_TEMP
                )
            if n < 2:
                put_shifted(shifted[n + 1], r, pair)
            else:
                third_ref[r - HALO] = pair[0]
            if HALO <= r < HALO + rows:
                rate, _ = rate_of(pair[0])
                loss = loss + weights[LINKS].get(r, 0, PAD, depth) * rate
    part[...] = jnp.broadcast_to(jnp.sum(loss, axis=0, keepdims=True), part.shape)


def back_kernel(
    ext, weights_in, diag_in, shifted_in, third_in, table,
    adjoint_out, sens_out,
    weights_ref, diag_ref, valid_ref, shifted_ref, state_ref, adjoint_ref,
):
    rows = third_in.shape[0]
    depth = third_in.shape[1]
    plan = Plan(rows)
    temp, ids, coeff = Field(), Field(), Field()
    for field, f in ((temp, T0), (ids, ID), (coeff, COEFF)):
        field.add(ext, plan.all, (f,))
    outer = plan.ring(5, 2)
    slot = {r: (r - 1 if r < HALO else r - rows - 5) for r in outer}

    def ring_field(ref, lead, rows_):
        field = Field()
        for r in rows_:
            field.where[r] = (ref, (*lead, slot[r]))
        return field

    weights = []
    for k in range(LINKS + 1):
        field = ring_field(weights_ref, (k,), outer)
        clear_pads(field, [r for r in outer if r in plan.cone(3)], depth)
        field.add(weights_in, plan.cone(2), (k,), HALO - 2)
        weights.append(field)
    diag = ring_field(diag_ref, (), outer)
    diag.add(diag_in, plan.cone(2), (), HALO - 2)
    valid, shifted = {}, [{}, {}, {}]
    valid_rows = [r for r in plan.all if r not in plan.cone(1)]
    for oy in (-1, 0, 1):
        valid[oy] = Field()
        for i, r in enumerate(valid_rows):
            valid[oy].where[r] = (valid_ref, (oy + 1, i))
        clear_pads(valid[oy], valid_rows, depth)
        for n in range(3):
            shifted[n][oy] = Field()
            inner = plan.cone(3 - n)
            fresh = plan.ring(6 - n, 3 - n)
            for i, r in enumerate(fresh):
                shifted[n][oy].where[r] = (shifted_ref, (n, oy + 1, i))
            clear_pads(shifted[n][oy], fresh, depth)
            shifted[n][oy].add(shifted_in, inner, (n, oy + 1), HALO - 3)

    expand(table, weights, ids, outer, depth)
    for r in valid_rows:
        put_shifted(valid, r, [jnp.where(ids.get(r, t) > 0.5, 1.0, 0.0) for t in (0, 1)])
    for r in plan.ring(6, 3):
        put_shifted(shifted[0], r, [temp.get(r, t) for t in (0, 1)])
    cache = {}
    for r in outer:
        for t in (0, 1):
            diag.put(r, t, coeff.get(r, t) + near_sum(weights, valid, r, t, depth, cache))
    third = Field()
    third.add(state_ref, plan.cone(3), (), HALO - 3)
    for n in range(STEPS):
        cache = {}
        todo = [(r, t) for r in plan.ring(5 - n, 2 - n) for t in (0, 1)]
        if n == 2:
            todo = todo + [(r, 1) for r in plan.cone(0)]
        pair = {}
        for r, t in todo:
            center = shifted[n][0].get(r, t, PAD, depth)
            near = near_sum(weights, shifted[n], r, t, depth, cache)
            value = (1.0 - diag.get(r, t)) * center + near + coeff.get(r, t) * COOL_TEMP
            if n == 2:
                third.put(r, t, value)
                continue
            pair[t] = value
            if t == 1:
                put_shifted(shifted[n + 1], r, [pair[0], pair[1]])
    for r in plan.cone(0):
        third.put(r, 0, third_in[r - HALO])

    def state_of(n, r, t):
        return third.get(r, t) if n == 3 else shifted[n][0].get(r, t, PAD, depth)

    def drive(n, r, t):
        rate, inverse = rate_of(state_of(n, r, t))
        return weights[LINKS].get(r, t, PAD, depth) * AGE_BETA * rate * (inverse * inverse)

    vectors = []
    for n in range(3):
        field = Field()
        field.add(adjoint_ref, plan.cone(3 - n), (n,), HALO - 3)
        clear_pads(field, plan.cone(3 - n), depth)
        vectors.append(field)
    for r in plan.cone(3):
        for t in (0, 1):
            vectors[0].put(r, t, drive(3, r, t), PAD)
    sens = {r: jnp.zeros((depth, LANES), jnp.float32) for r in plan.cone(0)}
    for n in range(3):
        vector = vectors[n]
        sums = {}
        for source in plan.cone(3 - n):
            for t in (0, 1):
                reads = {oz: vector.get(source, t, PAD - oz, depth) for oz in (-1, 0, 1)}
                for k, offset in enumerate(HALF_OFFSETS):
                    product = {}
                    for sign in (1, -1):
                        oz, ox, oy = (sign * o for o in offset)
                        target = source + ox
                        if oz not in product:
                            product[oz] = reads[oz] * weights[k].get(source, t, PAD - oz, depth)
                        if target in plan.cone(2 - n):
                            key = (target, oy, t)
                            sums[key] = sums[key] + product[oz] if key in sums else product[oz]
            target = source - 1
            if target not in plan.cone(2 - n):
                continue
            plus = lane_shift([sums.pop((target, 1, t)) for t in (0, 1)], -1)
            minus = lane_shift([sums.pop((target, -1, t)) for t in (0, 1)], 1)
            for t in (0, 1) if n < 2 else (0,):
                result = (
                    (1.0 - diag.get(target, t)) * vector.get(target, t, PAD, depth)
                    + sums.pop((target, 0, t))
                    + (plus[t] + minus[t])
                )
                if n < 2:
                    vectors[n + 1].put(target, t, result + drive(2 - n, target, t), PAD)
                else:
                    adjoint_out[:, target - HALO, :] = result
    for r in plan.cone(0):
        total = None
        for n in range(3):
            term = vectors[2 - n].get(r, 0, PAD, depth) * (state_of(n, r, 0) - COOL_TEMP)
            total = term if total is None else total + term
        sens_out[:, r - HALO, :] = -total


def pairing(count, first):
    out = {}
    for i in range(first, count - 1, 2):
        out[i], out[i + 1] = i + 1, i
    return out


def swap(value, sizes, axis, first):
    count_x, count_y = sizes
    partner = pairing(sizes[axis], first)
    pairs = []
    for i in range(count_x):
        for j in range(count_y):
            other = partner.get((i, j)[axis])
            if other is not None:
                target = (other, j) if axis == 0 else (i, other)
                pairs.append((i * count_y + j, target[0] * count_y + target[1]))
    return lax.ppermute(value, ("gx", "gy"), pairs)


def local(initial_temp, material, plate, cooling, principal, angles, aging_scale):
    depth, rows, width = initial_temp.shape
    sizes = (lax.axis_size("gx"), lax.axis_size("gy"))
    devices = sizes[0] * sizes[1]
    f32 = jnp.float32

    def shape(*dims):
        return jax.ShapeDtypeStruct(dims, f32)

    raw = jnp.concatenate([principal, angles, aging_scale[:, None]], axis=1).T
    raw = jnp.pad(raw, ((0, 1), (1, LANES - 1 - raw.shape[1])))
    own, send_a, send_b, pack, table = pl.pallas_call(
        pack_kernel,
        out_shape=(
            shape(3, rows, depth, LANES),
            shape(3, HALO, depth, LANES),
            shape(3, HALO, depth, LANES),
            shape(3, depth, LANES),
            shape(LINKS + 1, 8, LANES),
        ),
        in_specs=[VMEM] * 5,
        out_specs=(VMEM,) * 5,
        name="pack",
    )(initial_temp, material, plate, cooling, raw)

    side_b = swap(pack, sizes, 1, 1)
    side_a = swap(pack, sizes, 1, 0)
    got_b = swap(send_b, sizes, 0, 1)
    got_a = swap(send_a, sizes, 0, 0)
    even = lax.rem(lax.axis_index("gy"), 2) == 0
    lane = lane_of(pack.shape)
    from_left = lax.rem(lane, SLOT) < HALO
    mid = jnp.where(from_left == even, side_b, side_a)
    mid_b = swap(mid, sizes, 0, 1)
    mid_a = swap(mid, sizes, 0, 0)

    total_rows = rows + 2 * HALO
    ext, weights, diag, shifted, third, part = pl.pallas_call(
        front_kernel,
        out_shape=(
            shape(3, total_rows, 2, depth, LANES),
            shape(LINKS + 1, rows + 4, 2, DEPTH_PAD, LANES),
            shape(rows + 4, 2, depth, LANES),
            shape(3, 3, rows + 6, 2, DEPTH_PAD, LANES),
            shape(rows, depth, LANES),
            shape(devices, LANES),
        ),
        in_specs=[VMEM] * 7,
        out_specs=(VMEM,) * 6,
        scratch_shapes=[pltpu.VMEM((3, rows + 6, 2, DEPTH_PAD, LANES), f32)],
        name="front",
    )(own, got_a, got_b, mid, mid_a, mid_b, table)

    parts = lax.all_to_all(part, ("gx", "gy"), 0, 0, tiled=True)

    adjoint, sens = pl.pallas_call(
        back_kernel,
        out_shape=(shape(depth, rows, LANES), shape(depth, rows, LANES)),
        in_specs=[VMEM] * 6,
        out_specs=(VMEM,) * 2,
        scratch_shapes=[
            pltpu.VMEM((LINKS + 1, 6, 2, DEPTH_PAD, LANES), f32),
            pltpu.VMEM((6, 2, depth, LANES), f32),
            pltpu.VMEM((3, 10, 2, DEPTH_PAD, LANES), f32),
            pltpu.VMEM((3, 3, 6, 2, DEPTH_PAD, LANES), f32),
            pltpu.VMEM((rows + 6, 2, depth, LANES), f32),
            pltpu.VMEM((3, rows + 6, 2, DEPTH_PAD, LANES), f32),
        ],
        name="back",
    )(ext, weights, diag, shifted, third, table)

    scale = float(depth * rows * width * devices) / jnp.sum(parts)
    return adjoint * scale, sens * plate.astype(f32) * scale


def solution(mesh):
    block = P(None, "gx", "gy")
    return jax.shard_map(
        local,
        mesh=mesh,
        in_specs=(block, block, block, block, P(), P(), P()),
        out_specs=(block, block),
        check_vma=False,
    )
```

time: 178 us -> 42.6 us (0.24)
  starting transfers between devices: 63 us -> 18.4 us
  blocking collectives: 42.1 us -> 0 us
  waiting for transfers between devices: 43 us -> 1.44 us
  Pallas kernels: 0 us -> 16.7 us
  other arithmetic: 17.7 us -> 2.91 us
  local copies, waits for them, and re-layouts: 5.97 us -> 1.36 us
  between operations: 3.95 us -> 1.43 us
    ppermute x28 -> x6, starting transfers between devices: 63 us -> 9.24 us  [swap(): return lax.ppermute(value, ('gx', 'gy'), pairs)]
    psum x1 -> x0, blocking collectives: 42.1 us -> none  [local(): total = lax.psum(local_total, ('gx', 'gy'))]
    ppermute x28 -> x6, waiting for transfers between devices: 43 us -> 1.43 us  [swap(): return lax.ppermute(value, ('gx', 'gy'), pairs)]
    pallas_call x0 -> x3, Pallas kernels: none -> 16.7 us  [the longest x1 8 us: local(): pl.pallas_call(back_kernel, out_shape=(shape(depth, rows, LANES), shape(d...]
    all_to_all x0 -> x1, starting transfers between devices: none -> 9.12 us  [local(): parts = lax.all_to_all(part, ('gx', 'gy'), 0, 0, tiled=True)]
    div x8 -> x0, other arithmetic: 5.99 us -> none  [the longest x7 5.94 us: weight_table(): rows.append(STEP_SCALE * kappa / (length_sq * length_sq))]
    slice x16 -> x0, local copies, waits for them, and re-layouts: 5.24 us -> none  [the longest x1 1.96 us: local(): inner[index]]
    mul x17 -> x1, other arithmetic: 5.79 us -> 1.54 us  [local(): return (adjoint * scale, sens * plate.astype(f32) * scale)]
  transfers between devices with their start and end apart: 28 -> 7, of which waited for: 13 -> 2; matrix products, arithmetic and copies ran while one was open for 8% -> 0% of each run, Pallas kernels for 0% -> 19%
where the time goes in v1:
time: 42.6 us; the launch traced here: 42.2 us
  starting transfers between devices  18.4 us (43%)
  Pallas kernels  16.7 us (39%)
  other arithmetic  2.91 us (7%)
  waiting for transfers between devices  1.44 us (3%)
  between operations  1.43 us (3%)
  local copies, waits for them, and re-layouts  1.36 us (3%)
    ppermute x6, starting transfers between devices, swap(): return lax.ppermute(value, ('gx', 'gy'), pairs)  9.24 us
    all_to_all x1, starting transfers between devices, local(): parts = lax.all_to_all(part, ('gx', 'gy'), 0, 0, tiled=True)  9.12 us
    pallas_call x1, Pallas kernels, local(): pl.pallas_call(back_kernel, out_shape=(shape(depth, rows, LANES), shape(d...  8 us
    pallas_call x1, Pallas kernels, local(): pl.pallas_call(front_kernel, out_shape=(shape(3, total_rows, 2, depth, LA...  6.72 us
    pallas_call x1, Pallas kernels, local(): pl.pallas_call(pack_kernel, out_shape=(shape(3, rows, depth, LANES), shap...  1.96 us
    mul x1, other arithmetic, local(): return (adjoint * scale, sens * plate.astype(f32) * scale)  1.54 us
    ppermute x6, waiting for transfers between devices, swap(): return lax.ppermute(value, ('gx', 'gy'), pairs)  1.43 us
  transfers between devices with their start and end apart: 7, of which 2 were waited for; matrix products, arithmetic and copies ran while one was open for 0% of the time, Pallas kernels for 19%

profile of v1, /device:TPU:0, one launch (start us, length us, event | category | flops | bytes accessed | tf_op | source)
XLA Modules:
  0.0 42.2 jit_solution(11940648316461660301)
XLA Ops:
  0.6 0.7 %maximum_bitcast_fusion = f32[7,16]{1,0:T(8,128)S(1)} fusion(f32[16,1]{0,1:T(1,128)} %bitcast.7, f32[16,3]{0,1:T(4,128)} %param.12, f32[16,3]{0,1:T(4,128)} %param.11), kind=kLoop, calls=%fused_computation.3 | loop fusion | flops 224 | bytes 896 | tf_op jit(solution)/shard_map/transpose | solution.py:419
  1.4 0.7 %pad.4.raw = f32[8,128]{1,0:T(8,128)} pad(f32[7,16]{1,0:T(8,128)S(1)} %maximum_bitcast_fusion, f32[]{:T(128)} %constant.17.clone.1), padding=0_1x1_111 | pad | bytes 4548 | tf_op jit(solution)/shard_map/jit(_pad)/pad | solution.py:420
  2.0 2.0 %pack.1 = (f32[3,8,16,128]{3,2,1,0:T(8,128)}, f32[3,6,16,128]{3,2,1,0:T(8,128)}, f32[3,6,16,128]{3,2,1,0:T(8,128)}, f32[3,16,128]{2,1,0:T(8,128)}, f32[14,8,128]{2,1,0:T(8,128)}) custom-call(f32[16,8,128]{2,1,0:T(8,128)} %temp.1, s32[16,8,128]{2,1,0:T(8,128)} %material.1, s32[16,8,128]{2,1,0:T(8,128)} %plate.1, f32[16,8,128]{2,1,0:T(8,128)} %cooling.1, ...), custom_call_target="tpu_custom_call" | custom-call | tf_op jit(solution)/shard_map/pack/pallas_call | solution.py:421
  4.0 3.0 %collective-permute-start.3 = (f32[3,16,128]{2,1,0:T(8,128)}, f32[3,16,128]{2,1,0:T(8,128)S(1)}, u32[]{:S(2)}, u32[]{:S(2)}) collective-permute-start(f32[3,16,128]{2,1,0:T(8,128)} %get-tuple-element.18), channel_id=1, source_target_pairs={{0,1},{1,0},{2,3},{3,2},{4,5},{5,4},{6,7},{7,6},{8,9},{9,8},{10,11... | collective-permute-start | bytes 73736 | tf_op jit(solution)/shard_map/ppermute | solution.py:407
  7.0 0.7 %collective-permute-start.2 = (f32[3,16,128]{2,1,0:T(8,128)}, f32[3,16,128]{2,1,0:T(8,128)S(1)}, u32[]{:S(2)}, u32[]{:S(2)}) collective-permute-start(f32[3,16,128]{2,1,0:T(8,128)} %get-tuple-element.18), channel_id=1, source_target_pairs={{1,2},{2,1},{5,6},{6,5},{9,10},{10,9},{13,14},{14,13},{17,18},{18,... | collective-permute-start | bytes 73736 | tf_op jit(solution)/shard_map/ppermute | solution.py:407
  7.6 0.1 collective-permute-start
  7.7 0.7 %collective-permute-start.1 = (f32[3,6,16,128]{3,2,1,0:T(8,128)}, f32[3,6,16,128]{3,2,1,0:T(8,128)S(1)}, u32[]{:S(2)}, u32[]{:S(2)}) collective-permute-start(f32[3,6,16,128]{3,2,1,0:T(8,128)} %get-tuple-element.17), channel_id=1, source_target_pairs={{4,8},{5,9},{6,10},{7,11},{8,4},{9,5},{10,6},{11,7},{12,16},{13,17... | collective-permute-start | bytes 442376 | tf_op jit(solution)/shard_map/ppermute | solution.py:407
  8.4 0.6 %collective-permute-done.3 = f32[3,16,128]{2,1,0:T(8,128)S(1)} collective-permute-done((f32[3,16,128]{2,1,0:T(8,128)}, f32[3,16,128]{2,1,0:T(8,128)S(1)}, u32[]{:S(2)}, u32[]{:S(2)}) %collective-permute-start.3) | collective-permute-done | bytes 24608 | tf_op jit(solution)/shard_map/ppermute | solution.py:407
  9.0 0.0 collective-permute-done.2
  9.0 0.0 copy-start.3
  9.0 0.7 %collective-permute-start.5 = (f32[3,16,128]{2,1,0:T(8,128)S(1)}, f32[3,16,128]{2,1,0:T(8,128)S(1)}, u32[]{:S(2)}, u32[]{:S(2)}) collective-permute-start(f32[3,16,128]{2,1,0:T(8,128)S(1)} %broadcast_select_fusion.mid), channel_id=1, source_target_pairs={{4,8},{5,9},{6,10},{7,11},{8,4},{9,5},{10,6},{11,7},{12,16},{13,17... | collective-permute-start | bytes 73736 | tf_op jit(solution)/shard_map/ppermute | solution.py:407
  9.7 4.2 %collective-permute-start.4 = (f32[3,16,128]{2,1,0:T(8,128)S(1)}, f32[3,16,128]{2,1,0:T(8,128)S(1)}, u32[]{:S(2)}, u32[]{:S(2)}) collective-permute-start(f32[3,16,128]{2,1,0:T(8,128)S(1)} %broadcast_select_fusion.mid), channel_id=1, source_target_pairs={{0,4},{1,5},{2,6},{3,7},{4,0},{5,1},{6,2},{7,3},{8,12},{9,13},{10,... | collective-permute-start | bytes 73736 | tf_op jit(solution)/shard_map/ppermute | solution.py:407
  13.9 0.8 %collective-permute-done.4.mid_a = f32[3,16,128]{2,1,0:T(8,128)S(1)} collective-permute-done((f32[3,16,128]{2,1,0:T(8,128)S(1)}, f32[3,16,128]{2,1,0:T(8,128)S(1)}, u32[]{:S(2)}, u32[]{:S(2)}) %collective-permute-start.4) | collective-permute-done | bytes 24608 | tf_op jit(solution)/shard_map/ppermute | solution.py:407
  14.7 0.0 collective-permute-done.got_a
  14.7 0.0 collective-permute-done.1.got_b
  14.8 0.6 %copy-done.5 = f32[3,16,128]{2,1,0:T(8,128)} copy-done((f32[3,16,128]{2,1,0:T(8,128)}, f32[3,16,128]{2,1,0:T(8,128)S(1)}, u32[]{:S(2)}) %copy-start.5) | copy-done | bytes 24600
  15.3 0.1 copy-done.1
  15.4 0.1 copy-done.2
  15.5 6.7 %front.1 = (f32[3,20,2,16,128]{4,3,2,1,0:T(8,128)}, f32[14,12,2,32,128]{4,3,2,1,0:T(8,128)}, f32[12,2,16,128]{3,2,1,0:T(8,128)}, f32[3,3,14,2,32,128]{5,4,3,2,1,...) custom-call(f32[3,8,16,128]{3,2,1,0:T(8,128)} %get-tuple-element.15.own, f32[3,6,16,128]{3,2,1,0:T(8,128)} %copy-done.1, ...), custom_call_target="tpu_custom_call" | custom-call | tf_op jit(solution)/shard_map/front/pallas_call | solution.py:447
  22.2 9.1 %all-to-all-start = ((f32[32,1,128]{2,1,0:T(1,128)}), f32[32,1,128]{2,1,0:T(1,128)S(1)}, u32[]{:S(2)}, u32[]{:S(2)}) async-start(f32[32,1,128]{2,1,0:T(1,128)} %bitcast.6), calls=%async_computation | async-start | bytes 32768 | tf_op jit(solution)/shard_map/all_to_all | solution.py:463
  31.3 8.0 %back.1 = (f32[16,8,128]{2,1,0:T(8,128)}, f32[16,8,128]{2,1,0:T(8,128)}) custom-call(f32[3,20,2,16,128]{4,3,2,1,0:T(8,128)} %get-tuple-element.20.ext, f32[14,12,2,32,128]{4,3,2,1,0:T(8,128)} %get-tuple-element.21.weights_in, f32[12,2,16,128]{3,2,1,0:T(8,128)} %get-tuple-element.22.diag_in, f32[3,3,14,2,32,128]{5,4,3,2,1,0:T(8,128)} %get-tuple-element.23.shifted_in, ...), custom_call_target="tpu_custom_call" | custom-call | tf_op jit(solution)/shard_map/back/pallas_call | solution.py:465
  39.3 0.0 all-to-all-done
  39.3 0.6 %reduce_sum.9 = f32[]{:T(128)} reduce(f32[32,1,128]{2,1,0:T(1,128)S(1)} %all-to-all-done, f32[]{:T(128)} %constant.17.clone.1), dimensions={0,1,2}, to_apply=%region_0.1 | reduce | flops 4095 | bytes 16392 | tf_op jit(solution)/shard_map/reduce_sum | solution.py:481
  40.6 1.5 %multiply_multiply_fusion = (f32[16,8,128]{2,1,0:T(8,128)}, f32[16,8,128]{2,1,0:T(8,128)}) fusion(f32[16,8,128]{2,1,0:T(8,128)} %get-tuple-element.27, s32[16,8,128]{2,1,0:T(8,128)S(1)} %copy-done, f32[]{:T(128)S(6)} %div.3, f32[16,8,128]{2,1,0:T(8,128)} %get-tuple-element.25), kind=kLoop, calls=%fused_computation | loop fusion | flops 65536 | bytes 327684 | tf_op jit(solution)/shard_map/mul | solution.py:482
  (11 shorter events, 0.0 us)
Async XLA Ops:
  4.0 5.0 %collective-permute-start.3 = (f32[3,16,128]{2,1,0:T(8,128)}, f32[3,16,128]{2,1,0:T(8,128)S(1)}, u32[]{:S(2)}, u32[]{:S(2)}) collective-permute-start(f32[3,16,128]{2,1,0:T(8,128)} %get-tuple-element.18), channel_id=1, source_target_pairs={{0,1},{1,0},{2,3},{3,2},{4,5},{5,4},{6,7},{7,6},{8,9},{9,8},{10,11... | collective-permute-start | bytes 73736 | tf_op jit(solution)/shard_map/ppermute | solution.py:407
  7.0 2.0 %collective-permute-start.2 = (f32[3,16,128]{2,1,0:T(8,128)}, f32[3,16,128]{2,1,0:T(8,128)S(1)}, u32[]{:S(2)}, u32[]{:S(2)}) collective-permute-start(f32[3,16,128]{2,1,0:T(8,128)} %get-tuple-element.18), channel_id=1, source_target_pairs={{1,2},{2,1},{5,6},{6,5},{9,10},{10,9},{13,14},{14,13},{17,18},{18,... | collective-permute-start | bytes 73736 | tf_op jit(solution)/shard_map/ppermute | solution.py:407
  7.6 7.1 %collective-permute-start = (f32[3,6,16,128]{3,2,1,0:T(8,128)}, f32[3,6,16,128]{3,2,1,0:T(8,128)S(1)}, u32[]{:S(2)}, u32[]{:S(2)}) collective-permute-start(f32[3,6,16,128]{3,2,1,0:T(8,128)} %get-tuple-element.16), channel_id=1, source_target_pairs={{0,4},{1,5},{2,6},{3,7},{4,0},{5,1},{6,2},{7,3},{8,12},{9,13},{10,... | collective-permute-start | bytes 442376 | tf_op jit(solution)/shard_map/ppermute | solution.py:407
  7.7 7.1 %collective-permute-start.1 = (f32[3,6,16,128]{3,2,1,0:T(8,128)}, f32[3,6,16,128]{3,2,1,0:T(8,128)S(1)}, u32[]{:S(2)}, u32[]{:S(2)}) collective-permute-start(f32[3,6,16,128]{3,2,1,0:T(8,128)} %get-tuple-element.17), channel_id=1, source_target_pairs={{4,8},{5,9},{6,10},{7,11},{8,4},{9,5},{10,6},{11,7},{12,16},{13,17... | collective-permute-start | bytes 442376 | tf_op jit(solution)/shard_map/ppermute | solution.py:407
  9.0 5.8 %copy-start.3 = (f32[3,16,128]{2,1,0:T(8,128)}, f32[3,16,128]{2,1,0:T(8,128)S(1)}, u32[]{:S(2)}) copy-start(f32[3,16,128]{2,1,0:T(8,128)S(1)} %broadcast_select_fusion.mid) | copy-start | bytes 73732
  9.0 4.9 %collective-permute-start.5 = (f32[3,16,128]{2,1,0:T(8,128)S(1)}, f32[3,16,128]{2,1,0:T(8,128)S(1)}, u32[]{:S(2)}, u32[]{:S(2)}) collective-permute-start(f32[3,16,128]{2,1,0:T(8,128)S(1)} %broadcast_select_fusion.mid), channel_id=1, source_target_pairs={{4,8},{5,9},{6,10},{7,11},{8,4},{9,5},{10,6},{11,7},{12,16},{13,17... | collective-permute-start | bytes 73736 | tf_op jit(solution)/shard_map/ppermute | solution.py:407
  9.7 5.1 %collective-permute-start.4 = (f32[3,16,128]{2,1,0:T(8,128)S(1)}, f32[3,16,128]{2,1,0:T(8,128)S(1)}, u32[]{:S(2)}, u32[]{:S(2)}) collective-permute-start(f32[3,16,128]{2,1,0:T(8,128)S(1)} %broadcast_select_fusion.mid), channel_id=1, source_target_pairs={{0,4},{1,5},{2,6},{3,7},{4,0},{5,1},{6,2},{7,3},{8,12},{9,13},{10,... | collective-permute-start | bytes 73736 | tf_op jit(solution)/shard_map/ppermute | solution.py:407
  13.9 0.9 %copy-start.4 = (f32[3,16,128]{2,1,0:T(8,128)}, f32[3,16,128]{2,1,0:T(8,128)S(1)}, u32[]{:S(2)}) copy-start(f32[3,16,128]{2,1,0:T(8,128)S(1)} %collective-permute-done.5.mid_b) | copy-start | bytes 73732
  14.7 0.6 %copy-start.5 = (f32[3,16,128]{2,1,0:T(8,128)}, f32[3,16,128]{2,1,0:T(8,128)S(1)}, u32[]{:S(2)}) copy-start(f32[3,16,128]{2,1,0:T(8,128)S(1)} %collective-permute-done.4.mid_a) | copy-start | bytes 73732
  14.7 0.7 %copy-start.1 = (f32[3,6,16,128]{3,2,1,0:T(8,128)}, f32[3,6,16,128]{3,2,1,0:T(8,128)S(1)}, u32[]{:S(2)}) copy-start(f32[3,6,16,128]{3,2,1,0:T(8,128)S(1)} %collective-permute-done.got_a) | copy-start | bytes 442372
  14.8 0.7 %copy-start.2 = (f32[3,6,16,128]{3,2,1,0:T(8,128)}, f32[3,6,16,128]{3,2,1,0:T(8,128)S(1)}, u32[]{:S(2)}) copy-start(f32[3,6,16,128]{3,2,1,0:T(8,128)S(1)} %collective-permute-done.1.got_b) | copy-start | bytes 442372
  22.2 18.5 %copy-start = (s32[16,8,128]{2,1,0:T(8,128)S(1)}, s32[16,8,128]{2,1,0:T(8,128)}, u32[]{:S(2)}) copy-start(s32[16,8,128]{2,1,0:T(8,128)} %plate.1) | copy-start | bytes 196612
  22.2 17.1 %all-to-all-start = ((f32[32,1,128]{2,1,0:T(1,128)}), f32[32,1,128]{2,1,0:T(1,128)S(1)}, u32[]{:S(2)}, u32[]{:S(2)}) async-start(f32[32,1,128]{2,1,0:T(1,128)} %bitcast.6), calls=%async_computation | async-start | bytes 32768 | tf_op jit(solution)/shard_map/all_to_all | solution.py:463

commit v2 on v1

v2 whole, which is shorter than its diff:
```python
import functools

import jax
import jax.numpy as jnp
from jax import lax
from jax.experimental import pallas as pl
from jax.experimental.pallas import tpu as pltpu
from jax.sharding import PartitionSpec as P

STEPS = 3
STEP_SCALE = 0.06
COOL_TEMP = 0.85
AGE_BETA = 8.0
HALF_OFFSETS = [
    (first, second, third)
    for first in (-1, 0, 1)
    for second in (-1, 0, 1)
    for third in (-1, 0, 1)
    if (first, second, third) > (0, 0, 0)
]
LINKS = len(HALF_OFFSETS)
HALO = 2 * STEPS
LANES = 128
SLOT = 16
T0, ID, COEFF = 0, 1, 2
VMEM = pl.BlockSpec(memory_space=pltpu.VMEM)
PAD = 8
GUARD = 8
PARTS = 7


def lane_of(shape):
    return lax.broadcasted_iota(jnp.int32, shape, len(shape) - 1)


def table_kernel(principal, angles, aging, table, line):
    count = aging.shape[1]
    line[...] = jnp.zeros_like(line)
    line[0:3, 0:count] = principal[...]
    line[3:6, 0:count] = angles[...]
    line[6:7, 0:count] = aging[...]
    raw = pltpu.roll(line[...], 1, 1)
    p = [raw[k : k + 1] for k in range(3)]
    cosine, sine = jnp.cos(raw[3:6]), jnp.sin(raw[3:6])
    c1, c2, c3 = cosine[0:1], cosine[1:2], cosine[2:3]
    s1, s2, s3 = sine[0:1], sine[1:2], sine[2:3]
    columns = [
        (c1 * c3 - s1 * c2 * s3, s1 * c3 + c1 * c2 * s3, s2 * s3),
        (-c1 * s3 - s1 * c2 * c3, -s1 * s3 + c1 * c2 * c3, s2 * c3),
        (s1 * s2, -c1 * s2, c2),
    ]
    rows = []
    for i, j, factor in ((0, 0, 1), (1, 1, 1), (2, 2, 1), (0, 1, 2), (0, 2, 2), (1, 2, 2)):
        total = sum(p[k] * (columns[k][i] * columns[k][j]) for k in range(3))
        rows.append(STEP_SCALE * factor * total)
    rows.append(raw[6:7])
    for k, row in enumerate(rows):
        table[k] = jnp.broadcast_to(row, (8, LANES))


def pack_kernel(temp, material, plate, cooling, own, send_a, send_b, pack):
    depth, rows, _ = temp.shape
    lane = lane_of((depth, LANES))
    packs = [jnp.zeros((depth, LANES), jnp.float32) for _ in range(3)]
    for x in range(rows):
        fields = (
            temp[:, x, :],
            (material[:, x, :] + 1).astype(jnp.float32),
            cooling[:, x, :] * plate[:, x, :].astype(jnp.float32),
        )
        mine = (lane >= SLOT * x) & (lane < SLOT * (x + 1))
        for f in range(3):
            own[f, x] = fields[f]
            moved = pltpu.roll(fields[f], (SLOT * x + HALO) % LANES, 1)
            packs[f] = jnp.where(mine, moved, packs[f])
    even = lax.rem(lax.axis_index("gx"), 2) == 0
    first_a = jnp.where(even, rows - HALO, 0)
    first_b = jnp.where(even, 0, rows - HALO)
    for f in range(3):
        pack[f] = packs[f]
        for r in range(HALO):
            send_a[f, r] = own[f, first_a + r]
            send_b[f, r] = own[f, first_b + r]


class Rows:
    def __init__(self):
        self.where = {}

    def flat(self, ref, rows, depth, pad, first_block=0, tiles=(0, 1)):
        block = first_block
        for r in rows:
            for t in tiles:
                start = block * (pad + depth) + (pad or GUARD)
                self.where[r, t] = (ref, None, start)
                block += 1
        return block

    def stacked(self, ref, rows, lead=(), first=0, tiles=(0, 1)):
        for r in rows:
            for t in tiles:
                self.where[r, t] = (ref, (*lead, r - first, t), 0)

    def of(self, r, t, depth, oz=0):
        ref, index, start = self.where[r, t]
        if index is None:
            return ref[pl.ds(start + oz, depth)]
        return ref[index]

    def put(self, r, t, value):
        ref, index, start = self.where[r, t]
        if index is None:
            ref[pl.ds(start, value.shape[0])] = value
        else:
            ref[index] = value


def clear_pads(ref, blocks, depth):
    zero = jnp.zeros((PAD, LANES), jnp.float32)
    for block in range(blocks + 1):
        ref[pl.ds(block * (PAD + depth), PAD)] = zero


def lane_shift(pair, by):
    lane = lane_of(pair[0].shape)
    moved = [pltpu.roll(value, (-by) % LANES, 1) for value in pair]
    edge = lane == (LANES - 1 if by > 0 else 0)
    return [jnp.where(edge, moved[1 - t], moved[t]) for t in (0, 1)]


def put_shifted(fields, r, pair):
    for by in (-1, 0, 1):
        moved = pair if by == 0 else lane_shift(pair, by)
        for t in (0, 1):
            fields[by].put(r, t, moved[t])


def near_sum(weights, fields, r, t, depth):
    total = None
    for k, (oz, ox, oy) in enumerate(HALF_OFFSETS):
        both = fields[oy].of(r + ox, t, depth, oz) + fields[-oy].of(r - ox, t, depth, -oz)
        term = weights[k].of(r, t, depth) * both
        total = term if total is None else total + term
    return total


def expand(table, weights, ids, rows, depth):
    tables = [table[k] for k in range(PARTS)]
    for r in rows:
        for t in (0, 1):
            index = ids.of(r, t, depth).astype(jnp.int32)
            halves = []
            for half in range(depth // 8):
                part = index[8 * half : 8 * half + 8]
                zz, xx, yy, zx, zy, xy, aging = (
                    jnp.take_along_axis(entry, part, axis=1, mode="promise_in_bounds")
                    for entry in tables
                )
                found = {(1, 0, 0): zz, (0, 1, 0): xx, (0, 0, 1): yy}
                for first, second, cross, one, two in (
                    (zz, xx, zx, (1, 1, 0), (1, -1, 0)),
                    (zz, yy, zy, (1, 0, 1), (1, 0, -1)),
                    (xx, yy, xy, (0, 1, 1), (0, 1, -1)),
                ):
                    mean = (first + second) * 0.25
                    cross = cross * 0.25
                    found[one], found[two] = mean + cross, mean - cross
                ninth = 1.0 / 9.0
                trace = (zz + xx + yy) * ninth
                zx, zy, xy = zx * ninth, zy * ninth, xy * ninth
                up, down = trace + zx, trace - zx
                plus, minus = zy + xy, zy - xy
                found[1, 1, 1], found[1, 1, -1] = up + plus, up - plus
                found[1, -1, 1], found[1, -1, -1] = down + minus, down - minus
                halves.append([found[offset] for offset in HALF_OFFSETS] + [aging])
            for k in range(LINKS + 1):
                weights[k].put(r, t, jnp.concatenate([half[k] for half in halves], axis=0))


def rate_of(state):
    good = state > 0.5
    inverse = 1.0 / jnp.where(good, state, 1.0)
    return jnp.where(good, jnp.exp(AGE_BETA * (1.0 - inverse)), 0.0), inverse


class Plan:
    def __init__(self, rows):
        self.rows = rows
        self.all = range(rows + 2 * HALO)

    def cone(self, radius):
        return range(HALO - radius, HALO + self.rows + radius)

    def ring(self, radius, inner):
        middle = self.cone(inner)
        return [r for r in self.cone(radius) if r not in middle]


def weight_rows(ref, rows, depth):
    weights, block = [], 0
    for _ in range(LINKS + 1):
        field = Rows()
        block = field.flat(ref, rows, depth, 0, block)
        weights.append(field)
    return weights


def shifted_rows(ref, rows, depth):
    fields, block = {}, 0
    for oy in (-1, 0, 1):
        fields[oy] = Rows()
        block = fields[oy].flat(ref, rows, depth, PAD, block)
    clear_pads(ref, block, depth)
    return fields


def padded_size(blocks, depth):
    return (blocks * (PAD + depth) + PAD, LANES)


def guarded_size(blocks, depth):
    return (blocks * depth + 2 * GUARD, LANES)


def validity(ids, r, depth):
    return [jnp.where(ids.of(r, t, depth) > 0.5, 1.0, 0.0) for t in (0, 1)]


def front_kernel(
    own, got_a, got_b, mid, mid_a, mid_b, table,
    ext, keep_ref, first_ref, second_ref, third_ref, part,
    weights_ref, even_ref, odd_ref,
):
    _, rows, depth, _ = own.shape
    plan = Plan(rows)
    even = lax.rem(lax.axis_index("gx"), 2) == 0
    base_a = jnp.where(even, HALO + rows, 0)
    base_b = jnp.where(even, 0, HALO + rows)
    lane = lane_of((depth, LANES))
    halo_lane = (lane < HALO) | (lane >= LANES - HALO)
    for f in range(3):
        for r in range(HALO):
            ext[f, base_a + r, 0] = got_a[f, r]
            ext[f, base_b + r, 0] = got_b[f, r]
        for x in range(rows):
            ext[f, HALO + x, 0] = own[f, x]
        low = jnp.where(even, mid_b[f], mid_a[f])
        high = jnp.where(even, mid_a[f], mid_b[f])
        for r in plan.all:
            x = r - HALO
            source, x = (
                (low, x + rows) if x < 0 else (high, x - rows) if x >= rows else (mid[f], x)
            )
            moved = pltpu.roll(source, (-(SLOT * x + HALO)) % LANES, 1)
            ext[f, r, 1] = jnp.where(halo_lane, moved, 0.0)

    temp, ids, coeff = Rows(), Rows(), Rows()
    for field, f in ((temp, T0), (ids, ID), (coeff, COEFF)):
        field.stacked(ext, plan.all, (f,))
    weights = weight_rows(weights_ref, plan.cone(2), depth)
    keep = Rows()
    keep.stacked(keep_ref, plan.cone(2), (), HALO - 2)
    shifted = [shifted_rows(ref, plan.cone(3), depth) for ref in (even_ref, odd_ref)]
    expand(table, weights, ids, plan.cone(2), depth)
    for r in plan.cone(3):
        put_shifted(shifted[1], r, validity(ids, r, depth))
        put_shifted(shifted[0], r, [temp.of(r, t, depth) for t in (0, 1)])
    for r in plan.cone(2):
        for t in (0, 1):
            diag = coeff.of(r, t, depth) + near_sum(weights, shifted[1], r, t, depth)
            keep.put(r, t, 1.0 - diag)
    loss = jnp.zeros((depth, LANES), jnp.float32)
    for n in range(STEPS):
        source = shifted[n % 2]
        for r in plan.cone(2 - n):
            pair = []
            for t in (0, 1) if n < 2 else (0,):
                center = source[0].of(r, t, depth)
                near = near_sum(weights, source, r, t, depth)
                pair.append(keep.of(r, t, depth) * center + near + coeff.of(r, t, depth) * COOL_TEMP)
            if n < 2:
                put_shifted(shifted[(n + 1) % 2], r, pair)
                for t in (0, 1):
                    (first_ref, second_ref)[n][r - HALO + 2 - n, t] = pair[t]
            else:
                third_ref[r - HALO] = pair[0]
            if HALO <= r < HALO + rows:
                rate, _ = rate_of(pair[0])
                loss = loss + weights[LINKS].of(r, 0, depth) * rate
    part[...] = jnp.broadcast_to(jnp.sum(loss, axis=0, keepdims=True), part.shape)


def back_kernel(
    ext, keep_in, first_in, second_in, third_in, table, plate,
    adjoint_out, sens_out,
    weights_ref, keep_ref, valid_ref, states_ref, third_ref, adjoint_ref,
):
    rows, depth, _ = third_in.shape
    plan = Plan(rows)
    temp, ids, coeff = Rows(), Rows(), Rows()
    for field, f in ((temp, T0), (ids, ID), (coeff, COEFF)):
        field.stacked(ext, plan.all, (f,))
    outer = plan.ring(5, 2)
    for start in (0, weights_ref.shape[0] - GUARD):
        weights_ref[pl.ds(start, GUARD)] = jnp.zeros((GUARD, LANES), jnp.float32)
    weights = weight_rows(weights_ref, plan.cone(5), depth)
    keep = Rows()
    keep.stacked(keep_in, plan.cone(2), (), HALO - 2)
    for i, r in enumerate(outer):
        for t in (0, 1):
            keep.where[r, t] = (keep_ref, (i, t), 0)
    valid_list = [r for r in plan.all if r not in plan.cone(1)]
    valid = shifted_rows(valid_ref, valid_list, depth)
    shifted, block = [{}, {}, {}], 0
    for n in range(3):
        held = plan.ring(6 - n, 1 - n) if n < 2 else plan.cone(4)
        for oy in (-1, 0, 1):
            shifted[n][oy] = Rows()
            block = shifted[n][oy].flat(states_ref, held, depth, PAD, block)
    clear_pads(states_ref, block, depth)

    expand(table, weights, ids, plan.cone(5), depth)
    for r in valid_list:
        put_shifted(valid, r, validity(ids, r, depth))
    for r in plan.ring(6, 1):
        put_shifted(shifted[0], r, [temp.of(r, t, depth) for t in (0, 1)])
    for r in plan.ring(2, 0):
        put_shifted(shifted[1], r, [first_in[r - HALO + 2, t] for t in (0, 1)])
    for r in plan.cone(1):
        put_shifted(shifted[2], r, [second_in[r - HALO + 1, t] for t in (0, 1)])
    for r in outer:
        for t in (0, 1):
            diag = coeff.of(r, t, depth) + near_sum(weights, valid, r, t, depth)
            keep.put(r, t, 1.0 - diag)
    states = [temp, Rows(), shifted[2][0], Rows()]
    states[1].stacked(first_in, plan.cone(2), (), HALO - 2)
    states[3].stacked(third_ref, plan.cone(3), (), HALO - 3)
    for r in plan.cone(0):
        states[3].where[r, 0] = (third_in, (r - HALO,), 0)
    for n in range(STEPS):
        todo = [(r, t) for r in plan.ring(5 - n, 2 - n) for t in (0, 1)]
        if n == 2:
            todo = todo + [(r, 1) for r in plan.cone(0)]
        pair = {}
        for r, t in todo:
            center = shifted[n][0].of(r, t, depth)
            near = near_sum(weights, shifted[n], r, t, depth)
            value = keep.of(r, t, depth) * center + near + coeff.of(r, t, depth) * COOL_TEMP
            if n == 2:
                states[3].put(r, t, value)
                continue
            pair[t] = value
            if t == 1:
                put_shifted(shifted[n + 1], r, [pair[0], pair[1]])

    def drive(n, r, t):
        rate, inverse = rate_of(states[n].of(r, t, depth))
        return weights[LINKS].of(r, t, depth) * AGE_BETA * rate * (inverse * inverse)

    vectors, block = [], 0
    for n in range(3):
        vectors.append(Rows())
        block = vectors[n].flat(adjoint_ref, plan.cone(3 - n), depth, PAD, block)
    clear_pads(adjoint_ref, block, depth)
    for r in plan.cone(3):
        for t in (0, 1):
            vectors[0].put(r, t, drive(3, r, t))
    for n in range(3):
        vector = vectors[n]
        sums = {}
        for source in plan.cone(3 - n):
            for t in (0, 1):
                reads = {oz: vector.of(source, t, depth, -oz) for oz in (-1, 0, 1)}
                for k, offset in enumerate(HALF_OFFSETS):
                    product = {}
                    for sign in (1, -1):
                        oz, ox, oy = (sign * o for o in offset)
                        target = source + ox
                        if oz not in product:
                            product[oz] = reads[oz] * weights[k].of(source, t, depth, -oz)
                        if target in plan.cone(2 - n):
                            key = (target, oy, t)
                            sums[key] = sums[key] + product[oz] if key in sums else product[oz]
            target = source - 1
            if target not in plan.cone(2 - n):
                continue
            plus = lane_shift([sums.pop((target, 1, t)) for t in (0, 1)], -1)
            minus = lane_shift([sums.pop((target, -1, t)) for t in (0, 1)], 1)
            for t in (0, 1) if n < 2 else (0,):
                result = (
                    keep.of(target, t, depth) * vector.of(target, t, depth)
                    + sums.pop((target, 0, t))
                    + (plus[t] + minus[t])
                )
                if n < 2:
                    vectors[n + 1].put(target, t, result + drive(2 - n, target, t))
                else:
                    adjoint_out[:, target - HALO, :] = result
    for r in plan.cone(0):
        total = None
        for n in range(3):
            term = vectors[2 - n].of(r, 0, depth) * (states[n].of(r, 0, depth) - COOL_TEMP)
            total = term if total is None else total + term
        sens_out[:, r - HALO, :] = -total * plate[:, r - HALO, :].astype(jnp.float32)


def scale_kernel(cells, parts, adjoint, sens, adjoint_out, sens_out):
    row = jnp.sum(parts[...], axis=0, keepdims=True)
    scale = cells / jnp.sum(row, axis=1, keepdims=True)
    adjoint_out[...] = adjoint[...] * scale.reshape(1, 1, 1)
    sens_out[...] = sens[...] * scale.reshape(1, 1, 1)


def pairing(count, first):
    out = {}
    for i in range(first, count - 1, 2):
        out[i], out[i + 1] = i + 1, i
    return out


def swap(value, sizes, axis, first):
    count_x, count_y = sizes
    partner = pairing(sizes[axis], first)
    pairs = []
    for i in range(count_x):
        for j in range(count_y):
            other = partner.get((i, j)[axis])
            if other is not None:
                target = (other, j) if axis == 0 else (i, other)
                pairs.append((i * count_y + j, target[0] * count_y + target[1]))
    return lax.ppermute(value, ("gx", "gy"), pairs)


def local(initial_temp, material, plate, cooling, principal, angles, aging_scale):
    depth, rows, width = initial_temp.shape
    sizes = (lax.axis_size("gx"), lax.axis_size("gy"))
    devices = sizes[0] * sizes[1]
    f32 = jnp.float32

    def shape(*dims):
        return jax.ShapeDtypeStruct(dims, f32)

    def call(kernel, name, mib, out_shape, scratch=()):
        return pl.pallas_call(
            kernel,
            out_shape=out_shape,
            scratch_shapes=[pltpu.VMEM(dims, f32) for dims in scratch],
            name=name,
            compiler_params=pltpu.CompilerParams(vmem_limit_bytes=mib * 2**20),
        )

    own, send_a, send_b, pack = call(
        pack_kernel,
        "pack",
        2,
        (
            shape(3, rows, depth, LANES),
            shape(3, HALO, depth, LANES),
            shape(3, HALO, depth, LANES),
            shape(3, depth, LANES),
        ),
    )(initial_temp, material, plate, cooling)
    side_b = swap(pack, sizes, 1, 1)
    side_a = swap(pack, sizes, 1, 0)
    got_b = swap(send_b, sizes, 0, 1)
    got_a = swap(send_a, sizes, 0, 0)
    table = call(table_kernel, "table", 2, shape(PARTS, 8, LANES), ((8, LANES),))(
        principal.T, angles.T, aging_scale[None]
    )
    even = lax.rem(lax.axis_index("gy"), 2) == 0
    from_left = lax.rem(lane_of(pack.shape), SLOT) < HALO
    mid = jnp.where(from_left == even, side_b, side_a)
    mid_b = swap(mid, sizes, 0, 1)
    mid_a = swap(mid, sizes, 0, 0)

    total_rows = rows + 2 * HALO
    pairs = 2 * rows
    ext, keep, first, second, third, part = call(
        front_kernel,
        "front",
        20,
        (
            shape(3, total_rows, 2, depth, LANES),
            shape(rows + 4, 2, depth, LANES),
            shape(rows + 4, 2, depth, LANES),
            shape(rows + 2, 2, depth, LANES),
            shape(rows, depth, LANES),
            shape(devices, LANES),
        ),
        (
            guarded_size((LINKS + 1) * (pairs + 8), depth),
            padded_size(3 * (pairs + 12), depth),
            padded_size(3 * (pairs + 12), depth),
        ),
    )(own, got_a, got_b, mid, mid_a, mid_b, table)
    parts = lax.all_to_all(part, ("gx", "gy"), 0, 0, tiled=True)
    adjoint, sens = call(
        back_kernel,
        "back",
        24,
        (shape(depth, rows, LANES), shape(depth, rows, LANES)),
        (
            guarded_size((LINKS + 1) * (pairs + 20), depth),
            (6, 2, depth, LANES),
            padded_size(3 * 2 * 10, depth),
            padded_size(3 * (2 * 10 + 2 * 10 + pairs + 16), depth),
            (rows + 6, 2, depth, LANES),
            padded_size(3 * pairs + 4 * (3 + 2 + 1), depth),
        ),
    )(ext, keep, first, second, third, table, plate)
    return call(
        functools.partial(scale_kernel, float(depth * rows * width * devices)),
        "scale",
        2,
        (shape(depth, rows, LANES), shape(depth, rows, LANES)),
    )(parts, adjoint, sens)


def solution(mesh):
    block = P(None, "gx", "gy")
    return jax.shard_map(
        local,
        mesh=mesh,
        in_specs=(block, block, block, block, P(), P(), P()),
        out_specs=(block, block),
        check_vma=False,
    )
```

time: 42.6 us -> 34.9 us (0.82)
  Pallas kernels: 16.7 us -> 6.88 us
  waiting for transfers between devices: 1.44 us -> 4.4 us
  other arithmetic: 2.91 us -> 0.01 us
  local copies, waits for them, and re-layouts: 1.36 us -> 4.06 us
  between operations: 1.43 us -> 0.76 us
    pallas_call x3 -> x5, Pallas kernels: 16.7 us -> 6.88 us  [the longest x1 3.09 us: local(): call(back_kernel, 'back', 24, (shape(depth, rows, LANES), shape(depth, ro...]
    all_to_all x1, waiting for transfers between devices: 0.01 us -> 4.02 us  [local(): parts = lax.all_to_all(part, ('gx', 'gy'), 0, 0, tiled=True)]
    unnamed x12 -> x16, local copies, waits for them, and re-layouts: 0.69 us -> 4.06 us
    mul x1 -> x0, other arithmetic: 1.54 us -> none  [local(): return (adjoint * scale, sens * plate.astype(f32) * scale)]
    ppermute x6, waiting for transfers between devices: 1.43 us -> 0.38 us  [swap(): return lax.ppermute(value, ('gx', 'gy'), pairs)]
    transpose x1 -> x0, other arithmetic: 0.72 us -> none  [local(): raw = jnp.concatenate([principal, angles, aging_scale[:, None]], axis=1).T]
    pad x1 -> x0, local copies, waits for them, and re-layouts: 0.67 us -> none  [local(): raw = jnp.pad(raw, ((0, 1), (1, LANES - 1 - raw.shape[1])))]
    reduce_sum x1 -> x0, other arithmetic: 0.63 us -> none  [local(): scale = float(depth * rows * width * devices) / jnp.sum(parts)]
  transfers between devices with their start and end apart: 7 -> 7, of which waited for: 2 -> 2; matrix products, arithmetic and copies ran while one was open for 0% -> 0% of each run, Pallas kernels for 19% -> 9%
where the time goes in v2:
time: 34.9 us; the launch traced here: 34.5 us
  starting transfers between devices  18.4 us (53%)
  Pallas kernels  6.88 us (20%)
  waiting for transfers between devices  4.4 us (13%)
  local copies, waits for them, and re-layouts  4.06 us (12%)
  between operations  0.76 us (2%)
    ppermute x6, starting transfers between devices, swap(): return lax.ppermute(value, ('gx', 'gy'), pairs)  9.51 us
    all_to_all x1, starting transfers between devices, local(): parts = lax.all_to_all(part, ('gx', 'gy'), 0, 0, tiled=True)  8.88 us
    unnamed x16, local copies, waits for them, and re-layouts  4.06 us
    all_to_all x1, waiting for transfers between devices, local(): parts = lax.all_to_all(part, ('gx', 'gy'), 0, 0, tiled=True)  4.02 us
    pallas_call x1, Pallas kernels, local(): call(back_kernel, 'back', 24, (shape(depth, rows, LANES), shape(depth, ro...  3.09 us
    pallas_call x1, Pallas kernels, local(): call(front_kernel, 'front', 20, (shape(3, total_rows, 2, depth, LANES), s...  2.63 us
    pallas_call x1, Pallas kernels, local(): call(functools.partial(scale_kernel, float(depth * rows * width * devices...  0.75 us
  transfers between devices with their start and end apart: 7, of which 2 were waited for; matrix products, arithmetic and copies ran while one was open for 0% of the time, Pallas kernels for 9%

profile of v2, /device:TPU:0, one launch (start us, length us, event | category | flops | bytes accessed | tf_op | source)
XLA Modules:
  0.0 34.5 jit_solution(3664059494629530394)
XLA Ops:
  0.6 0.0 copy-start
  0.6 0.8 %copy-done = s32[16,8,128]{2,1,0:T(8,128)S(1)} copy-done((s32[16,8,128]{2,1,0:T(8,128)S(1)}, s32[16,8,128]{2,1,0:T(8,128)}, u32[]{:S(2)}) %copy-start) | copy-done | bytes 65560
  1.5 0.8 %copy-done.2 = f32[16,8,128]{2,1,0:T(8,128)S(1)} copy-done((f32[16,8,128]{2,1,0:T(8,128)S(1)}, f32[16,8,128]{2,1,0:T(8,128)}, u32[]{:S(2)}) %copy-start.2) | copy-done | bytes 65560
  2.3 0.8 %copy-done.3 = s32[16,8,128]{2,1,0:T(8,128)S(1)} copy-done((s32[16,8,128]{2,1,0:T(8,128)S(1)}, s32[16,8,128]{2,1,0:T(8,128)}, u32[]{:S(2)}) %copy-start.3) | copy-done | bytes 65560
  3.2 0.8 %copy-done.4 = f32[16,8,128]{2,1,0:T(8,128)S(1)} copy-done((f32[16,8,128]{2,1,0:T(8,128)S(1)}, f32[16,8,128]{2,1,0:T(8,128)}, u32[]{:S(2)}) %copy-start.4) | copy-done | bytes 65560
  4.0 0.3 pack.1
  4.3 3.0 %collective-permute-start.3 = (f32[3,16,128]{2,1,0:T(8,128)S(1)}, f32[3,16,128]{2,1,0:T(8,128)S(1)}, u32[]{:S(2)}, u32[]{:S(2)}) collective-permute-start(f32[3,16,128]{2,1,0:T(8,128)S(1)} %get-tuple-element.17), channel_id=1, source_target_pairs={{0,1},{1,0},{2,3},{3,2},{4,5},{5,4},{6,7},{7,6},{8,9},{9,8},{10,11... | collective-permute-start | bytes 73736 | tf_op jit(solution)/shard_map/ppermute | solution.py:431
  7.3 0.7 %collective-permute-start.2 = (f32[3,16,128]{2,1,0:T(8,128)S(1)}, f32[3,16,128]{2,1,0:T(8,128)S(1)}, u32[]{:S(2)}, u32[]{:S(2)}) collective-permute-start(f32[3,16,128]{2,1,0:T(8,128)S(1)} %get-tuple-element.17), channel_id=1, source_target_pairs={{1,2},{2,1},{5,6},{6,5},{9,10},{10,9},{13,14},{14,13},{17,18},{18,... | collective-permute-start | bytes 73736 | tf_op jit(solution)/shard_map/ppermute | solution.py:431
  8.0 0.1 collective-permute-start
  8.0 0.7 %collective-permute-start.1 = (f32[3,6,16,128]{3,2,1,0:T(8,128)S(1)}, f32[3,6,16,128]{3,2,1,0:T(8,128)S(1)}, u32[]{:S(2)}, u32[]{:S(2)}) collective-permute-start(f32[3,6,16,128]{3,2,1,0:T(8,128)S(1)} %get-tuple-element.16), channel_id=1, source_target_pairs={{4,8},{5,9},{6,10},{7,11},{8,4},{9,5},{10,6},{11,7},{12,16},{13,17... | collective-permute-start | bytes 442376 | tf_op jit(solution)/shard_map/ppermute | solution.py:431
  8.7 0.4 %collective-permute-done.3 = f32[3,16,128]{2,1,0:T(8,128)S(1)} collective-permute-done((f32[3,16,128]{2,1,0:T(8,128)S(1)}, f32[3,16,128]{2,1,0:T(8,128)S(1)}, u32[]{:S(2)}, u32[]{:S(2)}) %collective-permute-start.3) | collective-permute-done | bytes 24608 | tf_op jit(solution)/shard_map/ppermute | solution.py:431
  9.1 0.0 collective-permute-done.2
  9.1 0.7 %collective-permute-start.5 = (f32[3,16,128]{2,1,0:T(8,128)S(1)}, f32[3,16,128]{2,1,0:T(8,128)S(1)}, u32[]{:S(2)}, u32[]{:S(2)}) collective-permute-start(f32[3,16,128]{2,1,0:T(8,128)S(1)} %broadcast_select_fusion.mid), channel_id=1, source_target_pairs={{4,8},{5,9},{6,10},{7,11},{8,4},{9,5},{10,6},{11,7},{12,16},{13,17... | collective-permute-start | bytes 73736 | tf_op jit(solution)/shard_map/ppermute | solution.py:431
  9.8 4.4 %collective-permute-start.4 = (f32[3,16,128]{2,1,0:T(8,128)S(1)}, f32[3,16,128]{2,1,0:T(8,128)S(1)}, u32[]{:S(2)}, u32[]{:S(2)}) collective-permute-start(f32[3,16,128]{2,1,0:T(8,128)S(1)} %broadcast_select_fusion.mid), channel_id=1, source_target_pairs={{0,4},{1,5},{2,6},{3,7},{4,0},{5,1},{6,2},{7,3},{8,12},{9,13},{10,... | collective-permute-start | bytes 73736 | tf_op jit(solution)/shard_map/ppermute | solution.py:431
  14.2 0.7 %copy-done.6 = f32[16,3]{0,1:T(4,128)S(1)} copy-done((f32[16,3]{0,1:T(4,128)S(1)}, f32[16,3]{0,1:T(4,128)}, u32[]{:S(2)}) %copy-start.6) | copy-done | bytes 216
  14.9 0.0 copy-done.5
  14.9 0.1 table.1
  15.1 0.0 collective-permute-done.4.mid_a
  15.1 0.0 copy-start.1
  15.1 2.6 %front.1 = (f32[3,20,2,16,128]{4,3,2,1,0:T(8,128)S(1)}, f32[12,2,16,128]{3,2,1,0:T(8,128)S(1)}, f32[12,2,16,128]{3,2,1,0:T(8,128)S(1)}, f32[10,2,16,128]{3,2,1,0...) custom-call(f32[3,8,16,128]{3,2,1,0:T(8,128)S(1)} %get-tuple-element.14.own, ...), custom_call_target="tpu_custom_call" | custom-call | tf_op jit(solution)/shard_map/front/pallas_call | solution.py:478
  17.7 8.9 %all-to-all-start = ((f32[32,1,128]{2,1,0:T(1,128)}), f32[32,1,128]{2,1,0:T(1,128)S(1)}, u32[]{:S(2)}, u32[]{:S(2)}) async-start(f32[32,1,128]{2,1,0:T(1,128)} %bitcast.4), calls=%async_computation | async-start | bytes 32768 | tf_op jit(solution)/shard_map/all_to_all | solution.py:496
  26.6 3.1 %back.1 = (f32[16,8,128]{2,1,0:T(8,128)S(1)}, f32[16,8,128]{2,1,0:T(8,128)S(1)}) custom-call(f32[3,20,2,16,128]{4,3,2,1,0:T(8,128)S(1)} %get-tuple-element.19.ext, f32[12,2,16,128]{3,2,1,0:T(8,128)S(1)} %get-tuple-element.20.keep_in, f32[12,2,16,128]{3,2,1,0:T(8,128)S(1)} %get-tuple-element.21.first_in, f32[10,2,16,128]{3,2,1,0:T(8,128)S(1)} %get-tuple-element.22.second_in, ...), custom_call_target="tpu_custom_call" | custom-call | tf_op jit(solution)/shard_map/back/pallas_call | solution.py:497
  29.7 4.0 %all-to-all-done = f32[32,1,128]{2,1,0:T(1,128)S(1)} async-done(((f32[32,1,128]{2,1,0:T(1,128)}), f32[32,1,128]{2,1,0:T(1,128)S(1)}, u32[]{:S(2)}, u32[]{:S(2)}) %all-to-all-start) | async-done | bytes 16416 | tf_op jit(solution)/shard_map/all_to_all | solution.py:496
  33.8 0.7 %scale.1 = (f32[16,8,128]{2,1,0:T(8,128)}, f32[16,8,128]{2,1,0:T(8,128)}) custom-call(f32[32,128]{1,0:T(8,128)S(1)} %bitcast.7, f32[16,8,128]{2,1,0:T(8,128)S(1)} %get-tuple-element.24.adjoint, f32[16,8,128]{2,1,0:T(8,128)S(1)} %get-tuple-element.25.sens), custom_call_target="tpu_custom_call" | custom-call | tf_op jit(solution)/shard_map/scale/pallas_call | solution.py:511
  (13 shorter events, 0.0 us)
Async XLA Ops:
  0.6 0.8 %copy-start = (s32[16,8,128]{2,1,0:T(8,128)S(1)}, s32[16,8,128]{2,1,0:T(8,128)}, u32[]{:S(2)}) copy-start(s32[16,8,128]{2,1,0:T(8,128)} %plate.3) | copy-start | bytes 196612
  1.5 0.8 %copy-start.2 = (f32[16,8,128]{2,1,0:T(8,128)S(1)}, f32[16,8,128]{2,1,0:T(8,128)}, u32[]{:S(2)}) copy-start(f32[16,8,128]{2,1,0:T(8,128)} %temp.1) | copy-start | bytes 196612
  2.3 0.8 %copy-start.3 = (s32[16,8,128]{2,1,0:T(8,128)S(1)}, s32[16,8,128]{2,1,0:T(8,128)}, u32[]{:S(2)}) copy-start(s32[16,8,128]{2,1,0:T(8,128)} %material.1) | copy-start | bytes 196612
  3.2 0.8 %copy-start.4 = (f32[16,8,128]{2,1,0:T(8,128)S(1)}, f32[16,8,128]{2,1,0:T(8,128)}, u32[]{:S(2)}) copy-start(f32[16,8,128]{2,1,0:T(8,128)} %cooling.1) | copy-start | bytes 196612
  4.3 4.8 %collective-permute-start.3 = (f32[3,16,128]{2,1,0:T(8,128)S(1)}, f32[3,16,128]{2,1,0:T(8,128)S(1)}, u32[]{:S(2)}, u32[]{:S(2)}) collective-permute-start(f32[3,16,128]{2,1,0:T(8,128)S(1)} %get-tuple-element.17), channel_id=1, source_target_pairs={{0,1},{1,0},{2,3},{3,2},{4,5},{5,4},{6,7},{7,6},{8,9},{9,8},{10,11... | collective-permute-start | bytes 73736 | tf_op jit(solution)/shard_map/ppermute | solution.py:431
  7.3 1.8 %collective-permute-start.2 = (f32[3,16,128]{2,1,0:T(8,128)S(1)}, f32[3,16,128]{2,1,0:T(8,128)S(1)}, u32[]{:S(2)}, u32[]{:S(2)}) collective-permute-start(f32[3,16,128]{2,1,0:T(8,128)S(1)} %get-tuple-element.17), channel_id=1, source_target_pairs={{1,2},{2,1},{5,6},{6,5},{9,10},{10,9},{13,14},{14,13},{17,18},{18,... | collective-permute-start | bytes 73736 | tf_op jit(solution)/shard_map/ppermute | solution.py:431
  8.0 7.1 %collective-permute-start = (f32[3,6,16,128]{3,2,1,0:T(8,128)S(1)}, f32[3,6,16,128]{3,2,1,0:T(8,128)S(1)}, u32[]{:S(2)}, u32[]{:S(2)}) collective-permute-start(f32[3,6,16,128]{3,2,1,0:T(8,128)S(1)} %get-tuple-element.15), channel_id=1, source_target_pairs={{0,4},{1,5},{2,6},{3,7},{4,0},{5,1},{6,2},{7,3},{8,12},{9,13},{10,... | collective-permute-start | bytes 442376 | tf_op jit(solution)/shard_map/ppermute | solution.py:431
  8.0 7.1 %collective-permute-start.1 = (f32[3,6,16,128]{3,2,1,0:T(8,128)S(1)}, f32[3,6,16,128]{3,2,1,0:T(8,128)S(1)}, u32[]{:S(2)}, u32[]{:S(2)}) collective-permute-start(f32[3,6,16,128]{3,2,1,0:T(8,128)S(1)} %get-tuple-element.16), channel_id=1, source_target_pairs={{4,8},{5,9},{6,10},{7,11},{8,4},{9,5},{10,6},{11,7},{12,16},{13,17... | collective-permute-start | bytes 442376 | tf_op jit(solution)/shard_map/ppermute | solution.py:431
  9.1 5.9 %collective-permute-start.5 = (f32[3,16,128]{2,1,0:T(8,128)S(1)}, f32[3,16,128]{2,1,0:T(8,128)S(1)}, u32[]{:S(2)}, u32[]{:S(2)}) collective-permute-start(f32[3,16,128]{2,1,0:T(8,128)S(1)} %broadcast_select_fusion.mid), channel_id=1, source_target_pairs={{4,8},{5,9},{6,10},{7,11},{8,4},{9,5},{10,6},{11,7},{12,16},{13,17... | collective-permute-start | bytes 73736 | tf_op jit(solution)/shard_map/ppermute | solution.py:431
  9.8 5.3 %collective-permute-start.4 = (f32[3,16,128]{2,1,0:T(8,128)S(1)}, f32[3,16,128]{2,1,0:T(8,128)S(1)}, u32[]{:S(2)}, u32[]{:S(2)}) collective-permute-start(f32[3,16,128]{2,1,0:T(8,128)S(1)} %broadcast_select_fusion.mid), channel_id=1, source_target_pairs={{0,4},{1,5},{2,6},{3,7},{4,0},{5,1},{6,2},{7,3},{8,12},{9,13},{10,... | collective-permute-start | bytes 73736 | tf_op jit(solution)/shard_map/ppermute | solution.py:431
  14.2 0.7 %copy-start.6 = (f32[16,3]{0,1:T(4,128)S(1)}, f32[16,3]{0,1:T(4,128)}, u32[]{:S(2)}) copy-start(f32[16,3]{0,1:T(4,128)} %param.12) | copy-start | bytes 580
  14.2 0.7 %copy-start.5 = (f32[16,3]{0,1:T(4,128)S(1)}, f32[16,3]{0,1:T(4,128)}, u32[]{:S(2)}) copy-start(f32[16,3]{0,1:T(4,128)} %param.11) | copy-start | bytes 580
  14.2 0.7 %copy-start.7 = (f32[16]{0:T(128)S(1)}, f32[16]{0:T(128)}, u32[]{:S(2)}) copy-start(f32[16]{0:T(128)} %param.13) | copy-start | bytes 196
  15.1 11.5 %copy-start.1 = (s32[16,8,128]{2,1,0:T(8,128)S(1)}, s32[16,8,128]{2,1,0:T(8,128)}, u32[]{:S(2)}) copy-start(s32[16,8,128]{2,1,0:T(8,128)} %plate.3) | copy-start | bytes 196612
  17.7 16.0 %all-to-all-start = ((f32[32,1,128]{2,1,0:T(1,128)}), f32[32,1,128]{2,1,0:T(1,128)S(1)}, u32[]{:S(2)}, u32[]{:S(2)}) async-start(f32[32,1,128]{2,1,0:T(1,128)} %bitcast.4), calls=%async_computation | async-start | bytes 32768 | tf_op jit(solution)/shard_map/all_to_all | solution.py:496

commit v3 on v2

v3 whole, which is shorter than its diff:
```python
import functools

import jax
import jax.numpy as jnp
from jax import lax
from jax.experimental import pallas as pl
from jax.experimental.pallas import tpu as pltpu
from jax.sharding import PartitionSpec as P

STEPS = 3
STEP_SCALE = 0.06
COOL_TEMP = 0.85
AGE_BETA = 8.0
HALF_OFFSETS = [
    (first, second, third)
    for first in (-1, 0, 1)
    for second in (-1, 0, 1)
    for third in (-1, 0, 1)
    if (first, second, third) > (0, 0, 0)
]
LINKS = len(HALF_OFFSETS)
HALO = 2 * STEPS
LANES = 128
SLOT = 16
T0, ID, COEFF = 0, 1, 2
VMEM = pl.BlockSpec(memory_space=pltpu.VMEM)
PAD = 8
GUARD = 8
PARTS = 7


def lane_of(shape):
    return lax.broadcasted_iota(jnp.int32, shape, len(shape) - 1)


def table_kernel(principal, angles, aging, table, line):
    count = aging.shape[1]
    line[...] = jnp.zeros_like(line)
    line[0:3, 0:count] = principal[...]
    line[3:6, 0:count] = angles[...]
    line[6:7, 0:count] = aging[...]
    raw = pltpu.roll(line[...], 1, 1)
    p = [raw[k : k + 1] for k in range(3)]
    cosine, sine = jnp.cos(raw[3:6]), jnp.sin(raw[3:6])
    c1, c2, c3 = cosine[0:1], cosine[1:2], cosine[2:3]
    s1, s2, s3 = sine[0:1], sine[1:2], sine[2:3]
    columns = [
        (c1 * c3 - s1 * c2 * s3, s1 * c3 + c1 * c2 * s3, s2 * s3),
        (-c1 * s3 - s1 * c2 * c3, -s1 * s3 + c1 * c2 * c3, s2 * c3),
        (s1 * s2, -c1 * s2, c2),
    ]
    rows = []
    for i, j, factor in ((0, 0, 1), (1, 1, 1), (2, 2, 1), (0, 1, 2), (0, 2, 2), (1, 2, 2)):
        total = sum(p[k] * (columns[k][i] * columns[k][j]) for k in range(3))
        rows.append(STEP_SCALE * factor * total)
    rows.append(raw[6:7])
    for k, row in enumerate(rows):
        table[k] = jnp.broadcast_to(row, (8, LANES))


def pack_kernel(temp_in, material_in, plate_in, cooling_in, own, pack, temp, material, plate, cooling, sems):
    copies = [
        pltpu.make_async_copy(source, target, sems.at[i])
        for i, (source, target) in enumerate(
            ((temp_in, temp), (material_in, material), (plate_in, plate), (cooling_in, cooling))
        )
    ]
    for copy in copies:
        copy.start()
    for copy in copies:
        copy.wait()
    depth, rows, _ = temp.shape
    lane = lane_of((depth, LANES))
    packs = [jnp.zeros((depth, LANES), jnp.float32) for _ in range(3)]
    for x in range(rows):
        fields = (
            temp[:, x, :],
            (material[:, x, :] + 1).astype(jnp.float32),
            cooling[:, x, :] * plate[:, x, :].astype(jnp.float32),
        )
        mine = (lane >= SLOT * x) & (lane < SLOT * (x + 1))
        for f in range(3):
            own[f, x] = fields[f]
            moved = pltpu.roll(fields[f], (SLOT * x + HALO) % LANES, 1)
            packs[f] = jnp.where(mine, moved, packs[f])
    for f in range(3):
        pack[f] = packs[f]


def middle_kernel(last_y, own, side_a, side_b, mid, send_a, send_b):
    _, rows, depth, _ = own.shape
    at_y = lax.axis_index("gy")
    even_y = lax.rem(at_y, 2) == 0
    even_x = lax.rem(lax.axis_index("gx"), 2) == 0
    from_left = lax.rem(lane_of((depth, LANES)), SLOT) < HALO
    for f in range(3):
        left = jnp.where(at_y == 0, 0.0, jnp.where(even_y, side_b[f], side_a[f]))
        right = jnp.where(at_y == last_y, 0.0, jnp.where(even_y, side_a[f], side_b[f]))
        value = jnp.where(from_left, left, right)
        mid[f] = value
        send_a[f, HALO] = value
        send_b[f, HALO] = value
    first_a = jnp.where(even_x, rows - HALO, 0)
    first_b = jnp.where(even_x, 0, rows - HALO)
    for f in range(3):
        for r in range(HALO):
            send_a[f, r] = own[f, first_a + r]
            send_b[f, r] = own[f, first_b + r]


class Rows:
    def __init__(self):
        self.where = {}

    def flat(self, ref, rows, depth, pad, first_block=0, tiles=(0, 1)):
        block = first_block
        for r in rows:
            for t in tiles:
                start = block * (pad + depth) + (pad or GUARD)
                self.where[r, t] = (ref, None, start)
                block += 1
        return block

    def stacked(self, ref, rows, lead=(), first=0, tiles=(0, 1)):
        for r in rows:
            for t in tiles:
                self.where[r, t] = (ref, (*lead, r - first, t), 0)

    def of(self, r, t, size, offset=0):
        ref, index, start = self.where[r, t]
        if index is None:
            return ref[pl.ds(start + offset, size)]
        return ref[(*index, pl.ds(offset, size))]

    def put(self, r, t, value, offset=0):
        ref, index, start = self.where[r, t]
        if index is None:
            ref[pl.ds(start + offset, value.shape[0])] = value
        else:
            ref[(*index, pl.ds(offset, value.shape[0]))] = value


def clear_pads(ref, blocks, depth):
    zero = jnp.zeros((PAD, LANES), jnp.float32)
    for block in range(blocks + 1):
        ref[pl.ds(block * (PAD + depth), PAD)] = zero


def lane_shift(pair, by):
    lane = lane_of(pair[0].shape)
    moved = [pltpu.roll(value, (-by) % LANES, 1) for value in pair]
    edge = lane == (LANES - 1 if by > 0 else 0)
    return [jnp.where(edge, moved[1 - t], moved[t]) for t in (0, 1)]


def put_shifted(fields, r, pair):
    for by in (-1, 0, 1):
        moved = pair if by == 0 else lane_shift(pair, by)
        for t in (0, 1):
            fields[by].put(r, t, moved[t])


def advance(weights, keep, coeff, fields, rows, tiles, depth, done):
    for t in tiles:
        for half in range(depth // 8):
            base = 8 * half
            window = {}
            for r in rows:
                for other in (r - 1, r, r + 1):
                    if other not in window:
                        window[other] = {
                            (oz, oy): fields[oy].of(other, t, 8, base + oz)
                            for oz in (-1, 0, 1)
                            for oy in (-1, 0, 1)
                        }
                total = coeff.of(r, t, 8, base) * COOL_TEMP
                total = total + keep.of(r, t, 8, base) * window[r][0, 0]
                for k, (oz, ox, oy) in enumerate(HALF_OFFSETS):
                    both = window[r + ox][oz, oy] + window[r - ox][-oz, -oy]
                    total = total + weights[k].of(r, t, 8, base) * both
                done(r, t, base, total)
                window.pop(r - 1)


def reach(at, size):
    above = jnp.where(at < size - 1, 1.0, 0.0)
    below = jnp.where(at > 0, 1.0, 0.0)
    return above + below, above - below


def expand(table, weights, keep, ids, coeff, rows, grid, own_rows, depth):
    tables = [table[k] for k in range(PARTS)]
    quarter, ninth = 0.25, 1.0 / 9.0
    lane = lane_of((8, LANES))
    first_y = lax.axis_index("gy") * LANES
    first_x = lax.axis_index("gx") * own_rows - HALO
    for t in (0, 1):
        y = first_y + (lane if t == 0 else jnp.where(lane < LANES // 2, lane + LANES, lane - LANES))
        sum_y, dif_y = reach(y, grid[1])
        for half in range(depth // 8):
            z = lax.broadcasted_iota(jnp.int32, (8, LANES), 0) + 8 * half
            sum_z, dif_z = reach(z, depth)
            zz_0, zz_1 = sum_z * (1.0 + quarter * sum_y), sum_z * (quarter + ninth * sum_y)
            yy_0, yy_1 = sum_y * (1.0 + quarter * sum_z), sum_y * (quarter + ninth * sum_z)
            xx_1 = 1.0 + quarter * (sum_z + sum_y) + ninth * sum_z * sum_y
            zx_1 = dif_z * (quarter + ninth * sum_y)
            xy_1 = dif_y * (quarter + ninth * sum_z)
            zy_0, zy_1 = quarter * dif_z * dif_y, ninth * dif_z * dif_y
            for r in rows:
                sum_x, dif_x = reach(first_x + r, grid[0])
                part = ids.of(r, t, 8, 8 * half).astype(jnp.int32)
                zz, xx, yy, zx, zy, xy, aging = (
                    jnp.take_along_axis(entry, part, axis=1, mode="promise_in_bounds")
                    for entry in tables
                )
                near = (
                    zz * (zz_0 + sum_x * zz_1)
                    + yy * (yy_0 + sum_x * yy_1)
                    + zy * (zy_0 + sum_x * zy_1)
                    + xx * (sum_x * xx_1)
                    + dif_x * (zx * zx_1 + xy * xy_1)
                )
                keep.put(r, t, 1.0 - (coeff.of(r, t, 8, 8 * half) + near), 8 * half)
                found = {(1, 0, 0): zz, (0, 1, 0): xx, (0, 0, 1): yy}
                for first, second, cross, one, two in (
                    (zz, xx, zx, (1, 1, 0), (1, -1, 0)),
                    (zz, yy, zy, (1, 0, 1), (1, 0, -1)),
                    (xx, yy, xy, (0, 1, 1), (0, 1, -1)),
                ):
                    mean = (first + second) * quarter
                    cross = cross * quarter
                    found[one], found[two] = mean + cross, mean - cross
                trace = (zz + xx + yy) * ninth
                zx, zy, xy = zx * ninth, zy * ninth, xy * ninth
                up, down = trace + zx, trace - zx
                plus, minus = zy + xy, zy - xy
                found[1, 1, 1], found[1, 1, -1] = up + plus, up - plus
                found[1, -1, 1], found[1, -1, -1] = down + minus, down - minus
                for k, offset in enumerate(HALF_OFFSETS):
                    weights[k].put(r, t, found[offset], 8 * half)
                weights[LINKS].put(r, t, aging, 8 * half)


def rate_of(state):
    good = state > 0.5
    inverse = 1.0 / jnp.where(good, state, 1.0)
    return jnp.where(good, jnp.exp(AGE_BETA * (1.0 - inverse)), 0.0), inverse


class Plan:
    def __init__(self, rows):
        self.rows = rows
        self.all = range(rows + 2 * HALO)

    def cone(self, radius):
        return range(HALO - radius, HALO + self.rows + radius)

    def ring(self, radius, inner):
        middle = self.cone(inner)
        return [r for r in self.cone(radius) if r not in middle]


def weight_rows(ref, rows, depth):
    weights, block = [], 0
    for _ in range(LINKS + 1):
        field = Rows()
        block = field.flat(ref, rows, depth, 0, block)
        weights.append(field)
    return weights


def shifted_rows(ref, rows, depth):
    fields, block = {}, 0
    for oy in (-1, 0, 1):
        fields[oy] = Rows()
        block = fields[oy].flat(ref, rows, depth, PAD, block)
    clear_pads(ref, block, depth)
    return fields


def padded_size(blocks, depth):
    return (blocks * (PAD + depth) + PAD, LANES)


def guarded_size(blocks, depth):
    return (blocks * depth + 2 * GUARD, LANES)


def front_kernel(
    grid, own, mid, got_a, got_b, table,
    ext, first_ref, second_ref, third_ref, part,
    weights_ref, keep_ref, even_ref, odd_ref,
):
    _, rows, depth, _ = own.shape
    plan = Plan(rows)
    even = lax.rem(lax.axis_index("gx"), 2) == 0
    base_a = jnp.where(even, HALO + rows, 0)
    base_b = jnp.where(even, 0, HALO + rows)
    lane = lane_of((depth, LANES))
    halo_lane = (lane < HALO) | (lane >= LANES - HALO)
    for f in range(3):
        for r in range(HALO):
            ext[f, base_a + r, 0] = got_a[f, r]
            ext[f, base_b + r, 0] = got_b[f, r]
        for x in range(rows):
            ext[f, HALO + x, 0] = own[f, x]
        low = jnp.where(even, got_b[f, HALO], got_a[f, HALO])
        high = jnp.where(even, got_a[f, HALO], got_b[f, HALO])
        for r in plan.all:
            x = r - HALO
            source, x = (
                (low, x + rows) if x < 0 else (high, x - rows) if x >= rows else (mid[f], x)
            )
            moved = pltpu.roll(source, (-(SLOT * x + HALO)) % LANES, 1)
            ext[f, r, 1] = jnp.where(halo_lane, moved, 0.0)

    temp, ids, coeff = Rows(), Rows(), Rows()
    for field, f in ((temp, T0), (ids, ID), (coeff, COEFF)):
        field.stacked(ext, plan.all, (f,))
    weights = weight_rows(weights_ref, plan.cone(2), depth)
    keep = Rows()
    keep.stacked(keep_ref, plan.cone(2), (), HALO - 2)
    shifted = [shifted_rows(ref, plan.cone(3), depth) for ref in (even_ref, odd_ref)]
    expand(table, weights, keep, ids, coeff, plan.cone(2), grid, rows, depth)
    for r in plan.cone(3):
        put_shifted(shifted[0], r, [temp.of(r, t, depth) for t in (0, 1)])
    losses = []
    for n in range(STEPS):
        out = Rows()
        out.stacked((first_ref, second_ref, third_ref)[n], plan.cone(2 - n), (), HALO - 2 + n)

        def done(r, t, base, value):
            out.put(r, t, value, base)
            if t == 0 and HALO <= r < HALO + rows:
                rate, _ = rate_of(value)
                losses.append(weights[LINKS].of(r, 0, 8, base) * rate)

        tiles = (0, 1) if n < 2 else (0,)
        advance(weights, keep, coeff, shifted[n % 2], plan.cone(2 - n), tiles, depth, done)
        if n < 2:
            for r in plan.cone(2 - n):
                put_shifted(shifted[(n + 1) % 2], r, [out.of(r, t, depth) for t in (0, 1)])
    loss = losses[0]
    for term in losses[1:]:
        loss = loss + term
    part[...] = jnp.broadcast_to(jnp.sum(loss, axis=0, keepdims=True), part.shape)


def back_kernel(
    grid, ext, first_in, second_in, third_in, table, plate,
    adjoint_out, sens_out,
    weights_ref, keep_ref, states_ref, third_ref, adjoint_ref, sums_ref, drive_ref,
):
    rows, _, depth, _ = third_in.shape
    plan = Plan(rows)
    temp, ids, coeff = Rows(), Rows(), Rows()
    for field, f in ((temp, T0), (ids, ID), (coeff, COEFF)):
        field.stacked(ext, plan.all, (f,))
    for start in (0, weights_ref.shape[0] - GUARD):
        weights_ref[pl.ds(start, GUARD)] = jnp.zeros((GUARD, LANES), jnp.float32)
    weights = weight_rows(weights_ref, plan.cone(5), depth)
    keep = Rows()
    keep.stacked(keep_ref, plan.cone(5), (), HALO - 5)
    shifted, block = [{}, {}, {}], 0
    for n in range(3):
        held = plan.ring(6 - n, 1 - n) if n < 2 else plan.cone(4)
        for oy in (-1, 0, 1):
            shifted[n][oy] = Rows()
            block = shifted[n][oy].flat(states_ref, held, depth, PAD, block)
    clear_pads(states_ref, block, depth)

    expand(table, weights, keep, ids, coeff, plan.cone(5), grid, rows, depth)
    for r in plan.ring(6, 1):
        put_shifted(shifted[0], r, [temp.of(r, t, depth) for t in (0, 1)])
    for r in plan.ring(2, 0):
        put_shifted(shifted[1], r, [first_in[r - HALO + 2, t] for t in (0, 1)])
    for r in plan.cone(1):
        put_shifted(shifted[2], r, [second_in[r - HALO + 1, t] for t in (0, 1)])
    states = [temp, Rows(), shifted[2][0], Rows()]
    states[1].stacked(first_in, plan.cone(2), (), HALO - 2)
    states[3].stacked(third_ref, plan.cone(3), (), HALO - 3)
    for n in range(STEPS):
        fresh = plan.ring(5 - n, 2 - n)
        low, high = [r for r in fresh if r < HALO], [r for r in fresh if r >= HALO]
        out = states[3] if n == 2 else shifted[n + 1][0]

        def done(r, t, base, value):
            out.put(r, t, value, base)

        for part in (low, high):
            advance(weights, keep, coeff, shifted[n], part, (0, 1), depth, done)
        if n == 2:
            advance(weights, keep, coeff, shifted[n], plan.cone(0), (1,), depth, done)
            continue
        for r in fresh:
            pair = [out.of(r, t, depth) for t in (0, 1)]
            for by in (-1, 1):
                moved = lane_shift(pair, by)
                for t in (0, 1):
                    shifted[n + 1][by].put(r, t, moved[t])
    for r in plan.cone(0):
        states[3].where[r, 0] = (third_in, (r - HALO, 0), 0)

    vectors, block = [], 0
    for n in range(3):
        vectors.append(Rows())
        block = vectors[n].flat(adjoint_ref, plan.cone(3 - n), depth, PAD, block)
    clear_pads(adjoint_ref, block, depth)
    drives = [None, Rows(), Rows(), vectors[0]]
    drives[1].stacked(drive_ref, plan.cone(1), (0,), HALO - 2)
    drives[2].stacked(drive_ref, plan.cone(2), (1,), HALO - 2)
    for n in range(1, 4):
        for r in plan.cone(n):
            for t in (0, 1):
                rate, inverse = rate_of(states[n].of(r, t, depth))
                factor = weights[LINKS].of(r, t, depth) * AGE_BETA
                drives[n].put(r, t, factor * rate * (inverse * inverse))
    sums = {}
    for oy in (-1, 0, 1):
        sums[oy] = Rows()
        sums[oy].stacked(sums_ref, plan.cone(2), (oy + 1,), HALO - 2)
    for n in range(3):
        vector = vectors[n]
        targets = plan.cone(2 - n)
        for t in (0, 1):
            for half in range(depth // 8):
                base = 8 * half
                totals = {}
                for source in plan.cone(3 - n):
                    reads = {oz: vector.of(source, t, 8, base - oz) for oz in (-1, 0, 1)}
                    for k, offset in enumerate(HALF_OFFSETS):
                        product = {}
                        for sign in (1, -1):
                            oz, ox, oy = (sign * o for o in offset)
                            if oz not in product:
                                weight = weights[k].of(source, t, 8, base - oz)
                                product[oz] = reads[oz] * weight
                            key = (source + ox, oy)
                            if key[0] in targets:
                                totals[key] = (
                                    totals[key] + product[oz] if key in totals else product[oz]
                                )
                    if source - 1 in targets:
                        for oy in (-1, 0, 1):
                            sums[oy].put(source - 1, t, totals.pop((source - 1, oy)), base)
        for r in targets:
            plus = lane_shift([sums[1].of(r, t, depth) for t in (0, 1)], -1)
            minus = lane_shift([sums[-1].of(r, t, depth) for t in (0, 1)], 1)
            for t in (0, 1) if n < 2 else (0,):
                result = (
                    keep.of(r, t, depth) * vector.of(r, t, depth)
                    + sums[0].of(r, t, depth)
                    + (plus[t] + minus[t])
                )
                if n < 2:
                    vectors[n + 1].put(r, t, result + drives[2 - n].of(r, t, depth))
                else:
                    adjoint_out[:, r - HALO, :] = result
    for r in plan.cone(0):
        total = None
        for n in range(3):
            term = vectors[2 - n].of(r, 0, depth) * (states[n].of(r, 0, depth) - COOL_TEMP)
            total = term if total is None else total + term
        sens_out[:, r - HALO, :] = -total * plate[:, r - HALO, :].astype(jnp.float32)


def scale_kernel(cells, parts, adjoint, sens, adjoint_out, sens_out):
    row = jnp.sum(parts[...], axis=0, keepdims=True)
    scale = cells / jnp.sum(row, axis=1, keepdims=True)
    adjoint_out[...] = adjoint[...] * scale.reshape(1, 1, 1)
    sens_out[...] = sens[...] * scale.reshape(1, 1, 1)


def pairing(count, first, ring):
    out = {}
    for i in range(first, count - 1, 2):
        out[i], out[i + 1] = i + 1, i
    if ring and 0 not in out:
        out[0], out[count - 1] = count - 1, 0
    return out


def swap(value, sizes, axis, first, ring=False):
    count_x, count_y = sizes
    partner = pairing(sizes[axis], first, ring)
    pairs = []
    for i in range(count_x):
        for j in range(count_y):
            other = partner.get((i, j)[axis])
            if other is not None:
                target = (other, j) if axis == 0 else (i, other)
                pairs.append((i * count_y + j, target[0] * count_y + target[1]))
    return lax.ppermute(value, ("gx", "gy"), pairs)


def local(initial_temp, material, plate, cooling, principal, angles, aging_scale):
    depth, rows, width = initial_temp.shape
    sizes = (lax.axis_size("gx"), lax.axis_size("gy"))
    devices = sizes[0] * sizes[1]
    f32 = jnp.float32

    def shape(*dims):
        return jax.ShapeDtypeStruct(dims, f32)

    def call(kernel, name, mib, out_shape, scratch=(), **specs):
        return pl.pallas_call(
            kernel,
            out_shape=out_shape,
            scratch_shapes=[
                pltpu.VMEM(dims, f32) if isinstance(dims, tuple) else dims for dims in scratch
            ],
            name=name,
            compiler_params=pltpu.CompilerParams(vmem_limit_bytes=mib * 2**20),
            **specs,
        )

    block = (depth, rows, LANES)
    own, pack = call(
        pack_kernel,
        "pack",
        2,
        (shape(3, rows, depth, LANES), shape(3, depth, LANES)),
        (
            block,
            pltpu.VMEM(block, jnp.int32),
            pltpu.VMEM(block, jnp.int32),
            block,
            pltpu.SemaphoreType.DMA((4,)),
        ),
        in_specs=[pl.BlockSpec(memory_space=pltpu.HBM)] * 4,
    )(*(pltpu.with_memory_space_constraint(x, pltpu.HBM) for x in (initial_temp, material, plate, cooling)))
    side_b = swap(pack, sizes, 1, 1, True)
    side_a = swap(pack, sizes, 1, 0)
    mid, send_a, send_b = call(
        functools.partial(middle_kernel, sizes[1] - 1),
        "middle",
        2,
        (
            shape(3, depth, LANES),
            shape(3, HALO + 1, depth, LANES),
            shape(3, HALO + 1, depth, LANES),
        ),
    )(own, side_a, side_b)
    got_b = swap(send_b, sizes, 0, 1)
    got_a = swap(send_a, sizes, 0, 0)
    table = call(table_kernel, "table", 2, shape(PARTS, 8, LANES), ((8, LANES),))(
        principal.T, angles.T, aging_scale[None]
    )

    total_rows = rows + 2 * HALO
    pairs = 2 * rows
    grid = (rows * sizes[0], width * sizes[1])
    ext, first, second, third, part = call(
        functools.partial(front_kernel, grid),
        "front",
        20,
        (
            shape(3, total_rows, 2, depth, LANES),
            shape(rows + 4, 2, depth, LANES),
            shape(rows + 2, 2, depth, LANES),
            shape(rows, 1, depth, LANES),
            shape(devices, LANES),
        ),
        (
            guarded_size((LINKS + 1) * (pairs + 8), depth),
            (rows + 4, 2, depth, LANES),
            padded_size(3 * (pairs + 12), depth),
            padded_size(3 * (pairs + 12), depth),
        ),
    )(own, mid, got_a, got_b, table)
    parts = lax.all_to_all(part, ("gx", "gy"), 0, 0, tiled=True)
    adjoint, sens = call(
        functools.partial(back_kernel, grid),
        "back",
        24,
        (shape(*block), shape(*block)),
        (
            guarded_size((LINKS + 1) * (pairs + 20), depth),
            (rows + 10, 2, depth, LANES),
            padded_size(3 * (2 * 10 + 2 * 10 + pairs + 16), depth),
            (rows + 6, 2, depth, LANES),
            padded_size(3 * pairs + 4 * (3 + 2 + 1), depth),
            (3, rows + 4, 2, depth, LANES),
            (2, rows + 4, 2, depth, LANES),
        ),
    )(ext, first, second, third, table, plate)
    return call(
        functools.partial(scale_kernel, float(depth * rows * width * devices)),
        "scale",
        2,
        (shape(*block), shape(*block)),
    )(parts, adjoint, sens)


def solution(mesh):
    block = P(None, "gx", "gy")
    return jax.shard_map(
        local,
        mesh=mesh,
        in_specs=(block, block, block, block, P(), P(), P()),
        out_specs=(block, block),
        check_vma=False,
    )
```

time: 34.9 us -> 31.1 us (0.89)
  starting transfers between devices: 18.4 us -> 14.7 us
  local copies, waits for them, and re-layouts: 4.06 us -> 0.68 us
  waiting for transfers between devices: 4.4 us -> 7.53 us
    ppermute x6 -> x4, starting transfers between devices: 9.51 us -> 5.27 us  [swap(): return lax.ppermute(value, ('gx', 'gy'), pairs)]
    unnamed x16 -> x8, local copies, waits for them, and re-layouts: 4.06 us -> 0.68 us
    ppermute x6 -> x4, waiting for transfers between devices: 0.38 us -> 3.3 us  [swap(): return lax.ppermute(value, ('gx', 'gy'), pairs)]
    all_to_all x1, starting transfers between devices: 8.88 us -> 9.48 us  [local(): parts = lax.all_to_all(part, ('gx', 'gy'), 0, 0, tiled=True)]
    pallas_call x3 -> x4, Pallas kernels: 6 us -> 6.3 us  [the longest x1 2.87 us: local(): call(functools.partial(back_kernel, grid), 'back', 24, (shape(*block), sh...]
  transfers between devices with their start and end apart: 7 -> 5, of which waited for: 2 -> 3; matrix products, arithmetic and copies ran while one was open for 0% -> 0% of each run, Pallas kernels for 9% -> 10%
where the time goes in v3:
time: 31.1 us; the launch traced here: 30.9 us
  starting transfers between devices  14.7 us (47%)
  waiting for transfers between devices  7.53 us (24%)
  Pallas kernels  7.18 us (23%)
  between operations  0.74 us (2%)
  local copies, waits for them, and re-layouts  0.68 us (2%)
    all_to_all x1, starting transfers between devices, local(): parts = lax.all_to_all(part, ('gx', 'gy'), 0, 0, tiled=True)  9.48 us
    ppermute x4, starting transfers between devices, swap(): return lax.ppermute(value, ('gx', 'gy'), pairs)  5.27 us
    all_to_all x1, waiting for transfers between devices, local(): parts = lax.all_to_all(part, ('gx', 'gy'), 0, 0, tiled=True)  4.23 us
    ppermute x4, waiting for transfers between devices, swap(): return lax.ppermute(value, ('gx', 'gy'), pairs)  3.3 us
    pallas_call x1, Pallas kernels, local(): call(functools.partial(back_kernel, grid), 'back', 24, (shape(*block), sh...  2.87 us
    pallas_call x1, Pallas kernels, local(): call(functools.partial(front_kernel, grid), 'front', 20, (shape(3, total_...  2.19 us
    pallas_call x1, Pallas kernels, local(): call(pack_kernel, 'pack', 2, (shape(3, rows, depth, LANES), shape(3, dept...  1.2 us
    pallas_call x1, Pallas kernels, local(): call(functools.partial(scale_kernel, float(depth * rows * width * devices...  0.75 us
  transfers between devices with their start and end apart: 5, of which 3 were waited for; matrix products, arithmetic and copies ran while one was open for 0% of the time, Pallas kernels for 10%

profile of v3, /device:TPU:0, one launch (start us, length us, event | category | flops | bytes accessed | tf_op | source)
XLA Modules:
  0.0 30.9 jit_solution(14905234140748984795)
XLA Ops:
  0.6 1.2 %pack.1 = (f32[3,8,16,128]{3,2,1,0:T(8,128)S(1)}, f32[3,16,128]{2,1,0:T(8,128)S(1)}) custom-call(f32[16,8,128]{2,1,0:T(8,128)} %temp_in.1, s32[16,8,128]{2,1,0:T(8,128)} %material_in.1, s32[16,8,128]{2,1,0:T(8,128)} %plate.1, f32[16,8,128]{2,1,0:T(8,128)} %cooling_in.1), custom_call_target="tpu_custom_call" | custom-call | tf_op jit(solution)/shard_map/pack/pallas_call | solution.py:518
  1.8 4.0 %collective-permute-start.1 = (f32[3,16,128]{2,1,0:T(8,128)S(1)}, f32[3,16,128]{2,1,0:T(8,128)S(1)}, u32[]{:S(2)}, u32[]{:S(2)}) collective-permute-start(f32[3,16,128]{2,1,0:T(8,128)S(1)} %get-tuple-element.15), channel_id=1, source_target_pairs={{0,3},{1,2},{2,1},{3,0},{4,7},{5,6},{6,5},{7,4},{8,11},{9,10},{10,... | collective-permute-start | bytes 73736 | tf_op jit(solution)/shard_map/ppermute | solution.py:493
  5.8 0.5 %collective-permute-start = (f32[3,16,128]{2,1,0:T(8,128)S(1)}, f32[3,16,128]{2,1,0:T(8,128)S(1)}, u32[]{:S(2)}, u32[]{:S(2)}) collective-permute-start(f32[3,16,128]{2,1,0:T(8,128)S(1)} %get-tuple-element.15), channel_id=1, source_target_pairs={{0,1},{1,0},{2,3},{3,2},{4,5},{5,4},{6,7},{7,6},{8,9},{9,8},{10,11... | collective-permute-start | bytes 73736 | tf_op jit(solution)/shard_map/ppermute | solution.py:493
  6.4 1.3 %collective-permute-done.1.side_b = f32[3,16,128]{2,1,0:T(8,128)S(1)} collective-permute-done((f32[3,16,128]{2,1,0:T(8,128)S(1)}, f32[3,16,128]{2,1,0:T(8,128)S(1)}, u32[]{:S(2)}, u32[]{:S(2)}) %collective-permute-start.1) | collective-permute-done | bytes 24608 | tf_op jit(solution)/shard_map/ppermute | solution.py:493
  7.6 2.0 %collective-permute-done.side_a = f32[3,16,128]{2,1,0:T(8,128)S(1)} collective-permute-done((f32[3,16,128]{2,1,0:T(8,128)S(1)}, f32[3,16,128]{2,1,0:T(8,128)S(1)}, u32[]{:S(2)}, u32[]{:S(2)}) %collective-permute-start) | collective-permute-done | bytes 24608 | tf_op jit(solution)/shard_map/ppermute | solution.py:493
  9.7 0.1 collective-permute-start.2
  9.8 0.7 %collective-permute-start.3 = (f32[3,7,16,128]{3,2,1,0:T(8,128)S(1)}, f32[3,7,16,128]{3,2,1,0:T(8,128)S(1)}, u32[]{:S(2)}, u32[]{:S(2)}) collective-permute-start(f32[3,7,16,128]{3,2,1,0:T(8,128)S(1)} %get-tuple-element.18), channel_id=1, source_target_pairs={{4,8},{5,9},{6,10},{7,11},{8,4},{9,5},{10,6},{11,7},{12,16},{13,17... | collective-permute-start | bytes 516104 | tf_op jit(solution)/shard_map/ppermute | solution.py:493
  10.4 0.0 copy-start.2
  10.5 0.0 copy-start.1
  10.5 0.0 copy-start.3
  10.5 0.6 %copy-done.2 = f32[16,3]{0,1:T(4,128)S(1)} copy-done((f32[16,3]{0,1:T(4,128)S(1)}, f32[16,3]{0,1:T(4,128)}, u32[]{:S(2)}) %copy-start.2) | copy-done | bytes 216
  11.1 0.0 copy-done.1
  11.1 0.0 copy-done.3
  11.2 0.1 table.1
  11.3 0.0 collective-permute-done.2.got_a
  11.3 0.0 collective-permute-done.3.got_b
  11.3 0.0 copy-start
  11.3 2.2 %front.1 = (f32[3,20,2,16,128]{4,3,2,1,0:T(8,128)S(1)}, f32[12,2,16,128]{3,2,1,0:T(8,128)S(1)}, f32[10,2,16,128]{3,2,1,0:T(8,128)S(1)}, f32[8,1,16,128]{3,2,1,0:T(8,128)S(1)}, f32[32,128]{1,0:T(8,128)}) custom-call(f32[3,8,16,128]{3,2,1,0:T(8,128)S(1)} %get-tuple-element.14.own, f32[3,16,128]{2,1,0:T(8,128)S(1)} %get-tuple-element.16.mid, ...), custom_call_target="tpu_custom_call" | custom-call | tf_op jit(solution)/shard_map/front/pallas_call | solution.py:553
  13.5 9.5 %all-to-all-start = ((f32[32,1,128]{2,1,0:T(1,128)}), f32[32,1,128]{2,1,0:T(1,128)S(1)}, u32[]{:S(2)}, u32[]{:S(2)}) async-start(f32[32,1,128]{2,1,0:T(1,128)} %bitcast.4), calls=%async_computation | async-start | bytes 32768 | tf_op jit(solution)/shard_map/all_to_all | solution.py:571
  23.0 0.0 copy-done
  23.0 2.9 %back.1 = (f32[16,8,128]{2,1,0:T(8,128)S(1)}, f32[16,8,128]{2,1,0:T(8,128)S(1)}) custom-call(f32[3,20,2,16,128]{4,3,2,1,0:T(8,128)S(1)} %get-tuple-element.20.ext, f32[12,2,16,128]{3,2,1,0:T(8,128)S(1)} %get-tuple-element.21.first_in, f32[10,2,16,128]{3,2,1,0:T(8,128)S(1)} %get-tuple-element.22.second_in, f32[8,1,16,128]{3,2,1,0:T(8,128)S(1)} %get-tuple-element.23.third_in, ...), custom_call_target="tpu_custom_call" | custom-call | tf_op jit(solution)/shard_map/back/pallas_call | solution.py:572
  25.9 4.2 %all-to-all-done = f32[32,1,128]{2,1,0:T(1,128)S(1)} async-done(((f32[32,1,128]{2,1,0:T(1,128)}), f32[32,1,128]{2,1,0:T(1,128)S(1)}, u32[]{:S(2)}, u32[]{:S(2)}) %all-to-all-start) | async-done | bytes 16416 | tf_op jit(solution)/shard_map/all_to_all | solution.py:571
  30.1 0.7 %scale.1 = (f32[16,8,128]{2,1,0:T(8,128)}, f32[16,8,128]{2,1,0:T(8,128)}) custom-call(f32[32,128]{1,0:T(8,128)S(1)} %bitcast.7, f32[16,8,128]{2,1,0:T(8,128)S(1)} %get-tuple-element.24.adjoint, f32[16,8,128]{2,1,0:T(8,128)S(1)} %get-tuple-element.25.sens), custom_call_target="tpu_custom_call" | custom-call | tf_op jit(solution)/shard_map/scale/pallas_call | solution.py:587
  (1 shorter events, 0.0 us)
Async XLA Ops:
  1.8 5.8 %collective-permute-start.1 = (f32[3,16,128]{2,1,0:T(8,128)S(1)}, f32[3,16,128]{2,1,0:T(8,128)S(1)}, u32[]{:S(2)}, u32[]{:S(2)}) collective-permute-start(f32[3,16,128]{2,1,0:T(8,128)S(1)} %get-tuple-element.15), channel_id=1, source_target_pairs={{0,3},{1,2},{2,1},{3,0},{4,7},{5,6},{6,5},{7,4},{8,11},{9,10},{10,... | collective-permute-start | bytes 73736 | tf_op jit(solution)/shard_map/ppermute | solution.py:493
  5.8 3.8 %collective-permute-start = (f32[3,16,128]{2,1,0:T(8,128)S(1)}, f32[3,16,128]{2,1,0:T(8,128)S(1)}, u32[]{:S(2)}, u32[]{:S(2)}) collective-permute-start(f32[3,16,128]{2,1,0:T(8,128)S(1)} %get-tuple-element.15), channel_id=1, source_target_pairs={{0,1},{1,0},{2,3},{3,2},{4,5},{5,4},{6,7},{7,6},{8,9},{9,8},{10,11... | collective-permute-start | bytes 73736 | tf_op jit(solution)/shard_map/ppermute | solution.py:493
  9.7 1.6 %collective-permute-start.2 = (f32[3,7,16,128]{3,2,1,0:T(8,128)S(1)}, f32[3,7,16,128]{3,2,1,0:T(8,128)S(1)}, u32[]{:S(2)}, u32[]{:S(2)}) collective-permute-start(f32[3,7,16,128]{3,2,1,0:T(8,128)S(1)} %get-tuple-element.17), channel_id=1, source_target_pairs={{0,4},{1,5},{2,6},{3,7},{4,0},{5,1},{6,2},{7,3},{8,12},{9,13},{10,... | collective-permute-start | bytes 516104 | tf_op jit(solution)/shard_map/ppermute | solution.py:493
  9.8 1.5 %collective-permute-start.3 = (f32[3,7,16,128]{3,2,1,0:T(8,128)S(1)}, f32[3,7,16,128]{3,2,1,0:T(8,128)S(1)}, u32[]{:S(2)}, u32[]{:S(2)}) collective-permute-start(f32[3,7,16,128]{3,2,1,0:T(8,128)S(1)} %get-tuple-element.18), channel_id=1, source_target_pairs={{4,8},{5,9},{6,10},{7,11},{8,4},{9,5},{10,6},{11,7},{12,16},{13,17... | collective-permute-start | bytes 516104 | tf_op jit(solution)/shard_map/ppermute | solution.py:493
  10.4 0.7 %copy-start.2 = (f32[16,3]{0,1:T(4,128)S(1)}, f32[16,3]{0,1:T(4,128)}, u32[]{:S(2)}) copy-start(f32[16,3]{0,1:T(4,128)} %param.12) | copy-start | bytes 580
  10.5 0.7 %copy-start.1 = (f32[16,3]{0,1:T(4,128)S(1)}, f32[16,3]{0,1:T(4,128)}, u32[]{:S(2)}) copy-start(f32[16,3]{0,1:T(4,128)} %param.11) | copy-start | bytes 580
  10.5 0.7 %copy-start.3 = (f32[16]{0:T(128)S(1)}, f32[16]{0:T(128)}, u32[]{:S(2)}) copy-start(f32[16]{0:T(128)} %param.13) | copy-start | bytes 196
  11.3 11.7 %copy-start = (s32[16,8,128]{2,1,0:T(8,128)S(1)}, s32[16,8,128]{2,1,0:T(8,128)}, u32[]{:S(2)}) copy-start(s32[16,8,128]{2,1,0:T(8,128)} %plate.1) | copy-start | bytes 196612
  13.5 16.6 %all-to-all-start = ((f32[32,1,128]{2,1,0:T(1,128)}), f32[32,1,128]{2,1,0:T(1,128)S(1)}, u32[]{:S(2)}, u32[]{:S(2)}) async-start(f32[32,1,128]{2,1,0:T(1,128)} %bitcast.4), calls=%async_computation | async-start | bytes 32768 | tf_op jit(solution)/shard_map/all_to_all | solution.py:571

commit v4 on v3

--- a/solution.py
+++ b/solution.py
@@ -23,7 +23,9 @@
 LANES = 128
 SLOT = 16
 T0, ID, COEFF = 0, 1, 2
-VMEM = pl.BlockSpec(memory_space=pltpu.VMEM)
+SENT = (HALO, HALO - 1, HALO - 1)
+PLACE = (3, 3 + HALO, 3 + 2 * HALO - 1)
+PAYLOAD = 3 + sum(SENT)
 PAD = 8
 GUARD = 8
 PARTS = 7
@@ -33,7 +35,19 @@
     return lax.broadcasted_iota(jnp.int32, shape, len(shape) - 1)
 
 
-def table_kernel(principal, angles, aging, table, line):
+def copy_in(pairs, sems):
+    copies = [
+        pltpu.make_async_copy(source, target, sems.at[i])
+        for i, (source, target) in enumerate(pairs)
+    ]
+    for copy in copies:
+        copy.start()
+    for copy in copies:
+        copy.wait()
+
+
+def table_kernel(principal_in, angles_in, aging_in, table, principal, angles, aging, line, sems):
+    copy_in(((principal_in, principal), (angles_in, angles), (aging_in, aging)), sems)
     count = aging.shape[1]
     line[...] = jnp.zeros_like(line)
     line[0:3, 0:count] = principal[...]
@@ -59,16 +73,9 @@
 
 
 def pack_kernel(temp_in, material_in, plate_in, cooling_in, own, pack, temp, material, plate, cooling, sems):
-    copies = [
-        pltpu.make_async_copy(source, target, sems.at[i])
-        for i, (source, target) in enumerate(
-            ((temp_in, temp), (material_in, material), (plate_in, plate), (cooling_in, cooling))
-        )
-    ]
-    for copy in copies:
-        copy.start()
-    for copy in copies:
-        copy.wait()
+    copy_in(
+        ((temp_in, temp), (material_in, material), (plate_in, plate), (cooling_in, cooling)), sems
+    )
     depth, rows, _ = temp.shape
     lane = lane_of((depth, LANES))
     packs = [jnp.zeros((depth, LANES), jnp.float32) for _ in range(3)]
@@ -98,14 +105,15 @@
         right = jnp.where(at_y == last_y, 0.0, jnp.where(even_y, side_a[f], side_b[f]))
         value = jnp.where(from_left, left, right)
         mid[f] = value
-        send_a[f, HALO] = value
-        send_b[f, HALO] = value
-    first_a = jnp.where(even_x, rows - HALO, 0)
-    first_b = jnp.where(even_x, 0, rows - HALO)
+        send_a[f] = value
+        send_b[f] = value
     for f in range(3):
-        for r in range(HALO):
-            send_a[f, r] = own[f, first_a + r]
-            send_b[f, r] = own[f, first_b + r]
+        count = SENT[f]
+        first_a = jnp.where(even_x, rows - count, 0)
+        first_b = jnp.where(even_x, 0, rows - count)
+        for r in range(count):
+            send_a[PLACE[f] + r] = own[f, first_a + r]
+            send_b[PLACE[f] + r] = own[f, first_b + r]
 
 
 class Rows:
@@ -250,7 +258,7 @@
 class Plan:
     def __init__(self, rows):
         self.rows = rows
-        self.all = range(rows + 2 * HALO)
+        self.middle = HALO + rows // 2
 
     def cone(self, radius):
         return range(HALO - radius, HALO + self.rows + radius)
@@ -260,22 +268,42 @@
         return [r for r in self.cone(radius) if r not in middle]
 
 
-def weight_rows(ref, rows, depth):
-    weights, block = [], 0
-    for _ in range(LINKS + 1):
-        field = Rows()
+def weight_rows(weights, ref, rows, depth):
+    block = 0
+    for field in weights:
         block = field.flat(ref, rows, depth, 0, block)
-        weights.append(field)
-    return weights
-
-
-def shifted_rows(ref, rows, depth):
-    fields, block = {}, 0
+
+
+def shifted_rows(fields, ref, rows, depth, block=0):
     for oy in (-1, 0, 1):
-        fields[oy] = Rows()
         block = fields[oy].flat(ref, rows, depth, PAD, block)
-    clear_pads(ref, block, depth)
-    return fields
+    return block
+
+
+def new_weights():
+    return [Rows() for _ in range(LINKS + 1)]
+
+
+def new_shifted():
+    return {oy: Rows() for oy in (-1, 0, 1)}
+
+
+def halves(rows, middle):
+    return [r for r in rows if r < middle], [r for r in rows if r >= middle]
+
+
+def march(n, weights, keep, coeff, source, target, out, rows, tiles, depth, loss):
+    def done(r, t, base, value):
+        out.put(r, t, value, base)
+        if loss is not None and t == 0 and loss[0] <= r < loss[1]:
+            rate, _ = rate_of(value)
+            loss[2].append(weights[LINKS].of(r, 0, 8, base) * rate)
+
+    for part in rows if isinstance(rows, tuple) else (rows,):
+        advance(weights, keep, coeff, source, part, tiles, depth, done)
+        if target is not None:
+            for r in part:
+                put_shifted(target, r, [out.of(r, t, depth) for t in (0, 1)])
 
 
 def padded_size(blocks, depth):
@@ -286,108 +314,168 @@
     return (blocks * depth + 2 * GUARD, LANES)
 
 
+def total_of(terms):
+    total = terms[0]
+    for term in terms[1:]:
+        total = total + term
+    return total
+
+
+def unpack(target, f, at, source, x, halo_lane):
+    moved = pltpu.roll(source, (-(SLOT * x + HALO)) % LANES, 1)
+    target[(f, *at)] = jnp.where(halo_lane, moved, 0.0)
+
+
+def core_kernel(
+    grid, own, mid, table,
+    halo, weights_ref, keep_ref, start_ref, first, first_ref, second, second_ref, third, loss_ref,
+):
+    _, rows, depth, _ = own.shape
+    plan = Plan(rows)
+    lane = lane_of((depth, LANES))
+    halo_lane = (lane < HALO) | (lane >= LANES - HALO)
+    for f in range(3):
+        for x in range(rows):
+            unpack(halo, f, (x,), mid[f], x, halo_lane)
+    temp, ids, coeff = own_fields(own, halo, plan)
+    weights, keep = new_weights(), Rows()
+    weight_rows(weights, weights_ref, plan.cone(0), depth)
+    keep.stacked(keep_ref, plan.cone(0), (), HALO)
+    shifted, outs = [new_shifted() for _ in range(3)], [Rows() for _ in range(3)]
+    for n, (ref, out) in enumerate(((start_ref, first), (first_ref, second), (second_ref, third))):
+        clear_pads(ref, shifted_rows(shifted[n], ref, plan.cone(-n), depth), depth)
+        outs[n].stacked(out, plan.cone(-n - 1), (), HALO + n + 1)
+    expand(table, weights, keep, ids, coeff, plan.cone(0), grid, rows, depth)
+    for r in plan.cone(0):
+        put_shifted(shifted[0], r, [temp.of(r, t, depth) for t in (0, 1)])
+    loss = (HALO, HALO + rows, [])
+    for n in range(STEPS):
+        target = shifted[n + 1] if n < 2 else None
+        tiles = (0, 1) if n < 2 else (0,)
+        march(n, weights, keep, coeff, shifted[n], target, outs[n], plan.cone(-n - 1), tiles, depth, loss)
+    loss_ref[...] = total_of(loss[2])
+
+
+def own_fields(own, halo, plan):
+    fields = (Rows(), Rows(), Rows())
+    for f, field in enumerate(fields):
+        for r in plan.cone(0):
+            field.where[r, 0] = (own, (f, r - HALO), 0)
+            field.where[r, 1] = (halo, (f, r - HALO), 0)
+    return fields
+
+
+def all_fields(own, halo, ext, plan):
+    fields = own_fields(own, halo, plan)
+    for f, field in enumerate(fields):
+        for i, r in enumerate(plan.ring(HALO, 0)):
+            for t in (0, 1):
+                field.where[r, t] = (ext, (f, i, t), 0)
+    return fields
+
+
 def front_kernel(
-    grid, own, mid, got_a, got_b, table,
-    ext, first_ref, second_ref, third_ref, part,
-    weights_ref, keep_ref, even_ref, odd_ref,
+    grid, own, halo, got_a, got_b, table, weights_in, keep_in, start_in, first_in, second_in, loss_in,
+    ext, first, second, third, part,
+    weights_ref, keep_ref, start_ref, first_ref, second_ref,
 ):
     _, rows, depth, _ = own.shape
     plan = Plan(rows)
     even = lax.rem(lax.axis_index("gx"), 2) == 0
-    base_a = jnp.where(even, HALO + rows, 0)
-    base_b = jnp.where(even, 0, HALO + rows)
     lane = lane_of((depth, LANES))
     halo_lane = (lane < HALO) | (lane >= LANES - HALO)
     for f in range(3):
+        base_a = jnp.where(even, HALO, HALO - SENT[f])
+        base_b = jnp.where(even, HALO - SENT[f], HALO)
+        for r in range(SENT[f]):
+            ext[f, base_a + r, 0] = got_a[PLACE[f] + r]
+            ext[f, base_b + r, 0] = got_b[PLACE[f] + r]
+        low = jnp.where(even, got_b[f], got_a[f])
+        high = jnp.where(even, got_a[f], got_b[f])
         for r in range(HALO):
-            ext[f, base_a + r, 0] = got_a[f, r]
-            ext[f, base_b + r, 0] = got_b[f, r]
-        for x in range(rows):
-            ext[f, HALO + x, 0] = own[f, x]
-        low = jnp.where(even, got_b[f, HALO], got_a[f, HALO])
-        high = jnp.where(even, got_a[f, HALO], got_b[f, HALO])
-        for r in plan.all:
-            x = r - HALO
-            source, x = (
-                (low, x + rows) if x < 0 else (high, x - rows) if x >= rows else (mid[f], x)
-            )
-            moved = pltpu.roll(source, (-(SLOT * x + HALO)) % LANES, 1)
-            ext[f, r, 1] = jnp.where(halo_lane, moved, 0.0)
-
-    temp, ids, coeff = Rows(), Rows(), Rows()
-    for field, f in ((temp, T0), (ids, ID), (coeff, COEFF)):
-        field.stacked(ext, plan.all, (f,))
-    weights = weight_rows(weights_ref, plan.cone(2), depth)
-    keep = Rows()
-    keep.stacked(keep_ref, plan.cone(2), (), HALO - 2)
-    shifted = [shifted_rows(ref, plan.cone(3), depth) for ref in (even_ref, odd_ref)]
-    expand(table, weights, keep, ids, coeff, plan.cone(2), grid, rows, depth)
-    for r in plan.cone(3):
+            unpack(ext, f, (r, 1), low, rows - HALO + r, halo_lane)
+            unpack(ext, f, (HALO + r, 1), high, r, halo_lane)
+
+    temp, ids, coeff = all_fields(own, halo, ext, plan)
+    weights, keep = new_weights(), Rows()
+    outer = plan.ring(2, 0)
+    weight_rows(weights, weights_in, plan.cone(0), depth)
+    weight_rows(weights, weights_ref, outer, depth)
+    keep.stacked(keep_in, plan.cone(0), (), HALO)
+    for i, r in enumerate(outer):
+        for t in (0, 1):
+            keep.where[r, t] = (keep_ref, (i, t), 0)
+    shifted, outs = [new_shifted() for _ in range(3)], [Rows() for _ in range(3)]
+    for n, (given, ref, out) in enumerate(
+        ((start_in, start_ref, first), (first_in, first_ref, second), (second_in, second_ref, third))
+    ):
+        shifted_rows(shifted[n], given, plan.cone(-n), depth)
+        fresh = plan.ring(3 - n, -n)
+        clear_pads(ref, shifted_rows(shifted[n], ref, fresh, depth), depth)
+        for i, r in enumerate(plan.ring(2 - n, -n - 1)):
+            for t in (0, 1) if n < 2 else (0,):
+                outs[n].where[r, t] = (out, (i, t), 0)
+    expand(table, weights, keep, ids, coeff, outer, grid, rows, depth)
+    for r in plan.ring(3, 0):
         put_shifted(shifted[0], r, [temp.of(r, t, depth) for t in (0, 1)])
-    losses = []
+    loss = (HALO, HALO + rows, [])
     for n in range(STEPS):
-        out = Rows()
-        out.stacked((first_ref, second_ref, third_ref)[n], plan.cone(2 - n), (), HALO - 2 + n)
-
-        def done(r, t, base, value):
-            out.put(r, t, value, base)
-            if t == 0 and HALO <= r < HALO + rows:
-                rate, _ = rate_of(value)
-                losses.append(weights[LINKS].of(r, 0, 8, base) * rate)
-
+        ring = halves(plan.ring(2 - n, -n - 1), plan.middle)
+        target = shifted[n + 1] if n < 2 else None
         tiles = (0, 1) if n < 2 else (0,)
-        advance(weights, keep, coeff, shifted[n % 2], plan.cone(2 - n), tiles, depth, done)
-        if n < 2:
-            for r in plan.cone(2 - n):
-                put_shifted(shifted[(n + 1) % 2], r, [out.of(r, t, depth) for t in (0, 1)])
-    loss = losses[0]
-    for term in losses[1:]:
-        loss = loss + term
-    part[...] = jnp.broadcast_to(jnp.sum(loss, axis=0, keepdims=True), part.shape)
+        march(n, weights, keep, coeff, shifted[n], target, outs[n], ring, tiles, depth, loss)
+    total = loss_in[...] + total_of(loss[2])
+    part[...] = jnp.broadcast_to(jnp.sum(total, axis=0, keepdims=True), part.shape)
 
 
 def back_kernel(
-    grid, ext, first_in, second_in, third_in, table, plate,
+    grid, own, halo, ext, first_core, second_core, third_core, first_in, second_in, third_in, table, plate,
     adjoint_out, sens_out,
     weights_ref, keep_ref, states_ref, third_ref, adjoint_ref, sums_ref, drive_ref,
 ):
-    rows, _, depth, _ = third_in.shape
+    _, rows, depth, _ = own.shape
     plan = Plan(rows)
-    temp, ids, coeff = Rows(), Rows(), Rows()
-    for field, f in ((temp, T0), (ids, ID), (coeff, COEFF)):
-        field.stacked(ext, plan.all, (f,))
+    temp, ids, coeff = all_fields(own, halo, ext, plan)
     for start in (0, weights_ref.shape[0] - GUARD):
         weights_ref[pl.ds(start, GUARD)] = jnp.zeros((GUARD, LANES), jnp.float32)
-    weights = weight_rows(weights_ref, plan.cone(5), depth)
-    keep = Rows()
+    weights, keep = new_weights(), Rows()
+    weight_rows(weights, weights_ref, plan.cone(5), depth)
     keep.stacked(keep_ref, plan.cone(5), (), HALO - 5)
-    shifted, block = [{}, {}, {}], 0
+    shifted, block = [new_shifted() for _ in range(3)], 0
     for n in range(3):
         held = plan.ring(6 - n, 1 - n) if n < 2 else plan.cone(4)
-        for oy in (-1, 0, 1):
-            shifted[n][oy] = Rows()
-            block = shifted[n][oy].flat(states_ref, held, depth, PAD, block)
+        block = shifted_rows(shifted[n], states_ref, held, depth, block)
     clear_pads(states_ref, block, depth)
+    states = [temp, Rows(), Rows(), Rows()]
+    for n, (core, given) in enumerate(
+        ((first_core, first_in), (second_core, second_in), (third_core, third_in))
+    ):
+        tiles = (0, 1) if n < 2 else (0,)
+        states[n + 1].stacked(core, plan.cone(-n - 1), (), HALO + n + 1, tiles)
+        for i, r in enumerate(plan.ring(2 - n, -n - 1)):
+            for t in tiles:
+                states[n + 1].where[r, t] = (given, (i, t), 0)
 
     expand(table, weights, keep, ids, coeff, plan.cone(5), grid, rows, depth)
     for r in plan.ring(6, 1):
         put_shifted(shifted[0], r, [temp.of(r, t, depth) for t in (0, 1)])
     for r in plan.ring(2, 0):
-        put_shifted(shifted[1], r, [first_in[r - HALO + 2, t] for t in (0, 1)])
+        put_shifted(shifted[1], r, [states[1].of(r, t, depth) for t in (0, 1)])
     for r in plan.cone(1):
-        put_shifted(shifted[2], r, [second_in[r - HALO + 1, t] for t in (0, 1)])
-    states = [temp, Rows(), shifted[2][0], Rows()]
-    states[1].stacked(first_in, plan.cone(2), (), HALO - 2)
-    states[3].stacked(third_ref, plan.cone(3), (), HALO - 3)
+        put_shifted(shifted[2], r, [states[2].of(r, t, depth) for t in (0, 1)])
+    states[2] = shifted[2][0]
+    found = Rows()
+    found.stacked(third_ref, plan.cone(3), (), HALO - 3)
+    for key, place in found.where.items():
+        states[3].where.setdefault(key, place)
     for n in range(STEPS):
         fresh = plan.ring(5 - n, 2 - n)
-        low, high = [r for r in fresh if r < HALO], [r for r in fresh if r >= HALO]
         out = states[3] if n == 2 else shifted[n + 1][0]
 
         def done(r, t, base, value):
             out.put(r, t, value, base)
 
-        for part in (low, high):
+        for part in halves(fresh, plan.middle):
             advance(weights, keep, coeff, shifted[n], part, (0, 1), depth, done)
         if n == 2:
             advance(weights, keep, coeff, shifted[n], plan.cone(0), (1,), depth, done)
@@ -398,8 +486,6 @@
                 moved = lane_shift(pair, by)
                 for t in (0, 1):
                     shifted[n + 1][by].put(r, t, moved[t])
-    for r in plan.cone(0):
-        states[3].where[r, 0] = (third_in, (r - HALO, 0), 0)
 
     vectors, block = [], 0
     for n in range(3):
@@ -535,39 +621,58 @@
         functools.partial(middle_kernel, sizes[1] - 1),
         "middle",
         2,
-        (
-            shape(3, depth, LANES),
-            shape(3, HALO + 1, depth, LANES),
-            shape(3, HALO + 1, depth, LANES),
-        ),
+        (shape(3, depth, LANES), shape(PAYLOAD, depth, LANES), shape(PAYLOAD, depth, LANES)),
     )(own, side_a, side_b)
     got_b = swap(send_b, sizes, 0, 1)
     got_a = swap(send_a, sizes, 0, 0)
-    table = call(table_kernel, "table", 2, shape(PARTS, 8, LANES), ((8, LANES),))(
-        principal.T, angles.T, aging_scale[None]
-    )
-
-    total_rows = rows + 2 * HALO
+    small = [principal.T, angles.T, aging_scale[None]]
+    table = call(
+        table_kernel,
+        "table",
+        2,
+        shape(PARTS, 8, LANES),
+        (*(x.shape for x in small), (8, LANES), pltpu.SemaphoreType.DMA((3,))),
+        in_specs=[pl.BlockSpec(memory_space=pltpu.HBM)] * 3,
+    )(*(pltpu.with_memory_space_constraint(x, pltpu.HBM) for x in small))
+
     pairs = 2 * rows
     grid = (rows * sizes[0], width * sizes[1])
+    halo, weights, keep, start, first_core, first_moved, second_core, second_moved, third_core, loss = call(
+        functools.partial(core_kernel, grid),
+        "core",
+        8,
+        (
+            shape(3, rows, depth, LANES),
+            shape(*guarded_size((LINKS + 1) * pairs, depth)),
+            shape(rows, 2, depth, LANES),
+            shape(*padded_size(3 * pairs, depth)),
+            shape(rows - 2, 2, depth, LANES),
+            shape(*padded_size(3 * (pairs - 4), depth)),
+            shape(rows - 4, 2, depth, LANES),
+            shape(*padded_size(3 * (pairs - 8), depth)),
+            shape(rows - 6, 1, depth, LANES),
+            shape(8, LANES),
+        ),
+    )(own, mid, table)
     ext, first, second, third, part = call(
         functools.partial(front_kernel, grid),
         "front",
-        20,
+        16,
         (
-            shape(3, total_rows, 2, depth, LANES),
-            shape(rows + 4, 2, depth, LANES),
-            shape(rows + 2, 2, depth, LANES),
-            shape(rows, 1, depth, LANES),
+            shape(3, 2 * HALO, 2, depth, LANES),
+            shape(6, 2, depth, LANES),
+            shape(6, 2, depth, LANES),
+            shape(6, 1, depth, LANES),
             shape(devices, LANES),
         ),
         (
-            guarded_size((LINKS + 1) * (pairs + 8), depth),
-            (rows + 4, 2, depth, LANES),
-            padded_size(3 * (pairs + 12), depth),
-            padded_size(3 * (pairs + 12), depth),
+            guarded_size((LINKS + 1) * 8, depth),
+            (4, 2, depth, LANES),
+            padded_size(3 * 12, depth),
+            padded_size(3 * 12, depth),
+            padded_size(3 * 12, depth),
         ),
-    )(own, mid, got_a, got_b, table)
+    )(own, halo, got_a, got_b, table, weights, keep, start, first_moved, second_moved, loss)
     parts = lax.all_to_all(part, ("gx", "gy"), 0, 0, tiled=True)
     adjoint, sens = call(
         functools.partial(back_kernel, grid),
@@ -583,7 +688,7 @@
             (3, rows + 4, 2, depth, LANES),
             (2, rows + 4, 2, depth, LANES),
         ),
-    )(ext, first, second, third, table, plate)
+    )(own, halo, ext, first_core, second_core, third_core, first, second, third, table, plate)
     return call(
         functools.partial(scale_kernel, float(depth * rows * width * devices)),
         "scale",

time: 31.1 us -> 30.3 us (0.974)
  starting transfers between devices: 14.7 us -> 13.4 us
  Pallas kernels: 7.18 us -> 8.43 us
  local copies, waits for them, and re-layouts: 0.68 us -> 0.01 us
    all_to_all x1, starting transfers between devices: 9.48 us -> 8.17 us  [local(): parts = lax.all_to_all(part, ('gx', 'gy'), 0, 0, tiled=True)]
    pallas_call x2 -> x3, Pallas kernels: 2.32 us -> 3.57 us  [the longest x1 1.62 us: local(): call(functools.partial(front_kernel, grid), 'front', 16, (shape(3, 2 * HA...]
    unnamed x8 -> x2, local copies, waits for them, and re-layouts: 0.68 us -> 0.01 us
  transfers between devices with their start and end apart: 5 -> 5, of which waited for: 3 -> 3; matrix products, arithmetic and copies ran while one was open for 0% -> 0% of each run, Pallas kernels for 10% -> 16%
where the time goes in v4:
time: 30.3 us; the launch traced here: 30.1 us
  starting transfers between devices  13.4 us (44%)
  Pallas kernels  8.43 us (28%)
  waiting for transfers between devices  7.51 us (25%)
  between operations  0.72 us (2%)
    all_to_all x1, starting transfers between devices, local(): parts = lax.all_to_all(part, ('gx', 'gy'), 0, 0, tiled=True)  8.17 us
    ppermute x4, starting transfers between devices, swap(): return lax.ppermute(value, ('gx', 'gy'), pairs)  5.26 us
    all_to_all x1, waiting for transfers between devices, local(): parts = lax.all_to_all(part, ('gx', 'gy'), 0, 0, tiled=True)  4.22 us
    ppermute x4, waiting for transfers between devices, swap(): return lax.ppermute(value, ('gx', 'gy'), pairs)  3.3 us
    pallas_call x1, Pallas kernels, local(): call(functools.partial(back_kernel, grid), 'back', 24, (shape(*block), sh...  2.89 us
    pallas_call x1, Pallas kernels, local(): call(functools.partial(front_kernel, grid), 'front', 16, (shape(3, 2 * HA...  1.62 us
    pallas_call x1, Pallas kernels, local(): call(pack_kernel, 'pack', 2, (shape(3, rows, depth, LANES), shape(3, dept...  1.2 us
    pallas_call x1, Pallas kernels, local(): call(functools.partial(core_kernel, grid), 'core', 8, (shape(3, rows, dep...  1.09 us
  transfers between devices with their start and end apart: 5, of which 3 were waited for; matrix products, arithmetic and copies ran while one was open for 0% of the time, Pallas kernels for 16%

profile of v4, /device:TPU:0, one launch (start us, length us, event | category | flops | bytes accessed | tf_op | source)
XLA Modules:
  0.0 30.1 jit_solution(6121207753678644102)
XLA Ops:
  0.6 1.2 %pack.1 = (f32[3,8,16,128]{3,2,1,0:T(8,128)S(1)}, f32[3,16,128]{2,1,0:T(8,128)S(1)}) custom-call(f32[16,8,128]{2,1,0:T(8,128)} %temp_in.1, s32[16,8,128]{2,1,0:T(8,128)} %material_in.1, s32[16,8,128]{2,1,0:T(8,128)} %plate.1, f32[16,8,128]{2,1,0:T(8,128)} %cooling_in.1), custom_call_target="tpu_custom_call" | custom-call | tf_op jit(solution)/shard_map/pack/pallas_call | solution.py:604
  1.8 4.0 %collective-permute-start.1 = (f32[3,16,128]{2,1,0:T(8,128)S(1)}, f32[3,16,128]{2,1,0:T(8,128)S(1)}, u32[]{:S(2)}, u32[]{:S(2)}) collective-permute-start(f32[3,16,128]{2,1,0:T(8,128)S(1)} %get-tuple-element.25), channel_id=1, source_target_pairs={{0,3},{1,2},{2,1},{3,0},{4,7},{5,6},{6,5},{7,4},{8,11},{9,10},{10,... | collective-permute-start | bytes 73736 | tf_op jit(solution)/shard_map/ppermute | solution.py:579
  5.8 0.5 %collective-permute-start = (f32[3,16,128]{2,1,0:T(8,128)S(1)}, f32[3,16,128]{2,1,0:T(8,128)S(1)}, u32[]{:S(2)}, u32[]{:S(2)}) collective-permute-start(f32[3,16,128]{2,1,0:T(8,128)S(1)} %get-tuple-element.25), channel_id=1, source_target_pairs={{0,1},{1,0},{2,3},{3,2},{4,5},{5,4},{6,7},{7,6},{8,9},{9,8},{10,11... | collective-permute-start | bytes 73736 | tf_op jit(solution)/shard_map/ppermute | solution.py:579
  6.4 1.3 %collective-permute-done.1.side_b = f32[3,16,128]{2,1,0:T(8,128)S(1)} collective-permute-done((f32[3,16,128]{2,1,0:T(8,128)S(1)}, f32[3,16,128]{2,1,0:T(8,128)S(1)}, u32[]{:S(2)}, u32[]{:S(2)}) %collective-permute-start.1) | collective-permute-done | bytes 24608 | tf_op jit(solution)/shard_map/ppermute | solution.py:579
  7.6 2.0 %collective-permute-done.side_a = f32[3,16,128]{2,1,0:T(8,128)S(1)} collective-permute-done((f32[3,16,128]{2,1,0:T(8,128)S(1)}, f32[3,16,128]{2,1,0:T(8,128)S(1)}, u32[]{:S(2)}, u32[]{:S(2)}) %collective-permute-start) | collective-permute-done | bytes 24608 | tf_op jit(solution)/shard_map/ppermute | solution.py:579
  9.7 0.1 collective-permute-start.2
  9.8 0.7 %collective-permute-start.3 = (f32[19,16,128]{2,1,0:T(8,128)S(1)}, f32[19,16,128]{2,1,0:T(8,128)S(1)}, u32[]{:S(2)}, u32[]{:S(2)}) collective-permute-start(f32[19,16,128]{2,1,0:T(8,128)S(1)} %get-tuple-element.29), channel_id=1, source_target_pairs={{4,8},{5,9},{6,10},{7,11},{8,4},{9,5},{10,6},{11,7},{12,16},{13,17... | collective-permute-start | bytes 466952 | tf_op jit(solution)/shard_map/ppermute | solution.py:579
  10.4 0.9 %table.1 = f32[7,8,128]{2,1,0:T(8,128)S(1)} custom-call(f32[3,16]{1,0:T(4,128)} %bitcast.8, f32[3,16]{1,0:T(4,128)} %bitcast.9, f32[1,16]{1,0:T(1,128)} %bitcast.10), custom_call_target="tpu_custom_call" | custom-call | tf_op jit(solution)/shard_map/table/pallas_call | solution.py:629
  11.3 1.1 %core.1 = (f32[3,8,16,128]{3,2,1,0:T(8,128)S(1)}, f32[3600,128]{1,0:T(8,128)S(1)}, f32[8,2,16,128]{3,2,1,0:T(8,128)S(1)}, f32[1160,128]{1,0:T(8,128)S(1)}, f32[6...) custom-call(f32[3,8,16,128]{3,2,1,0:T(8,128)S(1)} %get-tuple-element, ...), custom_call_target="tpu_custom_call" | custom-call | tf_op jit(solution)/shard_map/core/pallas_call | solution.py:640
  12.4 0.0 collective-permute-done.2.got_a
  12.4 0.0 collective-permute-done.3.got_b
  12.4 0.0 copy-start
  12.4 1.6 %front.1 = (f32[3,12,2,16,128]{4,3,2,1,0:T(8,128)S(1)}, f32[6,2,16,128]{3,2,1,0:T(8,128)S(1)}, f32[6,2,16,128]{3,2,1,0:T(8,128)S(1)}, f32[6,1,16,128]{3,2,1,0:T(8,128)S(1)}, f32[32,128]{1,0:T(8,128)}) custom-call(f32[3,8,16,128]{3,2,1,0:T(8,128)S(1)} %get-tuple-element.24.own, f32[3,8,16,128]{3,2,1,0:T(8,128)S(1)} %get-tuple-element.27.halo, ...), custom_call_target="tpu_custom_call" | custom-call | tf_op jit(solution)/shard_map/front/pallas_call | solution.py:657
  14.1 8.2 %all-to-all-start = ((f32[32,1,128]{2,1,0:T(1,128)}), f32[32,1,128]{2,1,0:T(1,128)S(1)}, u32[]{:S(2)}, u32[]{:S(2)}) async-start(f32[32,1,128]{2,1,0:T(1,128)} %bitcast.4), calls=%async_computation | async-start | bytes 32768 | tf_op jit(solution)/shard_map/all_to_all | solution.py:676
  22.2 0.0 copy-done
  22.2 2.9 %back.1 = (f32[16,8,128]{2,1,0:T(8,128)S(1)}, f32[16,8,128]{2,1,0:T(8,128)S(1)}) custom-call(f32[3,8,16,128]{3,2,1,0:T(8,128)S(1)} %get-tuple-element.24.own, f32[3,8,16,128]{3,2,1,0:T(8,128)S(1)} %get-tuple-element.27.halo, f32[3,12,2,16,128]{4,3,2,1,0:T(8,128)S(1)} %get-tuple-element.37.ext, f32[6,2,16,128]{3,2,1,0:T(8,128)S(1)} %get-tuple-element.38.first_core, ...), custom_call_target="tpu_custom_call" | custom-call | tf_op jit(solution)/shard_map/back/pallas_call | solution.py:677
  25.1 4.2 %all-to-all-done = f32[32,1,128]{2,1,0:T(1,128)S(1)} async-done(((f32[32,1,128]{2,1,0:T(1,128)}), f32[32,1,128]{2,1,0:T(1,128)S(1)}, u32[]{:S(2)}, u32[]{:S(2)}) %all-to-all-start) | async-done | bytes 16416 | tf_op jit(solution)/shard_map/all_to_all | solution.py:676
  29.4 0.7 %scale.1 = (f32[16,8,128]{2,1,0:T(8,128)}, f32[16,8,128]{2,1,0:T(8,128)}) custom-call(f32[32,128]{1,0:T(8,128)S(1)} %bitcast.7, f32[16,8,128]{2,1,0:T(8,128)S(1)} %get-tuple-element.44.adjoint, f32[16,8,128]{2,1,0:T(8,128)S(1)} %get-tuple-element.45.sens), custom_call_target="tpu_custom_call" | custom-call | tf_op jit(solution)/shard_map/scale/pallas_call | solution.py:692
  (1 shorter events, 0.0 us)
Async XLA Ops:
  1.8 5.8 %collective-permute-start.1 = (f32[3,16,128]{2,1,0:T(8,128)S(1)}, f32[3,16,128]{2,1,0:T(8,128)S(1)}, u32[]{:S(2)}, u32[]{:S(2)}) collective-permute-start(f32[3,16,128]{2,1,0:T(8,128)S(1)} %get-tuple-element.25), channel_id=1, source_target_pairs={{0,3},{1,2},{2,1},{3,0},{4,7},{5,6},{6,5},{7,4},{8,11},{9,10},{10,... | collective-permute-start | bytes 73736 | tf_op jit(solution)/shard_map/ppermute | solution.py:579
  5.8 3.8 %collective-permute-start = (f32[3,16,128]{2,1,0:T(8,128)S(1)}, f32[3,16,128]{2,1,0:T(8,128)S(1)}, u32[]{:S(2)}, u32[]{:S(2)}) collective-permute-start(f32[3,16,128]{2,1,0:T(8,128)S(1)} %get-tuple-element.25), channel_id=1, source_target_pairs={{0,1},{1,0},{2,3},{3,2},{4,5},{5,4},{6,7},{7,6},{8,9},{9,8},{10,11... | collective-permute-start | bytes 73736 | tf_op jit(solution)/shard_map/ppermute | solution.py:579
  9.7 2.7 %collective-permute-start.2 = (f32[19,16,128]{2,1,0:T(8,128)S(1)}, f32[19,16,128]{2,1,0:T(8,128)S(1)}, u32[]{:S(2)}, u32[]{:S(2)}) collective-permute-start(f32[19,16,128]{2,1,0:T(8,128)S(1)} %get-tuple-element.28), channel_id=1, source_target_pairs={{0,4},{1,5},{2,6},{3,7},{4,0},{5,1},{6,2},{7,3},{8,12},{9,13},{10,... | collective-permute-start | bytes 466952 | tf_op jit(solution)/shard_map/ppermute | solution.py:579
  9.8 2.7 %collective-permute-start.3 = (f32[19,16,128]{2,1,0:T(8,128)S(1)}, f32[19,16,128]{2,1,0:T(8,128)S(1)}, u32[]{:S(2)}, u32[]{:S(2)}) collective-permute-start(f32[19,16,128]{2,1,0:T(8,128)S(1)} %get-tuple-element.29), channel_id=1, source_target_pairs={{4,8},{5,9},{6,10},{7,11},{8,4},{9,5},{10,6},{11,7},{12,16},{13,17... | collective-permute-start | bytes 466952 | tf_op jit(solution)/shard_map/ppermute | solution.py:579
  12.4 9.8 %copy-start = (s32[16,8,128]{2,1,0:T(8,128)S(1)}, s32[16,8,128]{2,1,0:T(8,128)}, u32[]{:S(2)}) copy-start(s32[16,8,128]{2,1,0:T(8,128)} %plate.1) | copy-start | bytes 196612
  14.1 15.3 %all-to-all-start = ((f32[32,1,128]{2,1,0:T(1,128)}), f32[32,1,128]{2,1,0:T(1,128)S(1)}, u32[]{:S(2)}, u32[]{:S(2)}) async-start(f32[32,1,128]{2,1,0:T(1,128)} %bitcast.4), calls=%async_computation | async-start | bytes 32768 | tf_op jit(solution)/shard_map/all_to_all | solution.py:676

commit v5 on v4

--- a/solution.py
+++ b/solution.py
@@ -6,6 +6,7 @@
 from jax.experimental import pallas as pl
 from jax.experimental.pallas import tpu as pltpu
 from jax.sharding import PartitionSpec as P
+
 
 STEPS = 3
 STEP_SCALE = 0.06
@@ -22,7 +23,6 @@
 HALO = 2 * STEPS
 LANES = 128
 SLOT = 16
-T0, ID, COEFF = 0, 1, 2
 SENT = (HALO, HALO - 1, HALO - 1)
 PLACE = (3, 3 + HALO, 3 + 2 * HALO - 1)
 PAYLOAD = 3 + sum(SENT)
@@ -35,19 +35,7 @@
     return lax.broadcasted_iota(jnp.int32, shape, len(shape) - 1)
 
 
-def copy_in(pairs, sems):
-    copies = [
-        pltpu.make_async_copy(source, target, sems.at[i])
-        for i, (source, target) in enumerate(pairs)
-    ]
-    for copy in copies:
-        copy.start()
-    for copy in copies:
-        copy.wait()
-
-
-def table_kernel(principal_in, angles_in, aging_in, table, principal, angles, aging, line, sems):
-    copy_in(((principal_in, principal), (angles_in, angles), (aging_in, aging)), sems)
+def put_table(principal, angles, aging, table, line):
     count = aging.shape[1]
     line[...] = jnp.zeros_like(line)
     line[0:3, 0:count] = principal[...]
@@ -72,10 +60,26 @@
         table[k] = jnp.broadcast_to(row, (8, LANES))
 
 
-def pack_kernel(temp_in, material_in, plate_in, cooling_in, own, pack, temp, material, plate, cooling, sems):
-    copy_in(
-        ((temp_in, temp), (material_in, material), (plate_in, plate), (cooling_in, cooling)), sems
+def pack_kernel(
+    principal_in, angles_in, aging_in, temp_in, material_in, plate_in, cooling_in,
+    own, pack, send_b, table,
+    principal, angles, aging, temp, material, plate, cooling, line, sems,
+):
+    pairs = (
+        (principal_in, principal), (angles_in, angles), (aging_in, aging),
+        (temp_in, temp), (material_in, material), (plate_in, plate), (cooling_in, cooling),
     )
+    copies = [
+        pltpu.make_async_copy(source, target, sems.at[i])
+        for i, (source, target) in enumerate(pairs)
+    ]
+    for copy in copies:
+        copy.start()
+    for copy in copies[:3]:
+        copy.wait()
+    put_table(principal, angles, aging, table, line)
+    for copy in copies[3:]:
+        copy.wait()
     depth, rows, _ = temp.shape
     lane = lane_of((depth, LANES))
     packs = [jnp.zeros((depth, LANES), jnp.float32) for _ in range(3)]
@@ -90,11 +94,16 @@
             own[f, x] = fields[f]
             moved = pltpu.roll(fields[f], (SLOT * x + HALO) % LANES, 1)
             packs[f] = jnp.where(mine, moved, packs[f])
+    even_x = lax.rem(lax.axis_index("gx"), 2) == 0
     for f in range(3):
         pack[f] = packs[f]
-
-
-def middle_kernel(last_y, own, side_a, side_b, mid, send_a, send_b):
+        count = SENT[f]
+        first_b = jnp.where(even_x, 0, rows - count)
+        for r in range(count):
+            send_b[PLACE[f] - 3 + r] = own[f, first_b + r]
+
+
+def middle_kernel(last_y, own, side_a, side_b, mid, send_a):
     _, rows, depth, _ = own.shape
     at_y = lax.axis_index("gy")
     even_y = lax.rem(at_y, 2) == 0
@@ -106,14 +115,11 @@
         value = jnp.where(from_left, left, right)
         mid[f] = value
         send_a[f] = value
-        send_b[f] = value
     for f in range(3):
         count = SENT[f]
         first_a = jnp.where(even_x, rows - count, 0)
-        first_b = jnp.where(even_x, 0, rows - count)
         for r in range(count):
             send_a[PLACE[f] + r] = own[f, first_a + r]
-            send_b[PLACE[f] + r] = own[f, first_b + r]
 
 
 class Rows:
@@ -292,7 +298,7 @@
     return [r for r in rows if r < middle], [r for r in rows if r >= middle]
 
 
-def march(n, weights, keep, coeff, source, target, out, rows, tiles, depth, loss):
+def march(weights, keep, coeff, source, target, out, rows, tiles, depth, loss):
     def done(r, t, base, value):
         out.put(r, t, value, base)
         if loss is not None and t == 0 and loss[0] <= r < loss[1]:
@@ -352,7 +358,7 @@
     for n in range(STEPS):
         target = shifted[n + 1] if n < 2 else None
         tiles = (0, 1) if n < 2 else (0,)
-        march(n, weights, keep, coeff, shifted[n], target, outs[n], plan.cone(-n - 1), tiles, depth, loss)
+        march(weights, keep, coeff, shifted[n], target, outs[n], plan.cone(-n - 1), tiles, depth, loss)
     loss_ref[...] = total_of(loss[2])
 
 
@@ -375,7 +381,7 @@
 
 
 def front_kernel(
-    grid, own, halo, got_a, got_b, table, weights_in, keep_in, start_in, first_in, second_in, loss_in,
+    grid, own, halo, got_b, far_b, got_a, table, weights_in, keep_in, start_in, first_in, second_in, loss_in,
     ext, first, second, third, part,
     weights_ref, keep_ref, start_ref, first_ref, second_ref,
 ):
@@ -389,7 +395,7 @@
         base_b = jnp.where(even, HALO - SENT[f], HALO)
         for r in range(SENT[f]):
             ext[f, base_a + r, 0] = got_a[PLACE[f] + r]
-            ext[f, base_b + r, 0] = got_b[PLACE[f] + r]
+            ext[f, base_b + r, 0] = far_b[PLACE[f] - 3 + r]
         low = jnp.where(even, got_b[f], got_a[f])
         high = jnp.where(even, got_a[f], got_b[f])
         for r in range(HALO):
@@ -423,7 +429,7 @@
         ring = halves(plan.ring(2 - n, -n - 1), plan.middle)
         target = shifted[n + 1] if n < 2 else None
         tiles = (0, 1) if n < 2 else (0,)
-        march(n, weights, keep, coeff, shifted[n], target, outs[n], ring, tiles, depth, loss)
+        march(weights, keep, coeff, shifted[n], target, outs[n], ring, tiles, depth, loss)
     total = loss_in[...] + total_of(loss[2])
     part[...] = jnp.broadcast_to(jnp.sum(total, axis=0, keepdims=True), part.shape)
 
@@ -588,58 +594,52 @@
     def shape(*dims):
         return jax.ShapeDtypeStruct(dims, f32)
 
-    def call(kernel, name, mib, out_shape, scratch=(), **specs):
+    def call(kernel, mib, out_shape, scratch=(), **specs):
         return pl.pallas_call(
             kernel,
             out_shape=out_shape,
             scratch_shapes=[
                 pltpu.VMEM(dims, f32) if isinstance(dims, tuple) else dims for dims in scratch
             ],
-            name=name,
             compiler_params=pltpu.CompilerParams(vmem_limit_bytes=mib * 2**20),
             **specs,
         )
 
     block = (depth, rows, LANES)
-    own, pack = call(
+    inputs = (
+        principal.T, angles.T, aging_scale[None], initial_temp, material, plate, cooling
+    )
+    own, pack, send_b, table = call(
         pack_kernel,
-        "pack",
         2,
-        (shape(3, rows, depth, LANES), shape(3, depth, LANES)),
         (
-            block,
-            pltpu.VMEM(block, jnp.int32),
-            pltpu.VMEM(block, jnp.int32),
-            block,
-            pltpu.SemaphoreType.DMA((4,)),
+            shape(3, rows, depth, LANES),
+            shape(3, depth, LANES),
+            shape(PAYLOAD - 3, depth, LANES),
+            shape(PARTS, 8, LANES),
         ),
-        in_specs=[pl.BlockSpec(memory_space=pltpu.HBM)] * 4,
-    )(*(pltpu.with_memory_space_constraint(x, pltpu.HBM) for x in (initial_temp, material, plate, cooling)))
+        (
+            *(pltpu.VMEM(x.shape, x.dtype) for x in inputs),
+            (8, LANES),
+            pltpu.SemaphoreType.DMA((len(inputs),)),
+        ),
+        in_specs=[pl.BlockSpec(memory_space=pltpu.HBM)] * len(inputs),
+    )(*(pltpu.with_memory_space_constraint(x, pltpu.HBM) for x in inputs))
     side_b = swap(pack, sizes, 1, 1, True)
     side_a = swap(pack, sizes, 1, 0)
-    mid, send_a, send_b = call(
+    far_b = swap(send_b, sizes, 0, 1)
+    mid, send_a = call(
         functools.partial(middle_kernel, sizes[1] - 1),
-        "middle",
         2,
-        (shape(3, depth, LANES), shape(PAYLOAD, depth, LANES), shape(PAYLOAD, depth, LANES)),
+        (shape(3, depth, LANES), shape(PAYLOAD, depth, LANES)),
     )(own, side_a, side_b)
-    got_b = swap(send_b, sizes, 0, 1)
+    got_b = swap(mid, sizes, 0, 1)
     got_a = swap(send_a, sizes, 0, 0)
-    small = [principal.T, angles.T, aging_scale[None]]
-    table = call(
-        table_kernel,
-        "table",
-        2,
-        shape(PARTS, 8, LANES),
-        (*(x.shape for x in small), (8, LANES), pltpu.SemaphoreType.DMA((3,))),
-        in_specs=[pl.BlockSpec(memory_space=pltpu.HBM)] * 3,
-    )(*(pltpu.with_memory_space_constraint(x, pltpu.HBM) for x in small))
 
     pairs = 2 * rows
     grid = (rows * sizes[0], width * sizes[1])
     halo, weights, keep, start, first_core, first_moved, second_core, second_moved, third_core, loss = call(
         functools.partial(core_kernel, grid),
-        "core",
         8,
         (
             shape(3, rows, depth, LANES),
@@ -656,7 +656,6 @@
     )(own, mid, table)
     ext, first, second, third, part = call(
         functools.partial(front_kernel, grid),
-        "front",
         16,
         (
             shape(3, 2 * HALO, 2, depth, LANES),
@@ -672,11 +671,10 @@
             padded_size(3 * 12, depth),
             padded_size(3 * 12, depth),
         ),
-    )(own, halo, got_a, got_b, table, weights, keep, start, first_moved, second_moved, loss)
+    )(own, halo, got_b, far_b, got_a, table, weights, keep, start, first_moved, second_moved, loss)
     parts = lax.all_to_all(part, ("gx", "gy"), 0, 0, tiled=True)
     adjoint, sens = call(
         functools.partial(back_kernel, grid),
-        "back",
         24,
         (shape(*block), shape(*block)),
         (
@@ -691,7 +689,6 @@
     )(own, halo, ext, first_core, second_core, third_core, first, second, third, table, plate)
     return call(
         functools.partial(scale_kernel, float(depth * rows * width * devices)),
-        "scale",
         2,
         (shape(*block), shape(*block)),
     )(parts, adjoint, sens)

time: 30.3 us -> 31.5 us (1.040)
  starting transfers between devices: 13.4 us -> 15.4 us
  Pallas kernels: 8.43 us -> 7.61 us
    all_to_all x1, starting transfers between devices: 8.17 us -> 9.43 us  [local(): parts = lax.all_to_all(part, ('gx', 'gy'), 0, 0, tiled=True)]
    pallas_call x6 -> x5, Pallas kernels: 7.69 us -> 6.86 us  [the longest x1 2.86 us: local(): call(functools.partial(back_kernel, grid), 24, (shape(*block), shape(*blo...]
    ppermute x4 -> x5, starting transfers between devices: 5.26 us -> 5.93 us  [swap(): return lax.ppermute(value, ('gx', 'gy'), pairs)]
    ppermute x4 -> x5, waiting for transfers between devices: 3.3 us -> 3.3 us  [swap(): return lax.ppermute(value, ('gx', 'gy'), pairs)]
  transfers between devices with their start and end apart: 5 -> 6, of which waited for: 3 -> 3; matrix products, arithmetic and copies ran while one was open for 0% -> 0% of each run, Pallas kernels for 16% -> 13%
where the time goes in v5:
time: 31.5 us; the launch traced here: 31.3 us
  starting transfers between devices  15.4 us (49%)
  Pallas kernels  7.61 us (24%)
  waiting for transfers between devices  7.55 us (24%)
  between operations  0.73 us (2%)
    all_to_all x1, starting transfers between devices, local(): parts = lax.all_to_all(part, ('gx', 'gy'), 0, 0, tiled=True)  9.43 us
    ppermute x5, starting transfers between devices, swap(): return lax.ppermute(value, ('gx', 'gy'), pairs)  5.93 us
    all_to_all x1, waiting for transfers between devices, local(): parts = lax.all_to_all(part, ('gx', 'gy'), 0, 0, tiled=True)  4.25 us
    ppermute x5, waiting for transfers between devices, swap(): return lax.ppermute(value, ('gx', 'gy'), pairs)  3.3 us
    pallas_call x1, Pallas kernels, local(): call(functools.partial(back_kernel, grid), 24, (shape(*block), shape(*blo...  2.86 us
    pallas_call x1, Pallas kernels, local(): call(functools.partial(front_kernel, grid), 16, (shape(3, 2 * HALO, 2, de...  1.62 us
    pallas_call x1, Pallas kernels, local(): call(pack_kernel, 2, (shape(3, rows, depth, LANES), shape(3, depth, LANES...  1.27 us
    pallas_call x1, Pallas kernels, local(): call(functools.partial(core_kernel, grid), 8, (shape(3, rows, depth, LANE...  1.09 us
  transfers between devices with their start and end apart: 6, of which 3 were waited for; matrix products, arithmetic and copies ran while one was open for 0% of the time, Pallas kernels for 13%

profile of v5, /device:TPU:0, one launch (start us, length us, event | category | flops | bytes accessed | tf_op | source)
XLA Modules:
  0.0 31.3 jit_solution(14945088044368855378)
XLA Ops:
  0.6 1.3 %shard_map.86 = (f32[3,8,16,128]{3,2,1,0:T(8,128)S(1)}, f32[3,16,128]{2,1,0:T(8,128)S(1)}, f32[16,16,128]{2,1,0:T(8,128)S(1)}, f32[7,8,128]{2,1,0:T(8,128)S(1)}) custom-call(f32[3,16]{1,0:T(4,128)} %bitcast.8, f32[3,16]{1,0:T(4,128)} %bitcast.9, f32[1,16]{1,0:T(1,128)} %bitcast.10, f32[16,8,128]{2,1,0:T(8,128)} %temp_in.1, s32[16,8,128]{2,1,0:T(8,128)} %material_in.1, ...), custom_call_target="tpu_custom_call" | custom-call | tf_op jit(solution)/shard_map/pallas_call | solution.py:612
  1.9 4.0 %collective-permute-start.1 = (f32[3,16,128]{2,1,0:T(8,128)S(1)}, f32[3,16,128]{2,1,0:T(8,128)S(1)}, u32[]{:S(2)}, u32[]{:S(2)}) collective-permute-start(f32[3,16,128]{2,1,0:T(8,128)S(1)} %get-tuple-element.26), channel_id=1, source_target_pairs={{0,3},{1,2},{2,1},{3,0},{4,7},{5,6},{6,5},{7,4},{8,11},{9,10},{10,... | collective-permute-start | bytes 73736 | tf_op jit(solution)/shard_map/ppermute | solution.py:585
  5.9 0.5 %collective-permute-start = (f32[3,16,128]{2,1,0:T(8,128)S(1)}, f32[3,16,128]{2,1,0:T(8,128)S(1)}, u32[]{:S(2)}, u32[]{:S(2)}) collective-permute-start(f32[3,16,128]{2,1,0:T(8,128)S(1)} %get-tuple-element.26), channel_id=1, source_target_pairs={{0,1},{1,0},{2,3},{3,2},{4,5},{5,4},{6,7},{7,6},{8,9},{9,8},{10,11... | collective-permute-start | bytes 73736 | tf_op jit(solution)/shard_map/ppermute | solution.py:585
  6.4 1.3 %collective-permute-done.1.side_b = f32[3,16,128]{2,1,0:T(8,128)S(1)} collective-permute-done((f32[3,16,128]{2,1,0:T(8,128)S(1)}, f32[3,16,128]{2,1,0:T(8,128)S(1)}, u32[]{:S(2)}, u32[]{:S(2)}) %collective-permute-start.1) | collective-permute-done | bytes 24608 | tf_op jit(solution)/shard_map/ppermute | solution.py:585
  7.7 2.0 %collective-permute-done.side_a = f32[3,16,128]{2,1,0:T(8,128)S(1)} collective-permute-done((f32[3,16,128]{2,1,0:T(8,128)S(1)}, f32[3,16,128]{2,1,0:T(8,128)S(1)}, u32[]{:S(2)}, u32[]{:S(2)}) %collective-permute-start) | collective-permute-done | bytes 24608 | tf_op jit(solution)/shard_map/ppermute | solution.py:585
  9.8 0.1 collective-permute-start.4
  9.8 0.7 %collective-permute-start.3 = (f32[16,16,128]{2,1,0:T(8,128)S(1)}, f32[16,16,128]{2,1,0:T(8,128)S(1)}, u32[]{:S(2)}, u32[]{:S(2)}) collective-permute-start(f32[16,16,128]{2,1,0:T(8,128)S(1)} %get-tuple-element.30), channel_id=1, source_target_pairs={{4,8},{5,9},{6,10},{7,11},{8,4},{9,5},{10,6},{11,7},{12,16},{13,17... | collective-permute-start | bytes 393224 | tf_op jit(solution)/shard_map/ppermute | solution.py:585
  10.5 0.7 %collective-permute-start.2 = (f32[3,16,128]{2,1,0:T(8,128)S(1)}, f32[3,16,128]{2,1,0:T(8,128)S(1)}, u32[]{:S(2)}, u32[]{:S(2)}) collective-permute-start(f32[3,16,128]{2,1,0:T(8,128)S(1)} %get-tuple-element.27.mid), channel_id=1, source_target_pairs={{4,8},{5,9},{6,10},{7,11},{8,4},{9,5},{10,6},{11,7},{12,16},{13,17... | collective-permute-start | bytes 73736 | tf_op jit(solution)/shard_map/ppermute | solution.py:585
  11.2 1.1 %shard_map.88 = (f32[3,8,16,128]{3,2,1,0:T(8,128)S(1)}, f32[3600,128]{1,0:T(8,128)S(1)}, f32[8,2,16,128]{3,2,1,0:T(8,128)S(1)}, f32[1160,128]{1,0:T(8,128)S(1)},...) custom-call(f32[3,8,16,128]{3,2,1,0:T(8,128)S(1)} %get-tuple-element, ...), custom_call_target="tpu_custom_call" | custom-call | tf_op jit(solution)/shard_map/pallas_call | solution.py:641
  12.3 0.0 collective-permute-done.2.got_b
  12.3 0.0 collective-permute-done.3.far_b
  12.3 0.0 collective-permute-done.4.got_a
  12.3 0.0 copy-start
  12.3 1.6 %shard_map.89 = (f32[3,12,2,16,128]{4,3,2,1,0:T(8,128)S(1)}, f32[6,2,16,128]{3,2,1,0:T(8,128)S(1)}, f32[6,2,16,128]{3,2,1,0:T(8,128)S(1)}, f32[6,1,16,128]{3,2,1,0:T(8,128)S(1)}, f32[32,128]{1,0:T(8,128)}) custom-call(f32[3,8,16,128]{3,2,1,0:T(8,128)S(1)} %get-tuple-element.25.own, f32[3,8,16,128]{3,2,1,0:T(8,128)S(1)} %get-tuple-element.29.halo, ...), custom_call_target="tpu_custom_call" | custom-call | tf_op jit(solution)/shard_map/pallas_call | solution.py:657
  13.9 9.4 %all-to-all-start = ((f32[32,1,128]{2,1,0:T(1,128)}), f32[32,1,128]{2,1,0:T(1,128)S(1)}, u32[]{:S(2)}, u32[]{:S(2)}) async-start(f32[32,1,128]{2,1,0:T(1,128)} %bitcast.4), calls=%async_computation | async-start | bytes 32768 | tf_op jit(solution)/shard_map/all_to_all | solution.py:675
  23.4 0.0 copy-done
  23.4 2.9 %shard_map.90 = (f32[16,8,128]{2,1,0:T(8,128)S(1)}, f32[16,8,128]{2,1,0:T(8,128)S(1)}) custom-call(f32[3,8,16,128]{3,2,1,0:T(8,128)S(1)} %get-tuple-element.25.own, f32[3,8,16,128]{3,2,1,0:T(8,128)S(1)} %get-tuple-element.29.halo, f32[3,12,2,16,128]{4,3,2,1,0:T(8,128)S(1)} %get-tuple-element.39.ext, f32[6,2,16,128]{3,2,1,0:T(8,128)S(1)} %get-tuple-element.40.first_core, ...), custom_call_target="tpu_custom_call" | custom-call | tf_op jit(solution)/shard_map/pallas_call | solution.py:676
  26.3 4.2 %all-to-all-done = f32[32,1,128]{2,1,0:T(1,128)S(1)} async-done(((f32[32,1,128]{2,1,0:T(1,128)}), f32[32,1,128]{2,1,0:T(1,128)S(1)}, u32[]{:S(2)}, u32[]{:S(2)}) %all-to-all-start) | async-done | bytes 16416 | tf_op jit(solution)/shard_map/all_to_all | solution.py:675
  30.5 0.7 %shard_map.91 = (f32[16,8,128]{2,1,0:T(8,128)}, f32[16,8,128]{2,1,0:T(8,128)}) custom-call(f32[32,128]{1,0:T(8,128)S(1)} %bitcast.7, f32[16,8,128]{2,1,0:T(8,128)S(1)} %get-tuple-element.46.adjoint, f32[16,8,128]{2,1,0:T(8,128)S(1)} %get-tuple-element.47.sens), custom_call_target="tpu_custom_call" | custom-call | tf_op jit(solution)/shard_map/pallas_call | solution.py:690
  (1 shorter events, 0.0 us)
Async XLA Ops:
  1.9 5.8 %collective-permute-start.1 = (f32[3,16,128]{2,1,0:T(8,128)S(1)}, f32[3,16,128]{2,1,0:T(8,128)S(1)}, u32[]{:S(2)}, u32[]{:S(2)}) collective-permute-start(f32[3,16,128]{2,1,0:T(8,128)S(1)} %get-tuple-element.26), channel_id=1, source_target_pairs={{0,3},{1,2},{2,1},{3,0},{4,7},{5,6},{6,5},{7,4},{8,11},{9,10},{10,... | collective-permute-start | bytes 73736 | tf_op jit(solution)/shard_map/ppermute | solution.py:585
  5.9 3.8 %collective-permute-start = (f32[3,16,128]{2,1,0:T(8,128)S(1)}, f32[3,16,128]{2,1,0:T(8,128)S(1)}, u32[]{:S(2)}, u32[]{:S(2)}) collective-permute-start(f32[3,16,128]{2,1,0:T(8,128)S(1)} %get-tuple-element.26), channel_id=1, source_target_pairs={{0,1},{1,0},{2,3},{3,2},{4,5},{5,4},{6,7},{7,6},{8,9},{9,8},{10,11... | collective-permute-start | bytes 73736 | tf_op jit(solution)/shard_map/ppermute | solution.py:585
  9.8 2.5 %collective-permute-start.4 = (f32[19,16,128]{2,1,0:T(8,128)S(1)}, f32[19,16,128]{2,1,0:T(8,128)S(1)}, u32[]{:S(2)}, u32[]{:S(2)}) collective-permute-start(f32[19,16,128]{2,1,0:T(8,128)S(1)} %get-tuple-element.31), channel_id=1, source_target_pairs={{0,4},{1,5},{2,6},{3,7},{4,0},{5,1},{6,2},{7,3},{8,12},{9,13},{10,... | collective-permute-start | bytes 466952 | tf_op jit(solution)/shard_map/ppermute | solution.py:585
  9.8 2.5 %collective-permute-start.3 = (f32[16,16,128]{2,1,0:T(8,128)S(1)}, f32[16,16,128]{2,1,0:T(8,128)S(1)}, u32[]{:S(2)}, u32[]{:S(2)}) collective-permute-start(f32[16,16,128]{2,1,0:T(8,128)S(1)} %get-tuple-element.30), channel_id=1, source_target_pairs={{4,8},{5,9},{6,10},{7,11},{8,4},{9,5},{10,6},{11,7},{12,16},{13,17... | collective-permute-start | bytes 393224 | tf_op jit(solution)/shard_map/ppermute | solution.py:585
  10.5 1.8 %collective-permute-start.2 = (f32[3,16,128]{2,1,0:T(8,128)S(1)}, f32[3,16,128]{2,1,0:T(8,128)S(1)}, u32[]{:S(2)}, u32[]{:S(2)}) collective-permute-start(f32[3,16,128]{2,1,0:T(8,128)S(1)} %get-tuple-element.27.mid), channel_id=1, source_target_pairs={{4,8},{5,9},{6,10},{7,11},{8,4},{9,5},{10,6},{11,7},{12,16},{13,17... | collective-permute-start | bytes 73736 | tf_op jit(solution)/shard_map/ppermute | solution.py:585
  12.3 11.1 %copy-start = (s32[16,8,128]{2,1,0:T(8,128)S(1)}, s32[16,8,128]{2,1,0:T(8,128)}, u32[]{:S(2)}) copy-start(s32[16,8,128]{2,1,0:T(8,128)} %plate.1) | copy-start | bytes 196612
  13.9 16.6 %all-to-all-start = ((f32[32,1,128]{2,1,0:T(1,128)}), f32[32,1,128]{2,1,0:T(1,128)S(1)}, u32[]{:S(2)}, u32[]{:S(2)}) async-start(f32[32,1,128]{2,1,0:T(1,128)} %bitcast.4), calls=%async_computation | async-start | bytes 32768 | tf_op jit(solution)/shard_map/all_to_all | solution.py:675
